TPU v7x, 32 devices: a whole 2x2x4 slice. The times are simulated.
32 devices in a mesh: grp: 2 (over y), ccd: 4 (over z), row: 2 (over x), amp: 2 (over core).
Axes of the slice: x: 2, y: 2, z: 4, core: 2. Of those that a mesh axis runs over, the one named last changes fastest.
Arguments:
- science: float32 [8, 512, 1024], P(('grp', 'ccd'), 'row', 'amp'), parts along dimension 0, may hold values from -6 to 6
- template: bfloat16 [8, 2, 2, 8, 32, 512], P(('grp', 'ccd'), 'row', 'amp'), parts along dimension 0, may hold values from -6 to 6
- owners: int32 [8, 2, 2, 8, 1], P(('grp', 'ccd'), 'row', 'amp'), parts along dimension 0, may hold values from 0 to 3; in each aligned block of 8 rows (0 to 7, 8 to 15, ..., all dimensions but the last counted through in order) at most 2 rows name the same one
- patch_strip: int32 [8, 2, 2, 8], P(('grp', 'ccd'), 'row', 'amp'), parts along dimension 0, may hold values from 0 to 7
- shifts: int32 [8, 2, 2, 2, 8], P(('grp', 'ccd'), 'row', 'amp'), parts along dimension 0, may hold values from -3 to 3
- fractions: float32 [8, 2, 2, 2, 8], P(('grp', 'ccd'), 'row', 'amp'), parts along dimension 0, may hold values from 0.05 to 0.95
- coefs: float32 [8, 3, 9], P(('grp', 'ccd')), parts along dimension 0, may hold values from -3 to 3
Outputs:
- difference: float32 [8, 512, 1024], P(('grp', 'ccd'), 'row', 'amp'), parts along dimension 0
- stack: float32 [8, 2, 2, 8, 32, 512], P(('grp', 'ccd'), 'row', 'amp'), parts along dimension 0
There are 2 independent parts, one for each index of `grp`. A program takes and returns all parts, laid end to end along the dimension named above; each array names one. Nothing has to cross between parts.
Inputs may be any that keep to these rules, and one draw needn't show every extreme that they name: Among the 8 strips of one device's block no owner is named more than 2 times, and some block names one owner exactly 2 times in every draw; owners lie in the same row band and column half as the block.
All inputs are finite; a program needn't handle non-finite values.
Results may differ from a plain program's by a relative error of at most 0.0057.
Values may be sent and summed in bfloat16 or wider, within the bound.
A program may use at most 64 MiB of HBM per device.

v0:
```python
import jax
import jax.numpy as jnp
from jax import lax
from jax.sharding import PartitionSpec as P

RADIUS = 9


tap_margin = 6


def padded_2(value, sides, width):
    for axis, dim in sides:
        devices, length = (lax.axis_size(axis), value.shape[dim])
        up = [(i, (i + 1) % devices) for i in range(devices - 1)]
        down = [(j, i) for i, j in up]
        last = lax.slice_in_dim(value, length - width, length, axis=dim)
        first = lax.slice_in_dim(value, 0, width, axis=dim)
        before = lax.ppermute(last, axis, up)
        after = lax.ppermute(first, axis, down)
        value = jnp.concatenate([before, value, after], axis=dim)
    return value


def lanczos_taps(fraction):
    offsets = jnp.arange(-2, 4).astype(jnp.float32)
    spread = offsets[None, :] - fraction[:, None]
    return (jnp.sinc(spread) * jnp.sinc(spread / 3.0)).astype(jnp.bfloat16)


def kernel_table():
    support = jnp.arange(-RADIUS, RADIUS + 1).astype(jnp.float32)
    narrow = jnp.exp(-support * support / 4.5)
    slope = support * jnp.exp(-support * support / 12.5)
    broad = jnp.exp(-support * support / 40.5)
    return jnp.stack(
        [narrow / jnp.sum(narrow), slope / jnp.sum(jnp.abs(slope)), broad / jnp.sum(broad)]
    ).astype(jnp.bfloat16)


def strip_operator(taps, shift, strip_rows):
    out_rows = jnp.arange(strip_rows)[None, :, None]
    src_rows = jnp.arange(strip_rows)[None, None, :]
    offset = src_rows - out_rows - shift[:, None, None]
    table = jnp.zeros(offset.shape, jnp.bfloat16)
    for which in range(6):
        table = jnp.where(offset == which - 2, taps[:, which][:, None, None], table)
    return table


def shift_columns(values, taps, starts, width):

    def one_strip(block, tap_row, start_row):
        total = jnp.zeros((block.shape[0], width), jnp.float32)
        for which in range(6):
            moved = lax.dynamic_slice_in_dim(block, start_row[which], width, 1)
            total = total + tap_row[which].astype(jnp.float32) * moved.astype(jnp.float32)
        return total

    return jax.vmap(one_strip)(values, taps, starts)


def shift_weights(taps, shift):
    offsets = jnp.arange(-5, 7)[None, :, None]
    steps = (jnp.arange(6) - 2)[None, None, :]
    hit = offsets == shift[:, None, None] + steps
    return jnp.sum(jnp.where(hit, taps.astype(jnp.float32)[:, None, :], 0.0), axis=2)


def static_shift(values, weights, sign, width):
    wide = jnp.pad(values, ((0, 0), (0, 0), (tap_margin, tap_margin)))
    total = jnp.zeros((values.shape[0], values.shape[1], width), jnp.float32)
    for which in range(12):
        start = tap_margin + sign * (which - 5)
        moved = lax.slice_in_dim(wide, start, start + width, axis=2).astype(jnp.float32)
        total = total + weights[:, which][:, None, None] * moved
    return total


def band_operator(kernel, count):
    out_place = jnp.arange(count)[:, None]
    src_place = jnp.arange(count + 2 * RADIUS)[None, :]
    spacing = src_place - out_place
    table = jnp.zeros(spacing.shape, jnp.bfloat16)
    for offset in range(2 * RADIUS + 1):
        table = jnp.where(spacing == offset, kernel[offset], table)
    return table


def body(science, template, owners, patch_strip, shifts, fractions, coefs):
    ccd_count = lax.axis_size("ccd")
    row_count = lax.axis_size("row")
    amp_count = lax.axis_size("amp")
    band_rows = science.shape[1]
    half_cols = science.shape[2]
    strips = template.shape[3]
    strip_rows = template.shape[4]
    strip_size = strip_rows * half_cols
    capacity = max(2, strips // ccd_count)
    owner_list = owners.reshape(strips)
    strip_list = patch_strip.reshape(strips)
    earlier = jnp.arange(strips)[None, :] < jnp.arange(strips)[:, None]
    same_owner = owner_list[None, :] == owner_list[:, None]
    place_rank = jnp.sum(jnp.where(earlier & same_owner, 1, 0), axis=1).astype(jnp.int32)
    slot_index = owner_list * capacity + place_rank
    slot_match = jnp.arange(ccd_count * capacity)[:, None] == slot_index[None, :]
    wanted = jnp.sum(jnp.where(slot_match, strip_list[None, :] + 1, 0), axis=1) - 1
    asked = lax.all_to_all(
        wanted.reshape(ccd_count, capacity), "ccd", split_axis=0, concat_axis=0, tiled=True
    )
    asked_flat = asked.reshape(ccd_count * capacity)
    global_index = owner_list * strips + strip_list
    rows_here = lax.all_gather(template, "ccd", axis=0, tiled=True).reshape(-1, strip_size)
    labels = jnp.arange(rows_here.shape[0])
    select = (global_index[:, None] == labels[None, :]).astype(jnp.bfloat16)
    chosen = jnp.dot(select, rows_here, preferred_element_type=jnp.float32)
    chosen = chosen.astype(jnp.bfloat16)
    chosen = chosen.reshape(strips, strip_rows, half_cols)
    row_taps = lanczos_taps(fractions[0, 0, 0, 0])
    col_taps = lanczos_taps(fractions[0, 0, 0, 1])
    row_shift = shifts[0, 0, 0, 0]
    col_shift = shifts[0, 0, 0, 1]
    tap_steps = jnp.arange(6) - 2
    row_warp = strip_operator(row_taps, row_shift, strip_rows)
    rows_done = jnp.einsum(
        "qik,qkz->qiz", row_warp, chosen, preferred_element_type=jnp.float32
    ).astype(jnp.bfloat16)
    col_weights = shift_weights(col_taps, col_shift)
    warped = static_shift(rows_done, col_weights, 1, half_cols).astype(jnp.bfloat16)
    image = warped.reshape(band_rows, half_cols)
    padded = padded_2(image, (("row", 0), ("amp", 1)), RADIUS)
    kernels = kernel_table()
    row_place = (
        (lax.axis_index("row") * band_rows + jnp.arange(band_rows) + 0.5)
        / (band_rows * row_count)
        * 2.0
        - 1.0
    )[:, None]
    col_place = (
        (lax.axis_index("amp") * half_cols + jnp.arange(half_cols) + 0.5)
        / (half_cols * amp_count)
        * 2.0
        - 1.0
    )[None, :]
    coef_block = coefs[0]
    row_mats = jnp.concatenate([band_operator(kernels[kind], band_rows) for kind in range(3)], axis=0)
    column_mats = jnp.concatenate(
        [band_operator(kernels[kind], half_cols).T for kind in range(3)], axis=1
    )
    row_mats, column_mats = lax.optimization_barrier((row_mats, column_mats))
    across_all = jnp.dot(row_mats, padded, preferred_element_type=jnp.float32).astype(jnp.bfloat16)
    terms = jnp.dot(across_all, column_mats, preferred_element_type=jnp.float32)
    model = jnp.zeros((band_rows, half_cols), jnp.float32)
    for first in range(3):
        for second in range(3):
            basis = first * 3 + second
            term = terms[first * band_rows:(first + 1) * band_rows, second * half_cols:(second + 1) * half_cols]
            weight = (
                coef_block[0, basis]
                + coef_block[1, basis] * col_place
                + coef_block[2, basis] * row_place
            )
            model = model + weight * term
    difference = science[0] - model
    lowered = difference.astype(jnp.bfloat16).reshape(strips, strip_rows, half_cols)
    columns_back = static_shift(lowered, col_weights, -1, half_cols).astype(jnp.bfloat16)
    contribution = jnp.einsum(
        "qik,qiz->qkz", row_warp, columns_back, preferred_element_type=jnp.float32
    )
    outgoing_back = (
        jnp.zeros((ccd_count * capacity, strip_size), jnp.float32)
        .at[slot_index]
        .set(contribution.reshape(strips, strip_size))
    )
    returned = lax.all_to_all(
        outgoing_back.reshape(ccd_count, capacity, strip_size),
        "ccd",
        split_axis=0,
        concat_axis=0,
        tiled=True,
    )
    owner_select = (asked_flat[:, None] == jnp.arange(strips)[None, :]).astype(jnp.float32)
    stack = jnp.einsum(
        "sp,sz->pz",
        owner_select,
        returned.reshape(ccd_count * capacity, strip_size),
        precision=lax.Precision.HIGHEST,
    )
    return (difference[None], stack.reshape(template.shape))


def solution(mesh):
    return jax.shard_map(
        body,
        mesh=mesh,
        in_specs=(
            P(("grp", "ccd"), "row", "amp"),
            P(("grp", "ccd"), "row", "amp", None, None, None),
            P(("grp", "ccd"), "row", "amp", None, None),
            P(("grp", "ccd"), "row", "amp", None),
            P(("grp", "ccd"), "row", "amp", None, None),
            P(("grp", "ccd"), "row", "amp", None, None),
            P(("grp", "ccd"), None, None),
        ),
        out_specs=(
            P(("grp", "ccd"), "row", "amp"),
            P(("grp", "ccd"), "row", "amp", None, None, None),
        ),
        check_vma=False,
    )
```

profile of v0, /device:TPU:0, one launch (start us, length us, event | category | flops | bytes accessed | tf_op | source)
XLA Modules:
  0.0 173.9 jit_solution(10974692560965353115)
XLA Ops:
  7.2 0.7 all-gather.2.cloned.1.call-update
  7.9 0.9 select_reduce_fusion.2
  8.8 0.7 multiply_add_fusion.15
  9.5 0.1 select_reduce_fusion.1
  9.6 0.6 sub.846
  10.3 6.3 %all-to-all-start = ((s32[4,1,2]{2,1,0:T(1,128)}), s32[4,1,2]{2,1,0:T(1,128)S(1)}, u32[]{:S(2)}, u32[]{:S(2)}) async-start(s32[4,1,2]{2,1,0:T(1,128)} %bitcast.100), calls=%async_computation | async-start | bytes 4096 | tf_op jit(solution)/shard_map/all_to_all | solution.py:108
  16.6 0.6 exponential_reduce_fusion
  17.3 0.6 abs_reduce_fusion
  17.9 0.6 exponential_reduce_fusion.1
  18.5 0.7 copy.37
  19.2 0.7 fusion.307
  19.9 0.7 fusion.308
  20.6 0.7 fusion.285
  21.2 0.8 slice_bitcast_fusion.8
  22.0 0.1 fusion.282
  22.1 0.8 slice_bitcast_fusion.9
  23.0 0.4 slice_reduce_fusion.11
  23.4 0.7 divide_convert_fusion
  24.1 0.7 fusion.311
  24.8 0.6 divide_convert_fusion.1
  25.5 0.7 fusion.310
  26.2 0.6 divide_convert_fusion.2
  26.8 0.7 fusion.309
  27.5 1.2 broadcast_multiply_fusion
  28.7 1.3 broadcast_multiply_fusion.2
  30.0 1.2 broadcast_multiply_fusion.4
  31.2 2.5 %multiply_add_fusion.4 = (f32[512]{0:T(512)S(1)}, f32[512]{0:T(512)S(1)}) fusion(f32[]{:T(128)} %bitcast.97, f32[]{:T(128)} %bitcast.96, s32[]{:T(128)S(6)} %mul.605, f32[]{:T(128)} %bitcast.94, f32[]{:T(128)} %bitcast.93), kind=kLoop, calls=%fused_computation.374 | loop fusion | flops 4608 | bytes 4116 | tf_op jit(solution)/shard_map/add | solution.py:159
  33.8 2.5 %multiply_add_fusion.6 = (f32[512]{0:T(512)S(1)}, f32[512]{0:T(512)S(1)}) fusion(f32[]{:T(128)} %bitcast.91, f32[]{:T(128)} %bitcast.90, s32[]{:T(128)S(6)} %mul.605, f32[]{:T(128)} %bitcast.88, f32[]{:T(128)} %bitcast.87), kind=kLoop, calls=%fused_computation.376 | loop fusion | flops 4608 | bytes 4116 | tf_op jit(solution)/shard_map/add | solution.py:159
  36.2 2.6 %multiply_add_fusion.8 = (f32[512]{0:T(512)S(1)}, f32[512]{0:T(512)S(1)}) fusion(f32[]{:T(128)} %bitcast.85, f32[]{:T(128)} %bitcast.84, s32[]{:T(128)S(6)} %mul.605, f32[]{:T(128)} %bitcast.82, f32[]{:T(128)} %bitcast.81), kind=kLoop, calls=%fused_computation.378 | loop fusion | flops 4608 | bytes 4116 | tf_op jit(solution)/shard_map/add | solution.py:159
  38.8 2.6 %multiply_add_fusion.10 = (f32[512]{0:T(512)S(1)}, f32[512]{0:T(512)S(1)}) fusion(f32[]{:T(128)} %bitcast.79, f32[]{:T(128)} %bitcast.78, s32[]{:T(128)S(6)} %mul.605, f32[]{:T(128)} %bitcast.76, f32[]{:T(128)} %bitcast.75), kind=kLoop, calls=%fused_computation.380 | loop fusion | flops 4608 | bytes 4116 | tf_op jit(solution)/shard_map/add | solution.py:159
  41.4 12.1 %fusion.106 = bf16[256,274]{1,0:T(8,128)(2,1)S(1)} fusion(bf16[]{:T(256)} %bitcast.41, bf16[]{:T(256)} %bitcast.40, bf16[]{:T(256)} %bitcast.39, bf16[]{:T(256)} %bitcast.38, bf16[]{:T(256)} %bitcast.37, bf16[]{:T(256)} %bitcast.36, bf16[]{:T(256)} %bitcast.35, bf16[]{:T(256)} %bitcast.34, bf16[]{:T(256)} %bitcast.33, bf16[]{:T(256)} %bitcast.32, ...), kind=kLoop, calls=%fused_computation.133 | loop fusion | flops 2735616 | bytes 140326 | tf_op jit(solution)/shard_map/jit(_where)/select_n | solution.py:86
  53.5 11.8 %fusion.107 = bf16[256,274]{1,0:T(8,128)(2,1)S(1)} fusion(bf16[]{:T(256)} %bitcast.22, bf16[]{:T(256)} %bitcast.21, bf16[]{:T(256)} %bitcast.20, bf16[]{:T(256)} %bitcast.19, bf16[]{:T(256)} %bitcast.18, bf16[]{:T(256)} %bitcast.17, bf16[]{:T(256)} %bitcast.16, bf16[]{:T(256)} %bitcast.15, bf16[]{:T(256)} %bitcast.14, bf16[]{:T(256)} %bitcast.13, ...), kind=kLoop, calls=%fused_computation.134 | loop fusion | flops 2735616 | bytes 140326 | tf_op jit(solution)/shard_map/jit(_where)/select_n | solution.py:86
  65.4 12.0 %fusion.105 = bf16[256,274]{1,0:T(8,128)(2,1)S(1)} fusion(bf16[]{:T(256)} %bitcast.60, bf16[]{:T(256)} %bitcast.59, bf16[]{:T(256)} %bitcast.58, bf16[]{:T(256)} %bitcast.57, bf16[]{:T(256)} %bitcast.56, bf16[]{:T(256)} %bitcast.55, bf16[]{:T(256)} %bitcast.54, bf16[]{:T(256)} %bitcast.53, bf16[]{:T(256)} %bitcast.52, bf16[]{:T(256)} %bitcast.51, ...), kind=kLoop, calls=%fused_computation.132 | loop fusion | flops 2735616 | bytes 140326 | tf_op jit(solution)/shard_map/jit(_where)/select_n | solution.py:86
  77.4 1.2 multiply_add_fusion.12
  78.6 12.2 %fusion.20 = bf16[530,512]{1,0:T(8,128)(2,1)S(1)} fusion(bf16[]{:T(256)} %bitcast.60, bf16[]{:T(256)} %bitcast.59, bf16[]{:T(256)} %bitcast.58, bf16[]{:T(256)} %bitcast.57, bf16[]{:T(256)} %bitcast.56, bf16[]{:T(256)} %bitcast.55, bf16[]{:T(256)} %bitcast.54, bf16[]{:T(256)} %bitcast.53, bf16[]{:T(256)} %bitcast.52, bf16[]{:T(256)} %bitcast.51, ...), kind=kLoop, calls=%fused_computation.28 | loop fusion | flops 10583040 | bytes 542758 | tf_op jit(solution)/shard_map/jit(_where)/select_n | solution.py:86
  90.8 12.3 %fusion.21 = bf16[530,512]{1,0:T(8,128)(2,1)S(1)} fusion(bf16[]{:T(256)} %bitcast.41, bf16[]{:T(256)} %bitcast.40, bf16[]{:T(256)} %bitcast.39, bf16[]{:T(256)} %bitcast.38, bf16[]{:T(256)} %bitcast.37, bf16[]{:T(256)} %bitcast.36, bf16[]{:T(256)} %bitcast.35, bf16[]{:T(256)} %bitcast.34, bf16[]{:T(256)} %bitcast.33, bf16[]{:T(256)} %bitcast.32, ...), kind=kLoop, calls=%fused_computation.29 | loop fusion | flops 10583040 | bytes 542758 | tf_op jit(solution)/shard_map/jit(_where)/select_n | solution.py:86
  103.1 12.0 %fusion.22 = bf16[530,512]{1,0:T(8,128)(2,1)S(1)} fusion(bf16[]{:T(256)} %bitcast.22, bf16[]{:T(256)} %bitcast.21, bf16[]{:T(256)} %bitcast.20, bf16[]{:T(256)} %bitcast.19, bf16[]{:T(256)} %bitcast.18, bf16[]{:T(256)} %bitcast.17, bf16[]{:T(256)} %bitcast.16, bf16[]{:T(256)} %bitcast.15, bf16[]{:T(256)} %bitcast.14, bf16[]{:T(256)} %bitcast.13, ...), kind=kLoop, calls=%fused_computation.30 | loop fusion | flops 10583040 | bytes 542758 | tf_op jit(solution)/shard_map/jit(_where)/select_n | solution.py:86
  115.2 0.1 pad_maximum_fusion
  115.3 1.8 %copy.32 = bf16[4,8,32,512]{3,1,2,0:T(8,128)(2,1)S(1)} copy(bf16[4,8,32,512]{3,2,1,0:T(8,128)(2,1)} %bitcast.152) | data formatting | bytes 2097152
  117.1 0.3 convolution_convert_fusion
  117.4 0.4 convolution_convert_fusion.2
  117.8 1.2 add_convert_fusion.1
  119.1 3.4 %collective-permute-start = (bf16[9,512]{1,0:T(8,128)(2,1)S(1)}, bf16[9,512]{1,0:T(8,128)(2,1)S(1)}, u32[]{:S(2)}, u32[]{:S(2)}) collective-permute-start(bf16[9,512]{1,0:T(8,128)(2,1)S(1)} %get-tuple-element.33), channel_id=1, source_target_pairs={{0,2},{1,3},{4,6},{5,7},{8,10},{9,11},{12,14},{13,15},{16,18},{17,... | collective-permute-start | bytes 27656 | tf_op jit(solution)/shard_map/ppermute | solution.py:19
  122.5 1.3 collective-permute-start.1
  123.8 1.3 broadcast_multiply_fusion.6
  125.0 3.1 %collective-permute-done.1 = bf16[9,512]{1,0:T(8,128)(2,1)S(1)} collective-permute-done((bf16[9,512]{1,0:T(8,128)(2,1)S(1)}, bf16[9,512]{1,0:T(8,128)(2,1)S(1)}, u32[]{:S(2)}, u32[]{:S(2)}) %collective-permute-start.1) | collective-permute-done | bytes 9248 | tf_op jit(solution)/shard_map/ppermute | solution.py:20
  128.1 0.1 pad_maximum_fusion.4
  128.2 1.3 collective-permute-start.2
  129.5 1.5 collective-permute-start.3
  131.0 0.6 fusion.286
  131.7 1.0 collective-permute-done.3
  132.7 5.2 %fusion = f32[768,1536]{1,0:T(8,128)} fusion(bf16[530,1536]{1,0:T(8,128)(2,1)S(1)} %pad_maximum_fusion, bf16[768,274]{1,0:T(8,128)(2,1)S(1)} %pad_maximum_fusion.1, bf16[274,9]{1,0:T(8,128)(2,1)S(1)} %collective-permute-done.3, bf16[9,512]{1,0:T(8,128)(2,1)S(1)} %collective-permute-done.1, bf16[256,512]{1,0:T(8,128)(2,1)S(1)} %bitcast.151, ...), kind=kOutput, calls=%fused_computation.7 | convolution fusion | flops 1475344000 | bytes 7058056 | tf_op jit(solution)/shard_map/dot_general | solution.py:152
  137.9 3.7 %fusion.304 = (bf16[256,512]{1,0:T(8,128)(2,1)S(1)}, f32[256,512]{1,0:T(8,128)}) fusion(f32[768,1536]{1,0:T(8,128)} %fusion, f32[256]{0:T(256)S(1)} %get-tuple-element.134, f32[512]{0:T(512)S(1)} %get-tuple-element.142, f32[256]{0:T(256)S(1)} %get-tuple-element.135, f32[512]{0:T(512)S(1)} %get-tuple-element.143, f32[256]{0:T(256)S(1)} %get-tuple-element.136, ...), kind=kLoop, calls=%fused_computation.440 | loop fusion | flops 3670016 | bytes 6056960 | tf_op jit(solution)/shard_map/convert_element_type | solution.py:165
  141.7 1.2 convolution_bitcast_fusion.1
  142.9 0.3 copy.33
  143.2 1.0 scatter_custom_fusion
  144.2 1.1 reshape.463
  145.3 5.1 %all-to-all-start.1 = ((f32[4,2,16384]{2,1,0:T(2,128)}), f32[4,2,16384]{2,1,0:T(2,128)S(1)}, u32[]{:S(2)}, u32[]{:S(2)}) async-start(f32[4,2,16384]{2,1,0:T(2,128)} %reshape.463), calls=%async_computation.1 | async-start | bytes 1048576 | tf_op jit(solution)/shard_map/all_to_all | solution.py:175
  150.4 0.6 broadcast.1084
  151.0 0.7 reduce.27
  151.8 13.4 %all-to-all-done.1 = f32[4,2,16384]{2,1,0:T(2,128)S(1)} async-done(((f32[4,2,16384]{2,1,0:T(2,128)}), f32[4,2,16384]{2,1,0:T(2,128)S(1)}, u32[]{:S(2)}, u32[]{:S(2)}) %all-to-all-start.1) | async-done | bytes 524320 | tf_op jit(solution)/shard_map/all_to_all | solution.py:175
  165.2 0.4 reshape.464
  165.6 0.4 convolution_bitcast_fusion
  166.0 1.1 copy.29
  (18 shorter events, 0.4 us)
Async XLA Ops:
  7.2 108.1 %all-gather.2.cloned.1.call-start = ((), (), s32[]{:S(2)}) async-start(), calls=%async_computation.2 | async-start | bytes 1310720 | tf_op jit(solution)/shard_map/all_gather | solution.py:113
  10.3 135.1 %all-to-all-start = ((s32[4,1,2]{2,1,0:T(1,128)}), s32[4,1,2]{2,1,0:T(1,128)S(1)}, u32[]{:S(2)}, u32[]{:S(2)}) async-start(s32[4,1,2]{2,1,0:T(1,128)} %bitcast.100), calls=%async_computation | async-start | bytes 4096 | tf_op jit(solution)/shard_map/all_to_all | solution.py:108
  119.1 6.0 %collective-permute-start = (bf16[9,512]{1,0:T(8,128)(2,1)S(1)}, bf16[9,512]{1,0:T(8,128)(2,1)S(1)}, u32[]{:S(2)}, u32[]{:S(2)}) collective-permute-start(bf16[9,512]{1,0:T(8,128)(2,1)S(1)} %get-tuple-element.33), channel_id=1, source_target_pairs={{0,2},{1,3},{4,6},{5,7},{8,10},{9,11},{12,14},{13,15},{16,18},{17,... | collective-permute-start | bytes 27656 | tf_op jit(solution)/shard_map/ppermute | solution.py:19
  122.5 5.6 %collective-permute-start.1 = (bf16[9,512]{1,0:T(8,128)(2,1)S(1)}, bf16[9,512]{1,0:T(8,128)(2,1)S(1)}, u32[]{:S(2)}, u32[]{:S(2)}) collective-permute-start(bf16[9,512]{1,0:T(8,128)(2,1)S(1)} %get-tuple-element.34), channel_id=1, source_target_pairs={{2,0},{3,1},{6,4},{7,5},{10,8},{11,9},{14,12},{15,13},{18,16},{19,... | collective-permute-start | bytes 27656 | tf_op jit(solution)/shard_map/ppermute | solution.py:20
  128.2 3.4 %collective-permute-start.2 = (bf16[274,9]{1,0:T(8,128)(2,1)S(1)}, bf16[274,9]{1,0:T(8,128)(2,1)S(1)}, u32[]{:S(2)}, u32[]{:S(2)}) collective-permute-start(bf16[274,9]{1,0:T(8,128)(2,1)S(1)} %get-tuple-element.31), channel_id=1, source_target_pairs={{0,1},{2,3},{4,5},{6,7},{8,9},{10,11},{12,13},{14,15},{16,17},{18,... | collective-permute-start | bytes 14804 | tf_op jit(solution)/shard_map/ppermute | solution.py:19
  129.5 3.2 %collective-permute-start.3 = (bf16[274,9]{1,0:T(8,128)(2,1)S(1)}, bf16[274,9]{1,0:T(8,128)(2,1)S(1)}, u32[]{:S(2)}, u32[]{:S(2)}) collective-permute-start(bf16[274,9]{1,0:T(8,128)(2,1)S(1)} %get-tuple-element.32), channel_id=1, source_target_pairs={{1,0},{3,2},{5,4},{7,6},{9,8},{11,10},{13,12},{15,14},{17,16},{19,... | collective-permute-start | bytes 14804 | tf_op jit(solution)/shard_map/ppermute | solution.py:20
  131.6 6.3 %copy-start = (f32[1,256,512]{2,1,0:T(8,128)S(1)}, f32[1,256,512]{2,1,0:T(8,128)}, u32[]{:S(2)}) copy-start(f32[1,256,512]{2,1,0:T(8,128)} %param.8) | copy-start | bytes 1572868
  145.3 19.9 %all-to-all-start.1 = ((f32[4,2,16384]{2,1,0:T(2,128)}), f32[4,2,16384]{2,1,0:T(2,128)S(1)}, u32[]{:S(2)}, u32[]{:S(2)}) async-start(f32[4,2,16384]{2,1,0:T(2,128)} %reshape.463), calls=%async_computation.1 | async-start | bytes 1048576 | tf_op jit(solution)/shard_map/all_to_all | solution.py:175
Sparse Core Ops, SparseCore 0:
  9.5 30.6 all-gather.1
where the time goes:
time: 176 us; the launch traced here: 174 us
  other arithmetic  102 us (58%)
  starting transfers between devices  18.9 us (11%)
  waiting for transfers between devices  18.2 us (10%)
  between operations  14.3 us (8%)
  local copies, waits for them, and re-layouts  13.2 us (8%)
  matrix products  7.54 us (4%)
    select_n x6, other arithmetic, band_operator(): table = jnp.where(spacing == offset, kernel[offset], table)  72.5 us
    all_to_all x1, waiting for transfers between devices, body(): lax.all_to_all(outgoing_back.reshape(ccd_count, capacity, strip_size), 'c...  13.4 us
    add x5, other arithmetic, body(): coef_block[0, basis] + coef_block[1, basis] * col_place  11.3 us
    all_to_all x1, starting transfers between devices, body(): lax.all_to_all(wanted.reshape(ccd_count, capacity), 'ccd', split_axis=0,...  6.35 us
    mul x5, other arithmetic, body(): coef_block[2, basis] * row_place  5.61 us
    dot_general x1, matrix products, body(): terms = jnp.dot(across_all, column_mats, preferred_element_type=jnp.float32)  5.23 us
    all_to_all x1, starting transfers between devices, body(): lax.all_to_all(outgoing_back.reshape(ccd_count, capacity, strip_size), 'c...  5.09 us
    ppermute x2, starting transfers between devices, padded_2(): before = lax.ppermute(last, axis, up)  4.69 us
  transfers between devices with their start and end apart: 7, of which 3 were waited for; matrix products, arithmetic and copies ran while one was open for 69% of the time, Pallas kernels for 0%

commit v1 on v0

--- a/solution.py
+++ b/solution.py
@@ -78,13 +78,10 @@
 
 
 def band_operator(kernel, count):
-    out_place = jnp.arange(count)[:, None]
-    src_place = jnp.arange(count + 2 * RADIUS)[None, :]
-    spacing = src_place - out_place
-    table = jnp.zeros(spacing.shape, jnp.bfloat16)
-    for offset in range(2 * RADIUS + 1):
-        table = jnp.where(spacing == offset, kernel[offset], table)
-    return table
+    line = jnp.concatenate([kernel, jnp.zeros((count,), kernel.dtype)])
+    width = count + 2 * RADIUS
+    flat = jnp.tile(line, count)[: count * width]
+    return flat.reshape(count, width)
 
 
 def body(science, template, owners, patch_strip, shifts, fractions, coefs):
@@ -125,6 +122,7 @@
     rows_done = jnp.einsum(
         "qik,qkz->qiz", row_warp, chosen, preferred_element_type=jnp.float32
     ).astype(jnp.bfloat16)
+    rows_done = lax.optimization_barrier(rows_done)
     col_weights = shift_weights(col_taps, col_shift)
     warped = static_shift(rows_done, col_weights, 1, half_cols).astype(jnp.bfloat16)
     image = warped.reshape(band_rows, half_cols)
@@ -163,6 +161,7 @@
             model = model + weight * term
     difference = science[0] - model
     lowered = difference.astype(jnp.bfloat16).reshape(strips, strip_rows, half_cols)
+    lowered = lax.optimization_barrier(lowered)
     columns_back = static_shift(lowered, col_weights, -1, half_cols).astype(jnp.bfloat16)
     contribution = jnp.einsum(
         "qik,qiz->qkz", row_warp, columns_back, preferred_element_type=jnp.float32

time: 176 us -> 112 us (0.64)
  other arithmetic: 102 us -> 30.1 us
  local copies, waits for them, and re-layouts: 13.2 us -> 20.7 us
    select_n x6 -> x0, other arithmetic: 72.5 us -> none  [band_operator(): table = jnp.where(spacing == offset, kernel[offset], table)]
    reshape x0 -> x6, local copies, waits for them, and re-layouts: none -> 4.74 us  [band_operator(): return flat.reshape(count, width)]
    another operation x0 -> x12, local copies, waits for them, and re-layouts: none -> 4.16 us  [band_operator(): flat = jnp.tile(line, count)[:count * width]]
    slice x3, local copies, waits for them, and re-layouts: 2.18 us -> 0.11 us  [band_operator(): flat = jnp.tile(line, count)[:count * width]]
    squeeze x0 -> x3, other arithmetic: none -> 1.89 us  [body(): kernels[kind]]
    another operation x3 -> x0, other arithmetic: 1.89 us -> none
    unnamed x6 -> x12, local copies, waits for them, and re-layouts: 3.91 us -> 4.55 us
  transfers between devices with their start and end apart: 7 -> 7, of which waited for: 3 -> 3; matrix products, arithmetic and copies ran while one was open for 69% -> 51% of each run, Pallas kernels for 0% -> 0%
where the time goes in v1:
time: 112 us; the launch traced here: 111 us
  other arithmetic  30.1 us (27%)
  local copies, waits for them, and re-layouts  20.7 us (18%)
  waiting for transfers between devices  18.8 us (17%)
  starting transfers between devices  18.7 us (17%)
  between operations  14.5 us (13%)
  matrix products  8.27 us (7%)
    all_to_all x1, waiting for transfers between devices, body(): lax.all_to_all(outgoing_back.reshape(ccd_count, capacity, strip_size), 'c...  14.3 us
    add x5, other arithmetic, body(): coef_block[0, basis] + coef_block[1, basis] * col_place  11.4 us
    all_to_all x1, starting transfers between devices, body(): lax.all_to_all(wanted.reshape(ccd_count, capacity), 'ccd', split_axis=0,...  6.35 us
    dot_general x1, matrix products, body(): terms = jnp.dot(across_all, column_mats, preferred_element_type=jnp.float32)  5.97 us
    mul x5, other arithmetic, body(): coef_block[2, basis] * row_place  5.54 us
    all_to_all x1, starting transfers between devices, body(): lax.all_to_all(outgoing_back.reshape(ccd_count, capacity, strip_size), 'c...  5.09 us
    reshape x6, local copies, waits for them, and re-layouts, band_operator(): return flat.reshape(count, width)  4.74 us
    ppermute x2, starting transfers between devices, padded_2(): before = lax.ppermute(last, axis, up)  4.69 us
  transfers between devices with their start and end apart: 7, of which 3 were waited for; matrix products, arithmetic and copies ran while one was open for 51% of the time, Pallas kernels for 0%

profile of v1, /device:TPU:0, one launch (start us, length us, event | category | flops | bytes accessed | tf_op | source)
XLA Modules:
  0.0 111.2 jit_solution(2474861991878700014)
XLA Ops:
  7.2 0.7 all-gather.2.cloned.1.call-update
  7.9 0.9 select_reduce_fusion.2
  8.8 0.7 multiply_add_fusion.15
  9.6 0.7 sub.111
  10.3 6.3 %all-to-all-start = ((s32[4,1,2]{2,1,0:T(1,128)}), s32[4,1,2]{2,1,0:T(1,128)S(1)}, u32[]{:S(2)}, u32[]{:S(2)}) async-start(s32[4,1,2]{2,1,0:T(1,128)} %bitcast.49), calls=%async_computation | async-start | bytes 4096 | tf_op jit(solution)/shard_map/all_to_all | solution.py:105
  16.7 0.6 exponential_reduce_fusion.1
  17.3 0.6 abs_reduce_fusion
  17.9 0.6 exponential_reduce_fusion
  18.5 0.7 copy.37
  19.2 0.7 fusion.155
  19.9 0.7 fusion.156
  20.6 0.8 slice_bitcast_fusion.8
  21.4 0.8 slice_bitcast_fusion.9
  22.1 0.6 convert_bitcast_fusion.2
  22.7 0.7 convert_bitcast_fusion.1
  23.4 1.3 %broadcast_multiply_fusion = (f32[256]{0:T(256)S(1)}, f32[256]{0:T(256)S(1)}) fusion(f32[]{:T(128)} %bitcast.47, s32[]{:T(128)S(6)} %mul.610, f32[]{:T(128)} %bitcast.44), kind=kLoop, calls=%fused_computation.240 | loop fusion | flops 1792 | bytes 2060 | tf_op jit(solution)/shard_map/mul | solution.py:159
  24.6 1.2 %broadcast_multiply_fusion.2 = (f32[256]{0:T(256)S(1)}, f32[256]{0:T(256)S(1)}) fusion(f32[]{:T(128)} %bitcast.41, s32[]{:T(128)S(6)} %mul.610, f32[]{:T(128)} %bitcast.38), kind=kLoop, calls=%fused_computation.242 | loop fusion | flops 1792 | bytes 2060 | tf_op jit(solution)/shard_map/mul | solution.py:159
  25.8 1.3 %broadcast_multiply_fusion.4 = (f32[256]{0:T(256)S(1)}, f32[256]{0:T(256)S(1)}) fusion(f32[]{:T(128)} %bitcast.35, s32[]{:T(128)S(6)} %mul.610, f32[]{:T(128)} %bitcast.32), kind=kLoop, calls=%fused_computation.244 | loop fusion | flops 1792 | bytes 2060 | tf_op jit(solution)/shard_map/mul | solution.py:159
  27.1 1.2 %multiply_add_fusion.12 = f32[512]{0:T(512)S(1)} fusion(s32[]{:T(128)S(6)} %mul.605, f32[]{:T(128)} %bitcast.2, f32[]{:T(128)} %bitcast.1), kind=kLoop, calls=%fused_computation.230 | loop fusion | flops 3584 | bytes 2060 | tf_op jit(solution)/shard_map/add | solution.py:157
  28.3 2.6 %multiply_add_fusion.4 = (f32[512]{0:T(512)S(1)}, f32[512]{0:T(512)S(1)}) fusion(f32[]{:T(128)} %bitcast.46, f32[]{:T(128)} %bitcast.45, s32[]{:T(128)S(6)} %mul.605, f32[]{:T(128)} %bitcast.43, f32[]{:T(128)} %bitcast.42), kind=kLoop, calls=%fused_computation.220 | loop fusion | flops 4608 | bytes 4116 | tf_op jit(solution)/shard_map/add | solution.py:157
  30.9 2.5 %multiply_add_fusion.6 = (f32[512]{0:T(512)S(1)}, f32[512]{0:T(512)S(1)}) fusion(f32[]{:T(128)} %bitcast.40, f32[]{:T(128)} %bitcast.39, s32[]{:T(128)S(6)} %mul.605, f32[]{:T(128)} %bitcast.37, f32[]{:T(128)} %bitcast.36), kind=kLoop, calls=%fused_computation.222 | loop fusion | flops 4608 | bytes 4116 | tf_op jit(solution)/shard_map/add | solution.py:157
  33.5 2.5 %multiply_add_fusion.8 = (f32[512]{0:T(512)S(1)}, f32[512]{0:T(512)S(1)}) fusion(f32[]{:T(128)} %bitcast.34, f32[]{:T(128)} %bitcast.33, s32[]{:T(128)S(6)} %mul.605, f32[]{:T(128)} %bitcast.31, f32[]{:T(128)} %bitcast.30), kind=kLoop, calls=%fused_computation.224 | loop fusion | flops 4608 | bytes 4116 | tf_op jit(solution)/shard_map/add | solution.py:157
  36.0 2.6 %multiply_add_fusion.10 = (f32[512]{0:T(512)S(1)}, f32[512]{0:T(512)S(1)}) fusion(f32[]{:T(128)} %bitcast.28, f32[]{:T(128)} %bitcast.27, s32[]{:T(128)S(6)} %mul.605, f32[]{:T(128)} %bitcast.25, f32[]{:T(128)} %bitcast.24), kind=kLoop, calls=%fused_computation.226 | loop fusion | flops 4608 | bytes 4116 | tf_op jit(solution)/shard_map/add | solution.py:157
  38.5 0.7 convert_bitcast_fusion
  39.3 0.9 tile.61
  40.3 1.2 %reshape.369 = bf16[512,530]{1,0:T(8,128)(2,1)S(1)} reshape(bf16[271360]{0:T(1024)(128)(2,1)S(1)} %slice.392) | data formatting | bytes 1085440 | tf_op jit(solution)/shard_map/reshape | solution.py:84
  41.5 0.9 tile.63
  42.5 1.1 %reshape.370 = bf16[512,530]{1,0:T(8,128)(2,1)S(1)} reshape(bf16[271360]{0:T(1024)(128)(2,1)S(1)} %slice.393) | data formatting | bytes 1085440 | tf_op jit(solution)/shard_map/reshape | solution.py:84
  43.7 0.9 tile.65
  44.6 1.1 %reshape.371 = bf16[512,530]{1,0:T(8,128)(2,1)S(1)} reshape(bf16[271360]{0:T(1024)(128)(2,1)S(1)} %slice.394) | data formatting | bytes 1085440 | tf_op jit(solution)/shard_map/reshape | solution.py:84
  45.8 0.4 tile.25
  46.2 0.4 reshape.366
  46.7 0.4 tile.27
  47.1 0.4 reshape.367
  47.6 0.4 tile.29
  48.0 0.4 reshape.368
  48.7 0.4 slice_reduce_fusion.11
  49.2 1.5 %pad_maximum_fusion = bf16[530,1536]{0,1:T(8,128)(2,1)} fusion(bf16[530,512]{0,1:T(8,128)(2,1)S(1)} %bitcast.105, bf16[530,512]{0,1:T(8,128)(2,1)S(1)} %bitcast.104, bf16[530,512]{0,1:T(8,128)(2,1)S(1)} %bitcast.103), kind=kLoop, calls=%fused_computation.2 | loop fusion | flops 4884480 | bytes 3256320 | tf_op jit(solution)/shard_map/concatenate | solution.py:145
  50.6 1.8 %copy.32 = bf16[4,8,32,512]{3,1,2,0:T(8,128)(2,1)S(1)} copy(bf16[4,8,32,512]{3,2,1,0:T(8,128)(2,1)} %bitcast.110) | data formatting | bytes 2097152
  52.4 0.3 convolution_convert_fusion
  52.8 0.4 convolution_convert_fusion.2
  53.2 1.4 %add_convert_fusion.1 = bf16[8,32,512]{2,1,0:T(8,128)(2,1)S(1)} fusion(bf16[8,32,512]{2,1,0:T(8,128)(2,1)S(1)} %convolution_convert_fusion.2, f32[8]{0:T(128)S(1)} %get-tuple-element.18, f32[8]{0:T(128)S(1)} %get-tuple-element.19, f32[8]{0:T(128)S(1)} %get-tuple-element.20, f32[8]{0:T(128)S(1)} %get-tuple-element.21, f32[8]{0:T(128)S(1)} %get-tuple-element.22, ...), kind=kLoop, calls=%fused_computation.28 | loop fusion | flops 4718592 | bytes 524672 | tf_op jit(solution)/shard_map/convert_element_type | solution.py:127
  54.6 3.4 %collective-permute-start = (bf16[9,512]{1,0:T(8,128)(2,1)S(1)}, bf16[9,512]{1,0:T(8,128)(2,1)S(1)}, u32[]{:S(2)}, u32[]{:S(2)}) collective-permute-start(bf16[9,512]{1,0:T(8,128)(2,1)S(1)} %get-tuple-element.33), channel_id=1, source_target_pairs={{0,2},{1,3},{4,6},{5,7},{8,10},{9,11},{12,14},{13,15},{16,18},{17,... | collective-permute-start | bytes 27656 | tf_op jit(solution)/shard_map/ppermute | solution.py:19
  58.0 1.3 %collective-permute-start.1 = (bf16[9,512]{1,0:T(8,128)(2,1)S(1)}, bf16[9,512]{1,0:T(8,128)(2,1)S(1)}, u32[]{:S(2)}, u32[]{:S(2)}) collective-permute-start(bf16[9,512]{1,0:T(8,128)(2,1)S(1)} %get-tuple-element.34), channel_id=1, source_target_pairs={{2,0},{3,1},{6,4},{7,5},{10,8},{11,9},{14,12},{15,13},{18,16},{19,... | collective-permute-start | bytes 27656 | tf_op jit(solution)/shard_map/ppermute | solution.py:20
  59.3 1.2 %broadcast_multiply_fusion.6 = (f32[256]{0:T(256)S(1)}, f32[256]{0:T(256)S(1)}) fusion(f32[]{:T(128)} %bitcast.29, s32[]{:T(128)S(6)} %mul.610, f32[]{:T(128)} %bitcast.26), kind=kLoop, calls=%fused_computation.246 | loop fusion | flops 1792 | bytes 2060 | tf_op jit(solution)/shard_map/mul | solution.py:159
  60.5 3.1 %collective-permute-done.1 = bf16[9,512]{1,0:T(8,128)(2,1)S(1)} collective-permute-done((bf16[9,512]{1,0:T(8,128)(2,1)S(1)}, bf16[9,512]{1,0:T(8,128)(2,1)S(1)}, u32[]{:S(2)}, u32[]{:S(2)}) %collective-permute-start.1) | collective-permute-done | bytes 9248 | tf_op jit(solution)/shard_map/ppermute | solution.py:20
  63.7 1.3 %collective-permute-start.2 = (bf16[274,9]{1,0:T(8,128)(2,1)S(1)}, bf16[274,9]{1,0:T(8,128)(2,1)S(1)}, u32[]{:S(2)}, u32[]{:S(2)}) collective-permute-start(bf16[274,9]{1,0:T(8,128)(2,1)S(1)} %get-tuple-element.31), channel_id=1, source_target_pairs={{0,1},{2,3},{4,5},{6,7},{8,9},{10,11},{12,13},{14,15},{16,17},{18,... | collective-permute-start | bytes 14804 | tf_op jit(solution)/shard_map/ppermute | solution.py:19
  65.0 1.3 %collective-permute-start.3 = (bf16[274,9]{1,0:T(8,128)(2,1)S(1)}, bf16[274,9]{1,0:T(8,128)(2,1)}, u32[]{:S(2)}, u32[]{:S(2)}) collective-permute-start(bf16[274,9]{1,0:T(8,128)(2,1)S(1)} %get-tuple-element.32), channel_id=1, source_target_pairs={{1,0},{3,2},{5,4},{7,6},{9,8},{11,10},{13,12},{15,14},{17,16},{19,... | collective-permute-start | bytes 14804 | tf_op jit(solution)/shard_map/ppermute | solution.py:20
  66.3 0.6 fusion.134
  67.0 0.6 copy-done.3
  67.6 0.7 collective-permute-done.3
  68.3 6.0 %fusion = f32[768,1536]{1,0:T(8,128)} fusion(bf16[530,1536]{0,1:T(8,128)(2,1)S(1)} %copy-done, bf16[768,274]{1,0:T(8,128)(2,1)S(1)} %pad_maximum_fusion.1, bf16[274,9]{1,0:T(8,128)(2,1)} %collective-permute-done.3, bf16[9,512]{1,0:T(8,128)(2,1)S(1)} %collective-permute-done.1, bf16[256,512]{1,0:T(8,128)(2,1)S(1)} %bitcast.109, ...), kind=kOutput, calls=%fused_computation.7 | convolution fusion | flops 1475344000 | bytes 7058056 | tf_op jit(solution)/shard_map/dot_general | solution.py:150
  74.3 3.7 %fusion.152 = (bf16[256,512]{1,0:T(8,128)(2,1)S(1)}, f32[256,512]{1,0:T(8,128)}) fusion(f32[768,1536]{1,0:T(8,128)} %fusion, f32[256]{0:T(256)S(1)} %get-tuple-element.77, f32[512]{0:T(512)S(1)} %get-tuple-element.85, f32[256]{0:T(256)S(1)} %get-tuple-element.78, f32[512]{0:T(512)S(1)} %get-tuple-element.86, f32[256]{0:T(256)S(1)} %get-tuple-element.79, ...), kind=kLoop, calls=%fused_computation.286 | loop fusion | flops 3670016 | bytes 6056960 | tf_op jit(solution)/shard_map/convert_element_type | solution.py:163
  78.0 1.2 %convolution_bitcast_fusion.1 = f32[1,8,32,512]{3,2,1,0:T(8,128)S(1)} fusion(bf16[8,32,512]{2,1,0:T(8,128)(2,1)S(1)} %bitcast.116, f32[8]{0:T(128)S(1)} %get-tuple-element.18, f32[8]{0:T(128)S(1)} %get-tuple-element.19, f32[8]{0:T(128)S(1)} %get-tuple-element.20, f32[8]{0:T(128)S(1)} %get-tuple-element.21, f32[8]{0:T(128)S(1)} %get-tuple-element.22, ...), kind=kOutput, calls=%fused_computation.5 | convolution fusion | flops 13213696 | bytes 791040 | tf_op jit(solution)/shard_map/qik,qiz->qkz/dot_general | solution.py:166
  79.2 0.3 copy.33
  79.6 1.0 scatter_custom_fusion
  80.6 1.1 reshape.379
  81.7 5.1 %all-to-all-start.1 = ((f32[4,2,16384]{2,1,0:T(2,128)}), f32[4,2,16384]{2,1,0:T(2,128)S(1)}, u32[]{:S(2)}, u32[]{:S(2)}) async-start(f32[4,2,16384]{2,1,0:T(2,128)} %reshape.379), calls=%async_computation.1 | async-start | bytes 1048576 | tf_op jit(solution)/shard_map/all_to_all | solution.py:174
  86.8 0.6 broadcast.701
  87.4 0.7 reduce.27
  88.2 14.3 %all-to-all-done.1 = f32[4,2,16384]{2,1,0:T(2,128)S(1)} async-done(((f32[4,2,16384]{2,1,0:T(2,128)}), f32[4,2,16384]{2,1,0:T(2,128)S(1)}, u32[]{:S(2)}, u32[]{:S(2)}) %all-to-all-start.1) | async-done | bytes 524320 | tf_op jit(solution)/shard_map/all_to_all | solution.py:174
  102.5 0.4 reshape.380
  102.8 0.4 convolution_bitcast_fusion
  103.2 1.1 copy.29
  (42 shorter events, 1.1 us)
Async XLA Ops:
  7.2 43.5 %all-gather.2.cloned.1.call-start = ((), (), s32[]{:S(2)}) async-start(), calls=%async_computation.2 | async-start | bytes 1310720 | tf_op jit(solution)/shard_map/all_gather | solution.py:110
  10.3 71.4 %all-to-all-start = ((s32[4,1,2]{2,1,0:T(1,128)}), s32[4,1,2]{2,1,0:T(1,128)S(1)}, u32[]{:S(2)}, u32[]{:S(2)}) async-start(s32[4,1,2]{2,1,0:T(1,128)} %bitcast.49), calls=%async_computation | async-start | bytes 4096 | tf_op jit(solution)/shard_map/all_to_all | solution.py:105
  45.8 3.3 %copy-start.2 = (s32[1,1,1,8,1]{3,4,2,1,0:T(1,128)S(1)}, s32[1,1,1,8,1]{3,4,2,1,0:T(1,128)}, u32[]{:S(2)}) copy-start(s32[1,1,1,8,1]{3,4,2,1,0:T(1,128)} %param.10) | copy-start | bytes 100
  52.4 15.9 %copy-start = (bf16[530,1536]{0,1:T(8,128)(2,1)S(1)}, bf16[530,1536]{0,1:T(8,128)(2,1)}, u32[]{:S(2)}) copy-start(bf16[530,1536]{0,1:T(8,128)(2,1)} %pad_maximum_fusion) | copy-start | bytes 4884484
  54.6 5.9 %collective-permute-start = (bf16[9,512]{1,0:T(8,128)(2,1)S(1)}, bf16[9,512]{1,0:T(8,128)(2,1)S(1)}, u32[]{:S(2)}, u32[]{:S(2)}) collective-permute-start(bf16[9,512]{1,0:T(8,128)(2,1)S(1)} %get-tuple-element.33), channel_id=1, source_target_pairs={{0,2},{1,3},{4,6},{5,7},{8,10},{9,11},{12,14},{13,15},{16,18},{17,... | collective-permute-start | bytes 27656 | tf_op jit(solution)/shard_map/ppermute | solution.py:19
  58.0 5.6 %collective-permute-start.1 = (bf16[9,512]{1,0:T(8,128)(2,1)S(1)}, bf16[9,512]{1,0:T(8,128)(2,1)S(1)}, u32[]{:S(2)}, u32[]{:S(2)}) collective-permute-start(bf16[9,512]{1,0:T(8,128)(2,1)S(1)} %get-tuple-element.34), channel_id=1, source_target_pairs={{2,0},{3,1},{6,4},{7,5},{10,8},{11,9},{14,12},{15,13},{18,16},{19,... | collective-permute-start | bytes 27656 | tf_op jit(solution)/shard_map/ppermute | solution.py:20
  63.7 3.2 %collective-permute-start.2 = (bf16[274,9]{1,0:T(8,128)(2,1)S(1)}, bf16[274,9]{1,0:T(8,128)(2,1)S(1)}, u32[]{:S(2)}, u32[]{:S(2)}) collective-permute-start(bf16[274,9]{1,0:T(8,128)(2,1)S(1)} %get-tuple-element.31), channel_id=1, source_target_pairs={{0,1},{2,3},{4,5},{6,7},{8,9},{10,11},{12,13},{14,15},{16,17},{18,... | collective-permute-start | bytes 14804 | tf_op jit(solution)/shard_map/ppermute | solution.py:19
  65.0 3.3 %collective-permute-start.3 = (bf16[274,9]{1,0:T(8,128)(2,1)S(1)}, bf16[274,9]{1,0:T(8,128)(2,1)}, u32[]{:S(2)}, u32[]{:S(2)}) collective-permute-start(bf16[274,9]{1,0:T(8,128)(2,1)S(1)} %get-tuple-element.32), channel_id=1, source_target_pairs={{1,0},{3,2},{5,4},{7,6},{9,8},{11,10},{13,12},{15,14},{17,16},{19,... | collective-permute-start | bytes 14804 | tf_op jit(solution)/shard_map/ppermute | solution.py:20
  66.9 7.3 %copy-start.1 = (f32[1,256,512]{2,1,0:T(8,128)S(1)}, f32[1,256,512]{2,1,0:T(8,128)}, u32[]{:S(2)}) copy-start(f32[1,256,512]{2,1,0:T(8,128)} %param.8) | copy-start | bytes 1572868
  67.0 0.6 copy-start.3
  81.7 20.8 %all-to-all-start.1 = ((f32[4,2,16384]{2,1,0:T(2,128)}), f32[4,2,16384]{2,1,0:T(2,128)S(1)}, u32[]{:S(2)}, u32[]{:S(2)}) async-start(f32[4,2,16384]{2,1,0:T(2,128)} %reshape.379), calls=%async_computation.1 | async-start | bytes 1048576 | tf_op jit(solution)/shard_map/all_to_all | solution.py:174
Sparse Core Ops, SparseCore 0:
  9.5 30.6 all-gather.1

commit v2 on v1

--- a/solution.py
+++ b/solution.py
@@ -100,12 +100,6 @@
     same_owner = owner_list[None, :] == owner_list[:, None]
     place_rank = jnp.sum(jnp.where(earlier & same_owner, 1, 0), axis=1).astype(jnp.int32)
     slot_index = owner_list * capacity + place_rank
-    slot_match = jnp.arange(ccd_count * capacity)[:, None] == slot_index[None, :]
-    wanted = jnp.sum(jnp.where(slot_match, strip_list[None, :] + 1, 0), axis=1) - 1
-    asked = lax.all_to_all(
-        wanted.reshape(ccd_count, capacity), "ccd", split_axis=0, concat_axis=0, tiled=True
-    )
-    asked_flat = asked.reshape(ccd_count * capacity)
     global_index = owner_list * strips + strip_list
     rows_here = lax.all_gather(template, "ccd", axis=0, tiled=True).reshape(-1, strip_size)
     labels = jnp.arange(rows_here.shape[0])
@@ -127,7 +121,6 @@
     warped = static_shift(rows_done, col_weights, 1, half_cols).astype(jnp.bfloat16)
     image = warped.reshape(band_rows, half_cols)
     padded = padded_2(image, (("row", 0), ("amp", 1)), RADIUS)
-    kernels = kernel_table()
     row_place = (
         (lax.axis_index("row") * band_rows + jnp.arange(band_rows) + 0.5)
         / (band_rows * row_count)
@@ -141,11 +134,11 @@
         - 1.0
     )[None, :]
     coef_block = coefs[0]
+    kernels = kernel_table()
     row_mats = jnp.concatenate([band_operator(kernels[kind], band_rows) for kind in range(3)], axis=0)
     column_mats = jnp.concatenate(
         [band_operator(kernels[kind], half_cols).T for kind in range(3)], axis=1
     )
-    row_mats, column_mats = lax.optimization_barrier((row_mats, column_mats))
     across_all = jnp.dot(row_mats, padded, preferred_element_type=jnp.float32).astype(jnp.bfloat16)
     terms = jnp.dot(across_all, column_mats, preferred_element_type=jnp.float32)
     model = jnp.zeros((band_rows, half_cols), jnp.float32)
@@ -166,23 +159,30 @@
     contribution = jnp.einsum(
         "qik,qiz->qkz", row_warp, columns_back, preferred_element_type=jnp.float32
     )
+    tagged = jnp.concatenate(
+        [
+            contribution.reshape(strips, strip_size),
+            jnp.broadcast_to(strip_list.astype(jnp.float32)[:, None] + 1.0, (strips, 128)),
+        ],
+        axis=1,
+    )
     outgoing_back = (
-        jnp.zeros((ccd_count * capacity, strip_size), jnp.float32)
-        .at[slot_index]
-        .set(contribution.reshape(strips, strip_size))
+        jnp.zeros((ccd_count * capacity, strip_size + 128), jnp.float32).at[slot_index].set(tagged)
     )
     returned = lax.all_to_all(
-        outgoing_back.reshape(ccd_count, capacity, strip_size),
+        outgoing_back.reshape(ccd_count, capacity, strip_size + 128),
         "ccd",
         split_axis=0,
         concat_axis=0,
         tiled=True,
     )
+    returned = returned.reshape(ccd_count * capacity, strip_size + 128)
+    asked_flat = returned[:, strip_size].astype(jnp.int32) - 1
     owner_select = (asked_flat[:, None] == jnp.arange(strips)[None, :]).astype(jnp.float32)
     stack = jnp.einsum(
         "sp,sz->pz",
         owner_select,
-        returned.reshape(ccd_count * capacity, strip_size),
+        returned[:, :strip_size],
         precision=lax.Precision.HIGHEST,
     )
     return (difference[None], stack.reshape(template.shape))

time: 112 us -> 111 us (level)
  blocking collectives: 0 us -> 20.3 us
  waiting for transfers between devices: 18.8 us -> 4.04 us
  starting transfers between devices: 18.7 us -> 9.3 us
  other arithmetic: 30.1 us -> 36.2 us
  local copies, waits for them, and re-layouts: 20.7 us -> 17.2 us
    all_to_all x0 -> x1, blocking collectives: none -> 20.3 us  [body(): lax.all_to_all(outgoing_back.reshape(ccd_count, capacity, strip_size + 12...]
    all_to_all x2 -> x0, waiting for transfers between devices: 14.3 us -> none  [the longest x1 14.3 us: body(): lax.all_to_all(outgoing_back.reshape(ccd_count, capacity, strip_size), 'c...]
    all_to_all x2 -> x0, starting transfers between devices: 11.4 us -> none  [the longest x1 6.35 us: body(): lax.all_to_all(wanted.reshape(ccd_count, capacity), 'ccd', split_axis=0,...]
    mul x5, other arithmetic: 5.54 us -> 8.68 us  [body(): coef_block[2, basis] * row_place]
    ppermute x2, starting transfers between devices: 4.69 us -> 6.51 us  [padded_2(): before = lax.ppermute(last, axis, up)]
    add x5, other arithmetic: 11.4 us -> 13 us  [body(): coef_block[0, basis] + coef_block[1, basis] * col_place]
    concatenate x2 -> x0, other arithmetic: 1.53 us -> none  [the longest x1 1.46 us: body(): jnp.concatenate([band_operator(kernels[kind], half_cols).T for kind in ra...]
    select_n x1, other arithmetic: 0.01 us -> 1.25 us  [body(): jnp.zeros((ccd_count * capacity, strip_size + 128), jnp.float32)]
  transfers between devices with their start and end apart: 7 -> 5, of which waited for: 3 -> 2; matrix products, arithmetic and copies ran while one was open for 51% -> 39% of each run, Pallas kernels for 0% -> 0%
where the time goes in v2:
time: 111 us
  other arithmetic  36.2 us (33%)
  blocking collectives  20.3 us (18%)
  local copies, waits for them, and re-layouts  17.2 us (15%)
  between operations  15.2 us (14%)
  starting transfers between devices  9.3 us (8%)
  matrix products  8.53 us (8%)
  waiting for transfers between devices  4.04 us (4%)
    all_to_all x1, blocking collectives, body(): lax.all_to_all(outgoing_back.reshape(ccd_count, capacity, strip_size + 12...  20.3 us
    add x5, other arithmetic, body(): coef_block[0, basis] + coef_block[1, basis] * col_place  13 us
    mul x5, other arithmetic, body(): coef_block[2, basis] * row_place  8.68 us
    ppermute x2, starting transfers between devices, padded_2(): before = lax.ppermute(last, axis, up)  6.51 us
    dot_general x1, matrix products, body(): terms = jnp.dot(across_all, column_mats, preferred_element_type=jnp.float32)  6.09 us
    reshape x6, local copies, waits for them, and re-layouts, band_operator(): return flat.reshape(count, width)  4.73 us
    unnamed x118, local copies, waits for them, and re-layouts  4.14 us
    another operation x12, local copies, waits for them, and re-layouts, band_operator(): flat = jnp.tile(line, count)[:count * width]  4.14 us
  transfers between devices with their start and end apart: 5, of which 2 were waited for; matrix products, arithmetic and copies ran while one was open for 39% of the time, Pallas kernels for 0%

profile of v2, /device:TPU:0, one launch (start us, length us, event | category | flops | bytes accessed | tf_op | source)
XLA Modules:
  0.0 110.8 jit_solution(8991737210806222372)
XLA Ops:
  7.2 0.7 all-gather.2.cloned.1.call-update
  7.9 0.7 exponential_reduce_fusion.1
  8.6 0.6 abs_reduce_fusion
  9.2 0.7 copy.38
  9.9 0.7 fusion.176
  10.6 0.7 fusion.177
  11.3 0.8 slice_bitcast_fusion.8
  12.1 0.8 slice_bitcast_fusion.9
  12.8 0.1 broadcast_add_fusion
  12.9 1.3 %fusion.155 = f32[256]{0:T(256)} fusion(s32[]{:T(128)S(6)} %mul.604, f32[]{:T(128)} %bitcast.3), kind=kLoop, calls=%fused_computation.280 | loop fusion | flops 1536 | bytes 1032 | tf_op jit(solution)/shard_map/mul | solution.py:152
  14.1 1.8 %broadcast_multiply_fusion = (f32[256]{0:T(256)}, f32[256]{0:T(256)}) fusion(f32[]{:T(128)} %bitcast.47, s32[]{:T(128)S(6)} %mul.604, f32[]{:T(128)} %bitcast.44), kind=kLoop, calls=%fused_computation.252 | loop fusion | flops 1792 | bytes 2060 | tf_op jit(solution)/shard_map/mul | solution.py:152
  16.0 1.8 %broadcast_multiply_fusion.2 = (f32[256]{0:T(256)}, f32[256]{0:T(256)}) fusion(f32[]{:T(128)} %bitcast.41, s32[]{:T(128)S(6)} %mul.604, f32[]{:T(128)} %bitcast.38), kind=kLoop, calls=%fused_computation.254 | loop fusion | flops 1792 | bytes 2060 | tf_op jit(solution)/shard_map/mul | solution.py:152
  17.7 1.9 %broadcast_multiply_fusion.4 = (f32[256]{0:T(256)}, f32[256]{0:T(256)}) fusion(f32[]{:T(128)} %bitcast.35, s32[]{:T(128)S(6)} %mul.604, f32[]{:T(128)} %bitcast.32), kind=kLoop, calls=%fused_computation.256 | loop fusion | flops 1792 | bytes 2060 | tf_op jit(solution)/shard_map/mul | solution.py:152
  19.6 1.9 %broadcast_multiply_fusion.6 = (f32[256]{0:T(256)}, f32[256]{0:T(256)}) fusion(f32[]{:T(128)} %bitcast.29, s32[]{:T(128)S(6)} %mul.604, f32[]{:T(128)} %bitcast.26), kind=kLoop, calls=%fused_computation.258 | loop fusion | flops 1792 | bytes 2060 | tf_op jit(solution)/shard_map/mul | solution.py:152
  21.6 1.3 %multiply_add_fusion.12 = f32[512]{0:T(512)S(1)} fusion(s32[]{:T(128)S(6)} %mul.599, f32[]{:T(128)} %bitcast.2, f32[]{:T(128)} %bitcast.1), kind=kLoop, calls=%fused_computation.242 | loop fusion | flops 3584 | bytes 2060 | tf_op jit(solution)/shard_map/add | solution.py:150
  22.9 2.5 %multiply_add_fusion.4 = (f32[512]{0:T(512)S(1)}, f32[512]{0:T(512)S(1)}) fusion(f32[]{:T(128)} %bitcast.46, f32[]{:T(128)} %bitcast.45, s32[]{:T(128)S(6)} %mul.599, f32[]{:T(128)} %bitcast.43, f32[]{:T(128)} %bitcast.42), kind=kLoop, calls=%fused_computation.232 | loop fusion | flops 4608 | bytes 4116 | tf_op jit(solution)/shard_map/add | solution.py:150
  25.4 3.0 %multiply_add_fusion.6 = (f32[512]{0:T(512)}, f32[512]{0:T(512)}) fusion(f32[]{:T(128)} %bitcast.40, f32[]{:T(128)} %bitcast.39, s32[]{:T(128)S(6)} %mul.599, f32[]{:T(128)} %bitcast.37, f32[]{:T(128)} %bitcast.36), kind=kLoop, calls=%fused_computation.234 | loop fusion | flops 4608 | bytes 4116 | tf_op jit(solution)/shard_map/add | solution.py:150
  28.3 3.1 %multiply_add_fusion.8 = (f32[512]{0:T(512)}, f32[512]{0:T(512)}) fusion(f32[]{:T(128)} %bitcast.34, f32[]{:T(128)} %bitcast.33, s32[]{:T(128)S(6)} %mul.599, f32[]{:T(128)} %bitcast.31, f32[]{:T(128)} %bitcast.30), kind=kLoop, calls=%fused_computation.236 | loop fusion | flops 4608 | bytes 4116 | tf_op jit(solution)/shard_map/add | solution.py:150
  31.4 3.1 %multiply_add_fusion.10 = (f32[512]{0:T(512)}, f32[512]{0:T(512)}) fusion(f32[]{:T(128)} %bitcast.28, f32[]{:T(128)} %bitcast.27, s32[]{:T(128)S(6)} %mul.599, f32[]{:T(128)} %bitcast.25, f32[]{:T(128)} %bitcast.24), kind=kLoop, calls=%fused_computation.238 | loop fusion | flops 4608 | bytes 4116 | tf_op jit(solution)/shard_map/add | solution.py:150
  34.6 0.6 convert_bitcast_fusion.2
  35.2 0.1 fusion.150
  35.3 0.1 select_reduce_fusion
  35.4 0.4 slice_reduce_fusion.11
  35.9 0.9 select_reduce_fusion.1
  36.8 1.2 %fusion.154 = f32[8]{0:T(128)} fusion(s32[1,1,1,8]{3,2,1,0:T(1,128)} %param.11), kind=kLoop, calls=%fused_computation.251 | loop fusion | flops 16 | bytes 64 | tf_op jit(solution)/shard_map/add | solution.py:165
  37.9 0.7 bitcast_add_fusion.1
  38.6 1.2 %fusion.153 = s32[8]{0:T(128)} fusion(s32[8]{0:T(128)S(1)} %select_reduce_fusion.1, s32[1,1,1,8,1]{3,4,2,1,0:T(1,128)} %param.10), kind=kLoop, calls=%fused_computation.247 | loop fusion | flops 40 | bytes 96 | tf_op jit(solution)/shard_map/select_n | solution.py:170
  39.9 0.3 all-gather.2.cloned.1.call-done
  40.2 1.8 %copy.33 = bf16[4,8,32,512]{3,1,2,0:T(8,128)(2,1)S(1)} copy(bf16[4,8,32,512]{3,2,1,0:T(8,128)(2,1)} %bitcast.98) | data formatting | bytes 2097152
  42.0 0.3 convolution_convert_fusion
  42.4 0.4 convolution_convert_fusion.2
  42.9 1.2 %add_convert_fusion.1 = bf16[8,32,512]{2,1,0:T(8,128)(2,1)S(1)} fusion(bf16[8,32,512]{2,1,0:T(8,128)(2,1)S(1)} %convolution_convert_fusion.2, f32[8]{0:T(128)S(1)} %get-tuple-element.16, f32[8]{0:T(128)S(1)} %get-tuple-element.17, f32[8]{0:T(128)S(1)} %get-tuple-element.18, f32[8]{0:T(128)S(1)} %get-tuple-element.19, f32[8]{0:T(128)S(1)} %get-tuple-element.20, ...), kind=kLoop, calls=%fused_computation.41 | loop fusion | flops 4718592 | bytes 524672 | tf_op jit(solution)/shard_map/convert_element_type | solution.py:121
  44.2 4.6 %collective-permute-start = (bf16[9,512]{1,0:T(8,128)(2,1)S(1)}, bf16[9,512]{1,0:T(8,128)(2,1)S(1)}, u32[]{:S(2)}, u32[]{:S(2)}) collective-permute-start(bf16[9,512]{1,0:T(8,128)(2,1)S(1)} %get-tuple-element.31), channel_id=1, source_target_pairs={{0,2},{1,3},{4,6},{5,7},{8,10},{9,11},{12,14},{13,15},{16,18},{17,... | collective-permute-start | bytes 27656 | tf_op jit(solution)/shard_map/ppermute | solution.py:19
  48.8 1.3 %collective-permute-start.1 = (bf16[9,512]{1,0:T(8,128)(2,1)S(1)}, bf16[9,512]{1,0:T(8,128)(2,1)S(1)}, u32[]{:S(2)}, u32[]{:S(2)}) collective-permute-start(bf16[9,512]{1,0:T(8,128)(2,1)S(1)} %get-tuple-element.32), channel_id=1, source_target_pairs={{2,0},{3,1},{6,4},{7,5},{10,8},{11,9},{14,12},{15,13},{18,16},{19,... | collective-permute-start | bytes 27656 | tf_op jit(solution)/shard_map/ppermute | solution.py:20
  50.1 0.7 convert_bitcast_fusion.1
  50.7 0.6 exponential_reduce_fusion
  51.4 3.0 %collective-permute-done.1 = bf16[9,512]{1,0:T(8,128)(2,1)S(1)} collective-permute-done((bf16[9,512]{1,0:T(8,128)(2,1)S(1)}, bf16[9,512]{1,0:T(8,128)(2,1)S(1)}, u32[]{:S(2)}, u32[]{:S(2)}) %collective-permute-start.1) | collective-permute-done | bytes 9248 | tf_op jit(solution)/shard_map/ppermute | solution.py:20
  54.4 0.1 pad_maximum_fusion.2
  54.5 1.9 %collective-permute-start.2 = (bf16[274,9]{1,0:T(8,128)(2,1)S(1)}, bf16[274,9]{1,0:T(8,128)(2,1)}, u32[]{:S(2)}, u32[]{:S(2)}) collective-permute-start(bf16[274,9]{1,0:T(8,128)(2,1)S(1)} %get-tuple-element.29), channel_id=1, source_target_pairs={{0,1},{2,3},{4,5},{6,7},{8,9},{10,11},{12,13},{14,15},{16,17},{18,... | collective-permute-start | bytes 14804 | tf_op jit(solution)/shard_map/ppermute | solution.py:19
  56.4 1.5 %collective-permute-start.3 = (bf16[274,9]{1,0:T(8,128)(2,1)S(1)}, bf16[274,9]{1,0:T(8,128)(2,1)}, u32[]{:S(2)}, u32[]{:S(2)}) collective-permute-start(bf16[274,9]{1,0:T(8,128)(2,1)S(1)} %get-tuple-element.30), channel_id=1, source_target_pairs={{1,0},{3,2},{5,4},{7,6},{9,8},{11,10},{13,12},{15,14},{17,16},{19,... | collective-permute-start | bytes 14804 | tf_op jit(solution)/shard_map/ppermute | solution.py:20
  57.9 0.6 convert_bitcast_fusion
  58.6 0.9 tile.61
  59.6 1.1 %reshape.345 = bf16[512,530]{1,0:T(8,128)(2,1)S(1)} reshape(bf16[271360]{0:T(1024)(128)(2,1)S(1)} %slice.402) | data formatting | bytes 1085440 | tf_op jit(solution)/shard_map/reshape | solution.py:84
  60.8 0.9 tile.63
  61.7 1.1 %reshape.346 = bf16[512,530]{1,0:T(8,128)(2,1)S(1)} reshape(bf16[271360]{0:T(1024)(128)(2,1)S(1)} %slice.403) | data formatting | bytes 1085440 | tf_op jit(solution)/shard_map/reshape | solution.py:84
  63.0 0.9 tile.65
  63.9 1.1 %reshape.347 = bf16[512,530]{1,0:T(8,128)(2,1)S(1)} reshape(bf16[271360]{0:T(1024)(128)(2,1)S(1)} %slice.404) | data formatting | bytes 1085440 | tf_op jit(solution)/shard_map/reshape | solution.py:84
  65.1 0.4 tile.25
  65.5 0.4 reshape.337
  66.0 0.4 tile.27
  66.4 0.4 reshape.338
  66.9 0.4 tile.29
  67.3 0.4 reshape.339
  67.9 6.1 %fusion = f32[768,1536]{1,0:T(8,128)} fusion(bf16[530,512]{0,1:T(8,128)(2,1)S(1)} %bitcast.101, bf16[530,512]{0,1:T(8,128)(2,1)S(1)} %bitcast.100, bf16[530,512]{0,1:T(8,128)(2,1)S(1)} %bitcast.99, bf16[256,274]{1,0:T(8,128)(2,1)S(1)} %reshape.339, bf16[256,274]{1,0:T(8,128)(2,1)S(1)} %reshape.338, bf16[256,274]{1,0:T(8,128)(2,1)S(1)} %reshape.337, ...), kind=kOutput, calls=%fused_computation.2 | convolution fusion | flops 1481491072 | bytes 7058056 | tf_op jit(solution)/shard_map/dot_general | solution.py:143
  74.3 4.0 %fusion.173 = (bf16[256,512]{1,0:T(8,128)(2,1)S(1)}, f32[256,512]{1,0:T(8,128)}) fusion(f32[768,1536]{1,0:T(8,128)} %fusion, f32[256]{0:T(256)S(1)} %copy-done.9, f32[512]{0:T(512)S(1)} %get-tuple-element.80, f32[256]{0:T(256)S(1)} %copy-done.10, f32[512]{0:T(512)S(1)} %get-tuple-element.81, f32[256]{0:T(256)S(1)} %copy-done.11, f32[512]{0:T(512)S(1)} %copy-done.3, ...), kind=kLoop, calls=%fused_computation.297 | loop fusion | flops 3670016 | bytes 6056960 | tf_op jit(solution)/shard_map/convert_element_type | solution.py:156
  78.5 1.2 %convolution_bitcast_fusion = f32[1,8,32,512]{3,2,1,0:T(8,128)S(1)} fusion(bf16[8,32,512]{2,1,0:T(8,128)(2,1)S(1)} %bitcast.106, f32[8]{0:T(128)S(1)} %copy-done.21, f32[8]{0:T(128)S(1)} %copy-done.23, f32[8]{0:T(128)S(1)} %copy-done.25, f32[8]{0:T(128)S(1)} %copy-done.27, f32[8]{0:T(128)S(1)} %copy-done.29, f32[8]{0:T(128)S(1)} %copy-done.31, ...), kind=kOutput, calls=%fused_computation.9 | convolution fusion | flops 13213696 | bytes 791040 | tf_op jit(solution)/shard_map/qik,qiz->qkz/dot_general | solution.py:159
  79.7 0.3 copy.34
  80.1 1.1 %scatter_custom_fusion = f32[8,16512]{1,0:T(8,128)S(1)} fusion(s32[8]{0:T(128)} %fusion.153, f32[8,128]{1,0:T(8,128)S(1)} %broadcast_in_dim.118, f32[]{:T(128)} %constant.140, f32[8,16384]{1,0:T(8,128)S(1)} %bitcast.93, f32[]{:T(128)} %constant.22.clone.1), kind=kCustom, calls=%fused_computation.16 | custom fusion | flops 132096 | bytes 1057792 | tf_op jit(solution)/shard_map/scatter | solution.py:170
  81.2 0.3 reshape.350
  81.6 20.3 %all_to_all.5 = f32[4,2,16512]{2,1,0:T(2,128)S(1)} all-to-all(f32[4,2,16512]{2,1,0:T(2,128)S(1)} %reshape.350), channel_id=1, replica_groups=mesh['grp'=2,'ccd'=4,'row'=2,'amp'=2] {'ccd'}, dimensions={0} | all-to-all | bytes 1056768 | tf_op jit(solution)/shard_map/all_to_all | solution.py:172
  101.9 0.4 reshape.351
  102.3 0.1 fusion.138
  102.4 0.5 fusion.20
  102.9 1.1 copy.30
  (140 shorter events, 0.8 us)
Async XLA Ops:
  7.2 33.1 %all-gather.2.cloned.1.call-start = ((), (), s32[]{:S(2)}) async-start(), calls=%async_computation.1 | async-start | bytes 1310720 | tf_op jit(solution)/shard_map/all_gather | solution.py:104
  12.8 29.9 %copy-start.55 = (s32[8]{0:T(128)}, s32[8]{0:T(128)S(1)}, u32[]{:S(2)}) copy-start(s32[8]{0:T(128)S(1)} %get-tuple-element.67) | copy-start | bytes 100
  35.7 7.1 %copy-start.18 = (f32[8]{0:T(128)}, f32[8]{0:T(128)S(1)}, u32[]{:S(2)}) copy-start(f32[8]{0:T(128)S(1)} %get-tuple-element.15) | copy-start | bytes 100
  35.7 7.1 %copy-start.20 = (f32[8]{0:T(128)}, f32[8]{0:T(128)S(1)}, u32[]{:S(2)}) copy-start(f32[8]{0:T(128)S(1)} %get-tuple-element.16) | copy-start | bytes 100
  35.8 7.1 %copy-start.22 = (f32[8]{0:T(128)}, f32[8]{0:T(128)S(1)}, u32[]{:S(2)}) copy-start(f32[8]{0:T(128)S(1)} %get-tuple-element.17) | copy-start | bytes 100
  35.8 7.1 %copy-start.24 = (f32[8]{0:T(128)}, f32[8]{0:T(128)S(1)}, u32[]{:S(2)}) copy-start(f32[8]{0:T(128)S(1)} %get-tuple-element.18) | copy-start | bytes 100
  35.8 7.1 %copy-start.26 = (f32[8]{0:T(128)}, f32[8]{0:T(128)S(1)}, u32[]{:S(2)}) copy-start(f32[8]{0:T(128)S(1)} %get-tuple-element.19) | copy-start | bytes 100
  35.8 7.1 %copy-start.28 = (f32[8]{0:T(128)}, f32[8]{0:T(128)S(1)}, u32[]{:S(2)}) copy-start(f32[8]{0:T(128)S(1)} %get-tuple-element.20) | copy-start | bytes 100
  35.8 7.1 %copy-start.30 = (f32[8]{0:T(128)}, f32[8]{0:T(128)S(1)}, u32[]{:S(2)}) copy-start(f32[8]{0:T(128)S(1)} %get-tuple-element.21) | copy-start | bytes 100
  35.8 7.1 %copy-start.32 = (f32[8]{0:T(128)}, f32[8]{0:T(128)S(1)}, u32[]{:S(2)}) copy-start(f32[8]{0:T(128)S(1)} %get-tuple-element.22) | copy-start | bytes 100
  35.8 7.1 %copy-start.34 = (f32[8]{0:T(128)}, f32[8]{0:T(128)S(1)}, u32[]{:S(2)}) copy-start(f32[8]{0:T(128)S(1)} %get-tuple-element.23) | copy-start | bytes 100
  35.8 7.1 %copy-start.36 = (f32[8]{0:T(128)}, f32[8]{0:T(128)S(1)}, u32[]{:S(2)}) copy-start(f32[8]{0:T(128)S(1)} %get-tuple-element.24) | copy-start | bytes 100
  35.8 7.1 %copy-start.38 = (f32[8]{0:T(128)}, f32[8]{0:T(128)S(1)}, u32[]{:S(2)}) copy-start(f32[8]{0:T(128)S(1)} %get-tuple-element.25) | copy-start | bytes 100
  35.8 7.1 %copy-start.40 = (f32[8]{0:T(128)}, f32[8]{0:T(128)S(1)}, u32[]{:S(2)}) copy-start(f32[8]{0:T(128)S(1)} %get-tuple-element.26) | copy-start | bytes 100
  39.9 2.9 %copy-start.43 = (bf16[8]{0:T(256)(128)(2,1)}, bf16[8]{0:T(256)(128)(2,1)S(1)}, u32[]{:S(2)}) copy-start(bf16[8]{0:T(256)(128)(2,1)S(1)} %get-tuple-element.60) | copy-start | bytes 52
  39.9 2.9 %copy-start.45 = (bf16[8]{0:T(256)(128)(2,1)}, bf16[8]{0:T(256)(128)(2,1)S(1)}, u32[]{:S(2)}) copy-start(bf16[8]{0:T(256)(128)(2,1)S(1)} %get-tuple-element.61) | copy-start | bytes 52
  39.9 2.9 %copy-start.47 = (bf16[8]{0:T(256)(128)(2,1)}, bf16[8]{0:T(256)(128)(2,1)S(1)}, u32[]{:S(2)}) copy-start(bf16[8]{0:T(256)(128)(2,1)S(1)} %get-tuple-element.62) | copy-start | bytes 52
  39.9 2.9 %copy-start.49 = (bf16[8]{0:T(256)(128)(2,1)}, bf16[8]{0:T(256)(128)(2,1)S(1)}, u32[]{:S(2)}) copy-start(bf16[8]{0:T(256)(128)(2,1)S(1)} %get-tuple-element.63) | copy-start | bytes 52
  39.9 2.9 %copy-start.51 = (bf16[8]{0:T(256)(128)(2,1)}, bf16[8]{0:T(256)(128)(2,1)S(1)}, u32[]{:S(2)}) copy-start(bf16[8]{0:T(256)(128)(2,1)S(1)} %get-tuple-element.64) | copy-start | bytes 52
  39.9 2.9 %copy-start.53 = (bf16[8]{0:T(256)(128)(2,1)}, bf16[8]{0:T(256)(128)(2,1)S(1)}, u32[]{:S(2)}) copy-start(bf16[8]{0:T(256)(128)(2,1)S(1)} %get-tuple-element.65) | copy-start | bytes 52
  44.2 7.2 %collective-permute-start = (bf16[9,512]{1,0:T(8,128)(2,1)S(1)}, bf16[9,512]{1,0:T(8,128)(2,1)S(1)}, u32[]{:S(2)}, u32[]{:S(2)}) collective-permute-start(bf16[9,512]{1,0:T(8,128)(2,1)S(1)} %get-tuple-element.31), channel_id=1, source_target_pairs={{0,2},{1,3},{4,6},{5,7},{8,10},{9,11},{12,14},{13,15},{16,18},{17,... | collective-permute-start | bytes 27656 | tf_op jit(solution)/shard_map/ppermute | solution.py:19
  48.8 5.6 %collective-permute-start.1 = (bf16[9,512]{1,0:T(8,128)(2,1)S(1)}, bf16[9,512]{1,0:T(8,128)(2,1)S(1)}, u32[]{:S(2)}, u32[]{:S(2)}) collective-permute-start(bf16[9,512]{1,0:T(8,128)(2,1)S(1)} %get-tuple-element.32), channel_id=1, source_target_pairs={{2,0},{3,1},{6,4},{7,5},{10,8},{11,9},{14,12},{15,13},{18,16},{19,... | collective-permute-start | bytes 27656 | tf_op jit(solution)/shard_map/ppermute | solution.py:20
  54.4 5.1 %copy-start.1 = (bf16[9,512]{1,0:T(8,128)(2,1)}, bf16[9,512]{1,0:T(8,128)(2,1)S(1)}, u32[]{:S(2)}) copy-start(bf16[9,512]{1,0:T(8,128)(2,1)S(1)} %collective-permute-done.1) | copy-start | bytes 27652
  54.5 13.2 %collective-permute-start.2 = (bf16[274,9]{1,0:T(8,128)(2,1)S(1)}, bf16[274,9]{1,0:T(8,128)(2,1)}, u32[]{:S(2)}, u32[]{:S(2)}) collective-permute-start(bf16[274,9]{1,0:T(8,128)(2,1)S(1)} %get-tuple-element.29), channel_id=1, source_target_pairs={{0,1},{2,3},{4,5},{6,7},{8,9},{10,11},{12,13},{14,15},{16,17},{18,... | collective-permute-start | bytes 14804 | tf_op jit(solution)/shard_map/ppermute | solution.py:19
  56.4 11.3 %collective-permute-start.3 = (bf16[274,9]{1,0:T(8,128)(2,1)S(1)}, bf16[274,9]{1,0:T(8,128)(2,1)}, u32[]{:S(2)}, u32[]{:S(2)}) collective-permute-start(bf16[274,9]{1,0:T(8,128)(2,1)S(1)} %get-tuple-element.30), channel_id=1, source_target_pairs={{1,0},{3,2},{5,4},{7,6},{9,8},{11,10},{13,12},{15,14},{17,16},{19,... | collective-permute-start | bytes 14804 | tf_op jit(solution)/shard_map/ppermute | solution.py:20
  65.1 2.7 %copy-start.2 = (bf16[9,512]{1,0:T(8,128)(2,1)S(1)}, bf16[9,512]{1,0:T(8,128)(2,1)}, u32[]{:S(2)}) copy-start(bf16[9,512]{1,0:T(8,128)(2,1)} %copy-done.1) | copy-start | bytes 27652
  67.7 6.3 %copy-start = (f32[1,256,512]{2,1,0:T(8,128)S(1)}, f32[1,256,512]{2,1,0:T(8,128)}, u32[]{:S(2)}) copy-start(f32[1,256,512]{2,1,0:T(8,128)} %param.8) | copy-start | bytes 1572868
  67.7 6.2 %copy-start.3 = (f32[512]{0:T(512)S(1)}, f32[512]{0:T(512)}, u32[]{:S(2)}) copy-start(f32[512]{0:T(512)} %get-tuple-element.82) | copy-start | bytes 6148
  67.8 6.2 %copy-start.4 = (f32[512]{0:T(512)S(1)}, f32[512]{0:T(512)}, u32[]{:S(2)}) copy-start(f32[512]{0:T(512)} %get-tuple-element.83) | copy-start | bytes 6148
  67.8 6.2 %copy-start.5 = (f32[512]{0:T(512)S(1)}, f32[512]{0:T(512)}, u32[]{:S(2)}) copy-start(f32[512]{0:T(512)} %get-tuple-element.84) | copy-start | bytes 6148
  67.8 6.2 %copy-start.6 = (f32[512]{0:T(512)S(1)}, f32[512]{0:T(512)}, u32[]{:S(2)}) copy-start(f32[512]{0:T(512)} %get-tuple-element.85) | copy-start | bytes 6148
  67.8 6.2 %copy-start.7 = (f32[512]{0:T(512)S(1)}, f32[512]{0:T(512)}, u32[]{:S(2)}) copy-start(f32[512]{0:T(512)} %get-tuple-element.86) | copy-start | bytes 6148
  67.8 6.2 %copy-start.8 = (f32[512]{0:T(512)S(1)}, f32[512]{0:T(512)}, u32[]{:S(2)}) copy-start(f32[512]{0:T(512)} %get-tuple-element.87) | copy-start | bytes 6148
  67.8 6.2 %copy-start.9 = (f32[256]{0:T(256)S(1)}, f32[256]{0:T(256)}, u32[]{:S(2)}) copy-start(f32[256]{0:T(256)} %get-tuple-element.72) | copy-start | bytes 3076
  67.8 6.2 %copy-start.10 = (f32[256]{0:T(256)S(1)}, f32[256]{0:T(256)}, u32[]{:S(2)}) copy-start(f32[256]{0:T(256)} %get-tuple-element.73) | copy-start | bytes 3076
  67.8 6.2 %copy-start.11 = (f32[256]{0:T(256)S(1)}, f32[256]{0:T(256)}, u32[]{:S(2)}) copy-start(f32[256]{0:T(256)} %get-tuple-element.74) | copy-start | bytes 3076
  67.8 6.2 %copy-start.12 = (f32[256]{0:T(256)S(1)}, f32[256]{0:T(256)}, u32[]{:S(2)}) copy-start(f32[256]{0:T(256)} %get-tuple-element.75) | copy-start | bytes 3076
  67.8 6.2 %copy-start.13 = (f32[256]{0:T(256)S(1)}, f32[256]{0:T(256)}, u32[]{:S(2)}) copy-start(f32[256]{0:T(256)} %get-tuple-element.76) | copy-start | bytes 3076
  67.9 6.2 %copy-start.14 = (f32[256]{0:T(256)S(1)}, f32[256]{0:T(256)}, u32[]{:S(2)}) copy-start(f32[256]{0:T(256)} %get-tuple-element.77) | copy-start | bytes 3076
  67.9 6.2 %copy-start.15 = (f32[256]{0:T(256)S(1)}, f32[256]{0:T(256)}, u32[]{:S(2)}) copy-start(f32[256]{0:T(256)} %get-tuple-element.78) | copy-start | bytes 3076
  67.9 6.2 %copy-start.16 = (f32[256]{0:T(256)S(1)}, f32[256]{0:T(256)}, u32[]{:S(2)}) copy-start(f32[256]{0:T(256)} %get-tuple-element.79) | copy-start | bytes 3076
  67.9 6.2 %copy-start.17 = (f32[256]{0:T(256)S(1)}, f32[256]{0:T(256)}, u32[]{:S(2)}) copy-start(f32[256]{0:T(256)} %fusion.155) | copy-start | bytes 3076
  74.1 4.1 %copy-start.19 = (f32[8]{0:T(128)S(1)}, f32[8]{0:T(128)}, u32[]{:S(2)}) copy-start(f32[8]{0:T(128)} %copy-done.18) | copy-start | bytes 100
  74.1 4.1 %copy-start.21 = (f32[8]{0:T(128)S(1)}, f32[8]{0:T(128)}, u32[]{:S(2)}) copy-start(f32[8]{0:T(128)} %copy-done.20) | copy-start | bytes 100
  74.1 4.1 %copy-start.23 = (f32[8]{0:T(128)S(1)}, f32[8]{0:T(128)}, u32[]{:S(2)}) copy-start(f32[8]{0:T(128)} %copy-done.22) | copy-start | bytes 100
  74.2 4.1 %copy-start.25 = (f32[8]{0:T(128)S(1)}, f32[8]{0:T(128)}, u32[]{:S(2)}) copy-start(f32[8]{0:T(128)} %copy-done.24) | copy-start | bytes 100
  74.2 4.1 %copy-start.27 = (f32[8]{0:T(128)S(1)}, f32[8]{0:T(128)}, u32[]{:S(2)}) copy-start(f32[8]{0:T(128)} %copy-done.26) | copy-start | bytes 100
  74.2 4.1 %copy-start.29 = (f32[8]{0:T(128)S(1)}, f32[8]{0:T(128)}, u32[]{:S(2)}) copy-start(f32[8]{0:T(128)} %copy-done.28) | copy-start | bytes 100
  74.2 4.1 %copy-start.31 = (f32[8]{0:T(128)S(1)}, f32[8]{0:T(128)}, u32[]{:S(2)}) copy-start(f32[8]{0:T(128)} %copy-done.30) | copy-start | bytes 100
  74.2 4.1 %copy-start.33 = (f32[8]{0:T(128)S(1)}, f32[8]{0:T(128)}, u32[]{:S(2)}) copy-start(f32[8]{0:T(128)} %copy-done.32) | copy-start | bytes 100
  74.2 4.1 %copy-start.35 = (f32[8]{0:T(128)S(1)}, f32[8]{0:T(128)}, u32[]{:S(2)}) copy-start(f32[8]{0:T(128)} %copy-done.34) | copy-start | bytes 100
  74.2 4.1 %copy-start.37 = (f32[8]{0:T(128)S(1)}, f32[8]{0:T(128)}, u32[]{:S(2)}) copy-start(f32[8]{0:T(128)} %copy-done.36) | copy-start | bytes 100
  74.2 4.1 %copy-start.39 = (f32[8]{0:T(128)S(1)}, f32[8]{0:T(128)}, u32[]{:S(2)}) copy-start(f32[8]{0:T(128)} %copy-done.38) | copy-start | bytes 100
  74.2 4.1 %copy-start.41 = (f32[8]{0:T(128)S(1)}, f32[8]{0:T(128)}, u32[]{:S(2)}) copy-start(f32[8]{0:T(128)} %copy-done.40) | copy-start | bytes 100
  74.2 4.1 %copy-start.44 = (bf16[8]{0:T(256)(128)(2,1)S(1)}, bf16[8]{0:T(256)(128)(2,1)}, u32[]{:S(2)}) copy-start(bf16[8]{0:T(256)(128)(2,1)} %copy-done.43) | copy-start | bytes 52
  74.3 4.1 %copy-start.46 = (bf16[8]{0:T(256)(128)(2,1)S(1)}, bf16[8]{0:T(256)(128)(2,1)}, u32[]{:S(2)}) copy-start(bf16[8]{0:T(256)(128)(2,1)} %copy-done.45) | copy-start | bytes 52
  74.3 4.1 %copy-start.48 = (bf16[8]{0:T(256)(128)(2,1)S(1)}, bf16[8]{0:T(256)(128)(2,1)}, u32[]{:S(2)}) copy-start(bf16[8]{0:T(256)(128)(2,1)} %copy-done.47) | copy-start | bytes 52
  74.3 4.1 %copy-start.50 = (bf16[8]{0:T(256)(128)(2,1)S(1)}, bf16[8]{0:T(256)(128)(2,1)}, u32[]{:S(2)}) copy-start(bf16[8]{0:T(256)(128)(2,1)} %copy-done.49) | copy-start | bytes 52
  74.3 4.1 %copy-start.52 = (bf16[8]{0:T(256)(128)(2,1)S(1)}, bf16[8]{0:T(256)(128)(2,1)}, u32[]{:S(2)}) copy-start(bf16[8]{0:T(256)(128)(2,1)} %copy-done.51) | copy-start | bytes 52
  74.3 4.1 %copy-start.54 = (bf16[8]{0:T(256)(128)(2,1)S(1)}, bf16[8]{0:T(256)(128)(2,1)}, u32[]{:S(2)}) copy-start(bf16[8]{0:T(256)(128)(2,1)} %copy-done.53) | copy-start | bytes 52
  74.3 4.1 %copy-start.56 = (s32[8]{0:T(128)S(1)}, s32[8]{0:T(128)}, u32[]{:S(2)}) copy-start(s32[8]{0:T(128)} %copy-done.55) | copy-start | bytes 100
  78.4 1.6 %copy-start.42 = (f32[8]{0:T(128)S(1)}, f32[8]{0:T(128)}, u32[]{:S(2)}) copy-start(f32[8]{0:T(128)} %fusion.154) | copy-start | bytes 100
Sparse Core Ops, SparseCore 0:
  9.5 30.6 all-gather.1

commit v3 on v2

--- a/solution.py
+++ b/solution.py
@@ -141,16 +141,14 @@
     )
     across_all = jnp.dot(row_mats, padded, preferred_element_type=jnp.float32).astype(jnp.bfloat16)
     terms = jnp.dot(across_all, column_mats, preferred_element_type=jnp.float32)
+    col_weight = coef_block[0][:, None] + coef_block[1][:, None] * col_place
+    row_weight = coef_block[2][:, None] * row_place[:, 0][None, :]
     model = jnp.zeros((band_rows, half_cols), jnp.float32)
     for first in range(3):
         for second in range(3):
             basis = first * 3 + second
             term = terms[first * band_rows:(first + 1) * band_rows, second * half_cols:(second + 1) * half_cols]
-            weight = (
-                coef_block[0, basis]
-                + coef_block[1, basis] * col_place
-                + coef_block[2, basis] * row_place
-            )
+            weight = col_weight[basis][None, :] + row_weight[basis][:, None]
             model = model + weight * term
     difference = science[0] - model
     lowered = difference.astype(jnp.bfloat16).reshape(strips, strip_rows, half_cols)

time: 111 us -> 108 us (0.973)
  waiting for transfers between devices: 4.04 us -> 25.6 us
  other arithmetic: 36.2 us -> 14.9 us
  blocking collectives: 20.3 us -> 18.6 us
  starting transfers between devices: 9.3 us -> 8.09 us
    all_gather x1, waiting for transfers between devices: 0.3 us -> 22 us  [body(): lax.all_gather(template, 'ccd', axis=0, tiled=True).reshape(-1, strip_size)]
    add x5 -> x1, other arithmetic: 13 us -> 0.07 us  [body(): col_weight = coef_block[0][:, None] + coef_block[1][:, None] * col_place]
    mul x5 -> x1, other arithmetic: 8.68 us -> 0.07 us  [body(): row_weight = coef_block[2][:, None] * row_place[:, 0][None, :]]
    all_to_all x1, blocking collectives: 20.3 us -> 18.6 us  [body(): lax.all_to_all(outgoing_back.reshape(ccd_count, capacity, strip_size + 12...]
    ppermute x2, starting transfers between devices: 6.51 us -> 5.3 us  [padded_2(): before = lax.ppermute(last, axis, up)]
    unnamed x118 -> x117, local copies, waits for them, and re-layouts: 4.14 us -> 3.47 us
  transfers between devices with their start and end apart: 5 -> 5, of which waited for: 2 -> 2; matrix products, arithmetic and copies ran while one was open for 39% -> 20% of each run, Pallas kernels for 0% -> 0%
where the time goes in v3:
time: 108 us
  waiting for transfers between devices  25.6 us (24%)
  blocking collectives  18.6 us (17%)
  local copies, waits for them, and re-layouts  17.1 us (16%)
  between operations  15.2 us (14%)
  other arithmetic  14.9 us (14%)
  matrix products  8.5 us (8%)
  starting transfers between devices  8.09 us (7%)
    all_gather x1, waiting for transfers between devices, body(): lax.all_gather(template, 'ccd', axis=0, tiled=True).reshape(-1, strip_size)  22 us
    all_to_all x1, blocking collectives, body(): lax.all_to_all(outgoing_back.reshape(ccd_count, capacity, strip_size + 12...  18.6 us
    dot_general x1, matrix products, body(): terms = jnp.dot(across_all, column_mats, preferred_element_type=jnp.float32)  6.07 us
    ppermute x2, starting transfers between devices, padded_2(): before = lax.ppermute(last, axis, up)  5.3 us
    reshape x6, local copies, waits for them, and re-layouts, band_operator(): return flat.reshape(count, width)  4.73 us
    another operation x12, local copies, waits for them, and re-layouts, band_operator(): flat = jnp.tile(line, count)[:count * width]  4.14 us
    convert_element_type x1, other arithmetic, body(): difference.astype(jnp.bfloat16).reshape(strips, strip_rows, half_cols)  3.96 us
    unnamed x117, local copies, waits for them, and re-layouts  3.47 us
  transfers between devices with their start and end apart: 5, of which 2 were waited for; matrix products, arithmetic and copies ran while one was open for 20% of the time, Pallas kernels for 0%

profile of v3, /device:TPU:0, one launch (start us, length us, event | category | flops | bytes accessed | tf_op | source)
XLA Modules:
  0.0 108.0 jit_solution(6441716003986079784)
XLA Ops:
  7.2 0.0 all-gather.2.cloned.1.call-start
  7.2 0.7 all-gather.2.cloned.1.call-update
  7.9 0.6 exponential_reduce_fusion.1
  8.6 0.8 slice_bitcast_fusion.8
  9.3 0.8 slice_bitcast_fusion.9
  10.1 1.2 %fusion.154 = f32[8]{0:T(128)} fusion(s32[1,1,1,8]{3,2,1,0:T(1,128)} %param.11), kind=kLoop, calls=%fused_computation.243 | loop fusion | flops 16 | bytes 64 | tf_op jit(solution)/shard_map/add | solution.py:163
  11.3 0.7 bitcast_add_fusion.1
  12.0 0.1 broadcast_add_fusion
  12.1 0.1 fusion.150
  12.2 0.1 select_reduce_fusion
  12.2 0.4 slice_reduce_fusion.11
  12.8 0.9 select_reduce_fusion.1
  13.7 0.7 convert_bitcast_fusion.2
  14.3 0.6 abs_reduce_fusion
  14.9 1.2 %fusion.153 = s32[8]{0:T(128)} fusion(s32[8]{0:T(128)S(1)} %select_reduce_fusion.1, s32[1,1,1,8,1]{3,4,2,1,0:T(1,128)} %param.10), kind=kLoop, calls=%fused_computation.239 | loop fusion | flops 40 | bytes 96 | tf_op jit(solution)/shard_map/select_n | solution.py:168
  16.1 0.7 slice_bitcast_fusion.12
  16.9 0.1 broadcast_multiply_fusion
  17.0 0.6 fusion.176
  17.6 0.1 multiply_add_fusion
  17.7 0.6 fusion.175
  18.3 22.0 %all-gather.2.cloned.1.call-done = bf16[4,1,1,8,32,512]{5,4,3,2,1,0:T(8,128)(2,1)} async-done(((bf16[1,1,1,8,32,512]{5,4,3,2,1,0:T(8,128)(2,1)}), bf16[4,1,1,8,32,512]{5,4,3,2,1,0:T(8,128)(2,1)}) %all-gather.2.cloned.1.call-update) | async-done | bytes 1048592 | tf_op jit(solution)/shard_map/all_gather | solution.py:104
  40.3 1.8 %copy.32 = bf16[4,8,32,512]{3,1,2,0:T(8,128)(2,1)S(1)} copy(bf16[4,8,32,512]{3,2,1,0:T(8,128)(2,1)} %bitcast.92) | data formatting | bytes 2097152
  42.1 0.3 convolution_convert_fusion
  42.4 0.4 convolution_convert_fusion.2
  43.0 1.2 %add_convert_fusion.1 = bf16[8,32,512]{2,1,0:T(8,128)(2,1)S(1)} fusion(bf16[8,32,512]{2,1,0:T(8,128)(2,1)S(1)} %convolution_convert_fusion.2, f32[8]{0:T(128)S(1)} %get-tuple-element.16, f32[8]{0:T(128)S(1)} %get-tuple-element.17, f32[8]{0:T(128)S(1)} %get-tuple-element.18, f32[8]{0:T(128)S(1)} %get-tuple-element.19, f32[8]{0:T(128)S(1)} %get-tuple-element.20, ...), kind=kLoop, calls=%fused_computation.41 | loop fusion | flops 4718592 | bytes 524672 | tf_op jit(solution)/shard_map/convert_element_type | solution.py:121
  44.2 3.4 %collective-permute-start = (bf16[9,512]{1,0:T(8,128)(2,1)S(1)}, bf16[9,512]{1,0:T(8,128)(2,1)S(1)}, u32[]{:S(2)}, u32[]{:S(2)}) collective-permute-start(bf16[9,512]{1,0:T(8,128)(2,1)S(1)} %get-tuple-element.31), channel_id=1, source_target_pairs={{0,2},{1,3},{4,6},{5,7},{8,10},{9,11},{12,14},{13,15},{16,18},{17,... | collective-permute-start | bytes 27656 | tf_op jit(solution)/shard_map/ppermute | solution.py:19
  47.6 1.3 %collective-permute-start.1 = (bf16[9,512]{1,0:T(8,128)(2,1)S(1)}, bf16[9,512]{1,0:T(8,128)(2,1)S(1)}, u32[]{:S(2)}, u32[]{:S(2)}) collective-permute-start(bf16[9,512]{1,0:T(8,128)(2,1)S(1)} %get-tuple-element.32), channel_id=1, source_target_pairs={{2,0},{3,1},{6,4},{7,5},{10,8},{11,9},{14,12},{15,13},{18,16},{19,... | collective-permute-start | bytes 27656 | tf_op jit(solution)/shard_map/ppermute | solution.py:20
  48.9 0.7 convert_bitcast_fusion.1
  49.6 0.7 exponential_reduce_fusion
  50.3 3.0 %collective-permute-done.1 = bf16[9,512]{1,0:T(8,128)(2,1)S(1)} collective-permute-done((bf16[9,512]{1,0:T(8,128)(2,1)S(1)}, bf16[9,512]{1,0:T(8,128)(2,1)S(1)}, u32[]{:S(2)}, u32[]{:S(2)}) %collective-permute-start.1) | collective-permute-done | bytes 9248 | tf_op jit(solution)/shard_map/ppermute | solution.py:20
  53.2 0.1 pad_maximum_fusion.2
  53.3 1.9 %collective-permute-start.2 = (bf16[274,9]{1,0:T(8,128)(2,1)S(1)}, bf16[274,9]{1,0:T(8,128)(2,1)}, u32[]{:S(2)}, u32[]{:S(2)}) collective-permute-start(bf16[274,9]{1,0:T(8,128)(2,1)S(1)} %get-tuple-element.29), channel_id=1, source_target_pairs={{0,1},{2,3},{4,5},{6,7},{8,9},{10,11},{12,13},{14,15},{16,17},{18,... | collective-permute-start | bytes 14804 | tf_op jit(solution)/shard_map/ppermute | solution.py:19
  55.3 1.5 %collective-permute-start.3 = (bf16[274,9]{1,0:T(8,128)(2,1)S(1)}, bf16[274,9]{1,0:T(8,128)(2,1)}, u32[]{:S(2)}, u32[]{:S(2)}) collective-permute-start(bf16[274,9]{1,0:T(8,128)(2,1)S(1)} %get-tuple-element.30), channel_id=1, source_target_pairs={{1,0},{3,2},{5,4},{7,6},{9,8},{11,10},{13,12},{15,14},{17,16},{19,... | collective-permute-start | bytes 14804 | tf_op jit(solution)/shard_map/ppermute | solution.py:20
  56.7 0.7 convert_bitcast_fusion
  57.5 0.1 tile.60
  57.6 0.9 tile.61
  58.5 1.1 %reshape.277 = bf16[512,530]{1,0:T(8,128)(2,1)S(1)} reshape(bf16[271360]{0:T(1024)(128)(2,1)S(1)} %slice.383) | data formatting | bytes 1085440 | tf_op jit(solution)/shard_map/reshape | solution.py:84
  59.7 0.1 tile.62
  59.8 0.9 tile.63
  60.7 1.1 %reshape.278 = bf16[512,530]{1,0:T(8,128)(2,1)S(1)} reshape(bf16[271360]{0:T(1024)(128)(2,1)S(1)} %slice.384) | data formatting | bytes 1085440 | tf_op jit(solution)/shard_map/reshape | solution.py:84
  61.9 0.1 tile.64
  61.9 0.9 tile.65
  62.9 1.1 %reshape.279 = bf16[512,530]{1,0:T(8,128)(2,1)S(1)} reshape(bf16[271360]{0:T(1024)(128)(2,1)S(1)} %slice.385) | data formatting | bytes 1085440 | tf_op jit(solution)/shard_map/reshape | solution.py:84
  64.0 0.0 copy-start.2
  64.1 0.4 tile.25
  64.5 0.4 reshape.269
  64.9 0.4 tile.27
  65.4 0.4 reshape.270
  65.8 0.4 tile.29
  66.2 0.4 reshape.271
  66.7 0.0 copy-start
  66.7 0.0 copy-start.3
  66.9 6.1 %fusion = f32[768,1536]{1,0:T(8,128)} fusion(bf16[530,512]{0,1:T(8,128)(2,1)S(1)} %bitcast.95, bf16[530,512]{0,1:T(8,128)(2,1)S(1)} %bitcast.94, bf16[530,512]{0,1:T(8,128)(2,1)S(1)} %bitcast.93, bf16[256,274]{1,0:T(8,128)(2,1)S(1)} %reshape.271, bf16[256,274]{1,0:T(8,128)(2,1)S(1)} %reshape.270, bf16[256,274]{1,0:T(8,128)(2,1)S(1)} %reshape.269, ...), kind=kOutput, calls=%fused_computation.2 | convolution fusion | flops 1481491072 | bytes 7058056 | tf_op jit(solution)/shard_map/dot_general | solution.py:143
  73.3 4.0 %fusion.172 = (bf16[256,512]{1,0:T(8,128)(2,1)S(1)}, f32[256,512]{1,0:T(8,128)}) fusion(f32[768,1536]{1,0:T(8,128)} %fusion, f32[256]{0:T(256)S(1)} %bitcast.112, f32[512]{0:T(512)S(1)} %bitcast.103, f32[256]{0:T(256)S(1)} %bitcast.113, f32[512]{0:T(512)S(1)} %bitcast.104, f32[256]{0:T(256)S(1)} %bitcast.114, f32[512]{0:T(512)S(1)} %bitcast.105, ...), kind=kLoop, calls=%fused_computation.283 | loop fusion | flops 3670016 | bytes 6056960 | tf_op jit(solution)/shard_map/convert_element_type | solution.py:154
  77.4 1.2 %convolution_bitcast_fusion = f32[1,8,32,512]{3,2,1,0:T(8,128)S(1)} fusion(bf16[8,32,512]{2,1,0:T(8,128)(2,1)S(1)} %bitcast.100, f32[8]{0:T(128)S(1)} %copy-done.21, f32[8]{0:T(128)S(1)} %copy-done.23, f32[8]{0:T(128)S(1)} %copy-done.25, f32[8]{0:T(128)S(1)} %copy-done.27, f32[8]{0:T(128)S(1)} %copy-done.29, f32[8]{0:T(128)S(1)} %copy-done.31, ...), kind=kOutput, calls=%fused_computation.9 | convolution fusion | flops 13213696 | bytes 791040 | tf_op jit(solution)/shard_map/qik,qiz->qkz/dot_general | solution.py:157
  78.6 0.3 copy.33
  79.0 0.1 broadcast_in_dim.117
  79.0 1.1 %scatter_custom_fusion = f32[8,16512]{1,0:T(8,128)S(1)} fusion(s32[8]{0:T(128)} %fusion.153, f32[8,128]{1,0:T(8,128)S(1)} %broadcast_in_dim.117, f32[]{:T(128)} %constant.140, f32[8,16384]{1,0:T(8,128)S(1)} %bitcast.87, f32[]{:T(128)} %constant.22.clone.1), kind=kCustom, calls=%fused_computation.16 | custom fusion | flops 132096 | bytes 1057792 | tf_op jit(solution)/shard_map/scatter | solution.py:168
  80.2 0.3 reshape.282
  80.5 18.6 %all_to_all.5 = f32[4,2,16512]{2,1,0:T(2,128)S(1)} all-to-all(f32[4,2,16512]{2,1,0:T(2,128)S(1)} %reshape.282), channel_id=1, replica_groups=mesh['grp'=2,'ccd'=4,'row'=2,'amp'=2] {'ccd'}, dimensions={0} | all-to-all | bytes 1056768 | tf_op jit(solution)/shard_map/all_to_all | solution.py:170
  99.1 0.4 reshape.283
  99.4 0.1 fusion.138
  99.5 0.5 fusion.20
  100.0 1.1 %copy.30 = f32[1,1,1,8,32,512]{5,4,3,2,1,0:T(8,128)} copy(f32[1,1,1,8,32,512]{5,3,4,2,1,0:T(8,128)S(1)} %bitcast.88) | data formatting | bytes 1048576
  (134 shorter events, 0.5 us)
Async XLA Ops:
  7.2 33.1 %all-gather.2.cloned.1.call-start = ((), (), s32[]{:S(2)}) async-start(), calls=%async_computation.1 | async-start | bytes 1310720 | tf_op jit(solution)/shard_map/all_gather | solution.py:104
  10.1 32.7 %copy-start.55 = (s32[8]{0:T(128)}, s32[8]{0:T(128)S(1)}, u32[]{:S(2)}) copy-start(s32[8]{0:T(128)S(1)} %get-tuple-element.61) | copy-start | bytes 100
  12.6 30.3 %copy-start.18 = (f32[8]{0:T(128)}, f32[8]{0:T(128)S(1)}, u32[]{:S(2)}) copy-start(f32[8]{0:T(128)S(1)} %get-tuple-element.15) | copy-start | bytes 100
  12.6 30.3 %copy-start.20 = (f32[8]{0:T(128)}, f32[8]{0:T(128)S(1)}, u32[]{:S(2)}) copy-start(f32[8]{0:T(128)S(1)} %get-tuple-element.16) | copy-start | bytes 100
  12.6 30.3 %copy-start.22 = (f32[8]{0:T(128)}, f32[8]{0:T(128)S(1)}, u32[]{:S(2)}) copy-start(f32[8]{0:T(128)S(1)} %get-tuple-element.17) | copy-start | bytes 100
  12.6 30.3 %copy-start.24 = (f32[8]{0:T(128)}, f32[8]{0:T(128)S(1)}, u32[]{:S(2)}) copy-start(f32[8]{0:T(128)S(1)} %get-tuple-element.18) | copy-start | bytes 100
  12.6 30.3 %copy-start.26 = (f32[8]{0:T(128)}, f32[8]{0:T(128)S(1)}, u32[]{:S(2)}) copy-start(f32[8]{0:T(128)S(1)} %get-tuple-element.19) | copy-start | bytes 100
  12.6 30.3 %copy-start.28 = (f32[8]{0:T(128)}, f32[8]{0:T(128)S(1)}, u32[]{:S(2)}) copy-start(f32[8]{0:T(128)S(1)} %get-tuple-element.20) | copy-start | bytes 100
  12.7 30.3 %copy-start.30 = (f32[8]{0:T(128)}, f32[8]{0:T(128)S(1)}, u32[]{:S(2)}) copy-start(f32[8]{0:T(128)S(1)} %get-tuple-element.21) | copy-start | bytes 100
  12.7 30.3 %copy-start.32 = (f32[8]{0:T(128)}, f32[8]{0:T(128)S(1)}, u32[]{:S(2)}) copy-start(f32[8]{0:T(128)S(1)} %get-tuple-element.22) | copy-start | bytes 100
  12.7 30.3 %copy-start.34 = (f32[8]{0:T(128)}, f32[8]{0:T(128)S(1)}, u32[]{:S(2)}) copy-start(f32[8]{0:T(128)S(1)} %get-tuple-element.23) | copy-start | bytes 100
  12.7 30.3 %copy-start.36 = (f32[8]{0:T(128)}, f32[8]{0:T(128)S(1)}, u32[]{:S(2)}) copy-start(f32[8]{0:T(128)S(1)} %get-tuple-element.24) | copy-start | bytes 100
  12.7 30.3 %copy-start.38 = (f32[8]{0:T(128)}, f32[8]{0:T(128)S(1)}, u32[]{:S(2)}) copy-start(f32[8]{0:T(128)S(1)} %get-tuple-element.25) | copy-start | bytes 100
  12.7 30.3 %copy-start.40 = (f32[8]{0:T(128)}, f32[8]{0:T(128)S(1)}, u32[]{:S(2)}) copy-start(f32[8]{0:T(128)S(1)} %get-tuple-element.26) | copy-start | bytes 100
  16.8 26.0 %copy-start.43 = (bf16[8]{0:T(256)(128)(2,1)}, bf16[8]{0:T(256)(128)(2,1)S(1)}, u32[]{:S(2)}) copy-start(bf16[8]{0:T(256)(128)(2,1)S(1)} %get-tuple-element.51) | copy-start | bytes 52
  16.8 26.0 %copy-start.45 = (bf16[8]{0:T(256)(128)(2,1)}, bf16[8]{0:T(256)(128)(2,1)S(1)}, u32[]{:S(2)}) copy-start(bf16[8]{0:T(256)(128)(2,1)S(1)} %get-tuple-element.52) | copy-start | bytes 52
  16.9 26.0 %copy-start.47 = (bf16[8]{0:T(256)(128)(2,1)}, bf16[8]{0:T(256)(128)(2,1)S(1)}, u32[]{:S(2)}) copy-start(bf16[8]{0:T(256)(128)(2,1)S(1)} %get-tuple-element.53) | copy-start | bytes 52
  16.9 26.0 %copy-start.49 = (bf16[8]{0:T(256)(128)(2,1)}, bf16[8]{0:T(256)(128)(2,1)S(1)}, u32[]{:S(2)}) copy-start(bf16[8]{0:T(256)(128)(2,1)S(1)} %get-tuple-element.54) | copy-start | bytes 52
  16.9 26.0 %copy-start.51 = (bf16[8]{0:T(256)(128)(2,1)}, bf16[8]{0:T(256)(128)(2,1)S(1)}, u32[]{:S(2)}) copy-start(bf16[8]{0:T(256)(128)(2,1)S(1)} %get-tuple-element.55) | copy-start | bytes 52
  16.9 26.0 %copy-start.53 = (bf16[8]{0:T(256)(128)(2,1)}, bf16[8]{0:T(256)(128)(2,1)S(1)}, u32[]{:S(2)}) copy-start(bf16[8]{0:T(256)(128)(2,1)S(1)} %get-tuple-element.56) | copy-start | bytes 52
  44.2 6.0 %collective-permute-start = (bf16[9,512]{1,0:T(8,128)(2,1)S(1)}, bf16[9,512]{1,0:T(8,128)(2,1)S(1)}, u32[]{:S(2)}, u32[]{:S(2)}) collective-permute-start(bf16[9,512]{1,0:T(8,128)(2,1)S(1)} %get-tuple-element.31), channel_id=1, source_target_pairs={{0,2},{1,3},{4,6},{5,7},{8,10},{9,11},{12,14},{13,15},{16,18},{17,... | collective-permute-start | bytes 27656 | tf_op jit(solution)/shard_map/ppermute | solution.py:19
  47.6 5.6 %collective-permute-start.1 = (bf16[9,512]{1,0:T(8,128)(2,1)S(1)}, bf16[9,512]{1,0:T(8,128)(2,1)S(1)}, u32[]{:S(2)}, u32[]{:S(2)}) collective-permute-start(bf16[9,512]{1,0:T(8,128)(2,1)S(1)} %get-tuple-element.32), channel_id=1, source_target_pairs={{2,0},{3,1},{6,4},{7,5},{10,8},{11,9},{14,12},{15,13},{18,16},{19,... | collective-permute-start | bytes 27656 | tf_op jit(solution)/shard_map/ppermute | solution.py:20
  53.2 5.3 %copy-start.1 = (bf16[9,512]{1,0:T(8,128)(2,1)}, bf16[9,512]{1,0:T(8,128)(2,1)S(1)}, u32[]{:S(2)}) copy-start(bf16[9,512]{1,0:T(8,128)(2,1)S(1)} %collective-permute-done.1) | copy-start | bytes 27652
  53.3 13.3 %collective-permute-start.2 = (bf16[274,9]{1,0:T(8,128)(2,1)S(1)}, bf16[274,9]{1,0:T(8,128)(2,1)}, u32[]{:S(2)}, u32[]{:S(2)}) collective-permute-start(bf16[274,9]{1,0:T(8,128)(2,1)S(1)} %get-tuple-element.29), channel_id=1, source_target_pairs={{0,1},{2,3},{4,5},{6,7},{8,9},{10,11},{12,13},{14,15},{16,17},{18,... | collective-permute-start | bytes 14804 | tf_op jit(solution)/shard_map/ppermute | solution.py:19
  55.3 11.4 %collective-permute-start.3 = (bf16[274,9]{1,0:T(8,128)(2,1)S(1)}, bf16[274,9]{1,0:T(8,128)(2,1)}, u32[]{:S(2)}, u32[]{:S(2)}) collective-permute-start(bf16[274,9]{1,0:T(8,128)(2,1)S(1)} %get-tuple-element.30), channel_id=1, source_target_pairs={{1,0},{3,2},{5,4},{7,6},{9,8},{11,10},{13,12},{15,14},{17,16},{19,... | collective-permute-start | bytes 14804 | tf_op jit(solution)/shard_map/ppermute | solution.py:20
  64.0 2.7 %copy-start.2 = (bf16[9,512]{1,0:T(8,128)(2,1)S(1)}, bf16[9,512]{1,0:T(8,128)(2,1)}, u32[]{:S(2)}) copy-start(bf16[9,512]{1,0:T(8,128)(2,1)} %copy-done.1) | copy-start | bytes 27652
  66.7 6.2 %copy-start = (f32[1,256,512]{2,1,0:T(8,128)S(1)}, f32[1,256,512]{2,1,0:T(8,128)}, u32[]{:S(2)}) copy-start(f32[1,256,512]{2,1,0:T(8,128)} %param.8) | copy-start | bytes 1572868
  66.7 6.2 %copy-start.3 = (f32[1,512]{1,0:T(1,128)S(1)}, f32[1,512]{1,0:T(1,128)}, u32[]{:S(2)}) copy-start(f32[1,512]{1,0:T(1,128)} %get-tuple-element.36) | copy-start | bytes 6148
  66.7 6.2 %copy-start.4 = (f32[1,512]{1,0:T(1,128)S(1)}, f32[1,512]{1,0:T(1,128)}, u32[]{:S(2)}) copy-start(f32[1,512]{1,0:T(1,128)} %get-tuple-element.37) | copy-start | bytes 6148
  66.7 6.2 %copy-start.5 = (f32[1,512]{1,0:T(1,128)S(1)}, f32[1,512]{1,0:T(1,128)}, u32[]{:S(2)}) copy-start(f32[1,512]{1,0:T(1,128)} %get-tuple-element.38) | copy-start | bytes 6148
  66.7 6.2 %copy-start.6 = (f32[1,512]{1,0:T(1,128)S(1)}, f32[1,512]{1,0:T(1,128)}, u32[]{:S(2)}) copy-start(f32[1,512]{1,0:T(1,128)} %get-tuple-element.39) | copy-start | bytes 6148
  66.7 6.2 %copy-start.7 = (f32[1,512]{1,0:T(1,128)S(1)}, f32[1,512]{1,0:T(1,128)}, u32[]{:S(2)}) copy-start(f32[1,512]{1,0:T(1,128)} %get-tuple-element.40) | copy-start | bytes 6148
  66.8 6.2 %copy-start.8 = (f32[1,512]{1,0:T(1,128)S(1)}, f32[1,512]{1,0:T(1,128)}, u32[]{:S(2)}) copy-start(f32[1,512]{1,0:T(1,128)} %get-tuple-element.41) | copy-start | bytes 6148
  66.8 6.2 %copy-start.9 = (f32[1,256]{1,0:T(1,128)S(1)}, f32[1,256]{1,0:T(1,128)}, u32[]{:S(2)}) copy-start(f32[1,256]{1,0:T(1,128)} %get-tuple-element.42) | copy-start | bytes 3076
  66.8 6.2 %copy-start.10 = (f32[1,256]{1,0:T(1,128)S(1)}, f32[1,256]{1,0:T(1,128)}, u32[]{:S(2)}) copy-start(f32[1,256]{1,0:T(1,128)} %get-tuple-element.43) | copy-start | bytes 3076
  66.8 6.2 %copy-start.11 = (f32[1,256]{1,0:T(1,128)S(1)}, f32[1,256]{1,0:T(1,128)}, u32[]{:S(2)}) copy-start(f32[1,256]{1,0:T(1,128)} %get-tuple-element.44) | copy-start | bytes 3076
  66.8 6.2 %copy-start.12 = (f32[1,256]{1,0:T(1,128)S(1)}, f32[1,256]{1,0:T(1,128)}, u32[]{:S(2)}) copy-start(f32[1,256]{1,0:T(1,128)} %get-tuple-element.45) | copy-start | bytes 3076
  66.8 6.2 %copy-start.13 = (f32[1,256]{1,0:T(1,128)S(1)}, f32[1,256]{1,0:T(1,128)}, u32[]{:S(2)}) copy-start(f32[1,256]{1,0:T(1,128)} %get-tuple-element.46) | copy-start | bytes 3076
  66.8 6.2 %copy-start.14 = (f32[1,256]{1,0:T(1,128)S(1)}, f32[1,256]{1,0:T(1,128)}, u32[]{:S(2)}) copy-start(f32[1,256]{1,0:T(1,128)} %get-tuple-element.47) | copy-start | bytes 3076
  66.8 6.2 %copy-start.15 = (f32[1,256]{1,0:T(1,128)S(1)}, f32[1,256]{1,0:T(1,128)}, u32[]{:S(2)}) copy-start(f32[1,256]{1,0:T(1,128)} %get-tuple-element.48) | copy-start | bytes 3076
  66.8 6.2 %copy-start.16 = (f32[1,256]{1,0:T(1,128)S(1)}, f32[1,256]{1,0:T(1,128)}, u32[]{:S(2)}) copy-start(f32[1,256]{1,0:T(1,128)} %get-tuple-element.49) | copy-start | bytes 3076
  66.8 6.2 %copy-start.17 = (f32[1,256]{1,0:T(1,128)S(1)}, f32[1,256]{1,0:T(1,128)}, u32[]{:S(2)}) copy-start(f32[1,256]{1,0:T(1,128)} %get-tuple-element.50) | copy-start | bytes 3076
  73.1 4.1 %copy-start.19 = (f32[8]{0:T(128)S(1)}, f32[8]{0:T(128)}, u32[]{:S(2)}) copy-start(f32[8]{0:T(128)} %copy-done.18) | copy-start | bytes 100
  73.1 4.1 %copy-start.21 = (f32[8]{0:T(128)S(1)}, f32[8]{0:T(128)}, u32[]{:S(2)}) copy-start(f32[8]{0:T(128)} %copy-done.20) | copy-start | bytes 100
  73.1 4.1 %copy-start.23 = (f32[8]{0:T(128)S(1)}, f32[8]{0:T(128)}, u32[]{:S(2)}) copy-start(f32[8]{0:T(128)} %copy-done.22) | copy-start | bytes 100
  73.1 4.1 %copy-start.25 = (f32[8]{0:T(128)S(1)}, f32[8]{0:T(128)}, u32[]{:S(2)}) copy-start(f32[8]{0:T(128)} %copy-done.24) | copy-start | bytes 100
  73.1 4.1 %copy-start.27 = (f32[8]{0:T(128)S(1)}, f32[8]{0:T(128)}, u32[]{:S(2)}) copy-start(f32[8]{0:T(128)} %copy-done.26) | copy-start | bytes 100
  73.1 4.1 %copy-start.29 = (f32[8]{0:T(128)S(1)}, f32[8]{0:T(128)}, u32[]{:S(2)}) copy-start(f32[8]{0:T(128)} %copy-done.28) | copy-start | bytes 100
  73.1 4.1 %copy-start.31 = (f32[8]{0:T(128)S(1)}, f32[8]{0:T(128)}, u32[]{:S(2)}) copy-start(f32[8]{0:T(128)} %copy-done.30) | copy-start | bytes 100
  73.1 4.1 %copy-start.33 = (f32[8]{0:T(128)S(1)}, f32[8]{0:T(128)}, u32[]{:S(2)}) copy-start(f32[8]{0:T(128)} %copy-done.32) | copy-start | bytes 100
  73.2 4.1 %copy-start.35 = (f32[8]{0:T(128)S(1)}, f32[8]{0:T(128)}, u32[]{:S(2)}) copy-start(f32[8]{0:T(128)} %copy-done.34) | copy-start | bytes 100
  73.2 4.1 %copy-start.37 = (f32[8]{0:T(128)S(1)}, f32[8]{0:T(128)}, u32[]{:S(2)}) copy-start(f32[8]{0:T(128)} %copy-done.36) | copy-start | bytes 100
  73.2 4.1 %copy-start.39 = (f32[8]{0:T(128)S(1)}, f32[8]{0:T(128)}, u32[]{:S(2)}) copy-start(f32[8]{0:T(128)} %copy-done.38) | copy-start | bytes 100
  73.2 4.1 %copy-start.41 = (f32[8]{0:T(128)S(1)}, f32[8]{0:T(128)}, u32[]{:S(2)}) copy-start(f32[8]{0:T(128)} %copy-done.40) | copy-start | bytes 100
  73.2 4.1 %copy-start.44 = (bf16[8]{0:T(256)(128)(2,1)S(1)}, bf16[8]{0:T(256)(128)(2,1)}, u32[]{:S(2)}) copy-start(bf16[8]{0:T(256)(128)(2,1)} %copy-done.43) | copy-start | bytes 52
  73.2 4.1 %copy-start.46 = (bf16[8]{0:T(256)(128)(2,1)S(1)}, bf16[8]{0:T(256)(128)(2,1)}, u32[]{:S(2)}) copy-start(bf16[8]{0:T(256)(128)(2,1)} %copy-done.45) | copy-start | bytes 52
  73.2 4.1 %copy-start.48 = (bf16[8]{0:T(256)(128)(2,1)S(1)}, bf16[8]{0:T(256)(128)(2,1)}, u32[]{:S(2)}) copy-start(bf16[8]{0:T(256)(128)(2,1)} %copy-done.47) | copy-start | bytes 52
  73.2 4.1 %copy-start.50 = (bf16[8]{0:T(256)(128)(2,1)S(1)}, bf16[8]{0:T(256)(128)(2,1)}, u32[]{:S(2)}) copy-start(bf16[8]{0:T(256)(128)(2,1)} %copy-done.49) | copy-start | bytes 52
  73.2 4.1 %copy-start.52 = (bf16[8]{0:T(256)(128)(2,1)S(1)}, bf16[8]{0:T(256)(128)(2,1)}, u32[]{:S(2)}) copy-start(bf16[8]{0:T(256)(128)(2,1)} %copy-done.51) | copy-start | bytes 52
  73.2 4.1 %copy-start.54 = (bf16[8]{0:T(256)(128)(2,1)S(1)}, bf16[8]{0:T(256)(128)(2,1)}, u32[]{:S(2)}) copy-start(bf16[8]{0:T(256)(128)(2,1)} %copy-done.53) | copy-start | bytes 52
  73.3 4.1 %copy-start.56 = (s32[8]{0:T(128)S(1)}, s32[8]{0:T(128)}, u32[]{:S(2)}) copy-start(s32[8]{0:T(128)} %copy-done.55) | copy-start | bytes 100
  77.4 1.6 %copy-start.42 = (f32[8]{0:T(128)S(1)}, f32[8]{0:T(128)}, u32[]{:S(2)}) copy-start(f32[8]{0:T(128)} %fusion.154) | copy-start | bytes 100
Sparse Core Ops, SparseCore 0:
  9.5 30.6 all-gather.1

commit v4 on v3

--- a/solution.py
+++ b/solution.py
@@ -153,34 +153,49 @@
     difference = science[0] - model
     lowered = difference.astype(jnp.bfloat16).reshape(strips, strip_rows, half_cols)
     lowered = lax.optimization_barrier(lowered)
-    columns_back = static_shift(lowered, col_weights, -1, half_cols).astype(jnp.bfloat16)
-    contribution = jnp.einsum(
-        "qik,qiz->qkz", row_warp, columns_back, preferred_element_type=jnp.float32
-    )
-    tagged = jnp.concatenate(
+    pad_cols = 128 - 15
+    tag = jnp.concatenate(
         [
-            contribution.reshape(strips, strip_size),
-            jnp.broadcast_to(strip_list.astype(jnp.float32)[:, None] + 1.0, (strips, 128)),
+            row_taps,
+            col_taps,
+            row_shift.astype(jnp.bfloat16)[:, None],
+            col_shift.astype(jnp.bfloat16)[:, None],
+            (strip_list + 1).astype(jnp.bfloat16)[:, None],
+            jnp.zeros((strips, pad_cols), jnp.bfloat16),
         ],
         axis=1,
     )
-    outgoing_back = (
-        jnp.zeros((ccd_count * capacity, strip_size + 128), jnp.float32).at[slot_index].set(tagged)
+    payload = jnp.concatenate([lowered.reshape(strips, strip_size), tag], axis=1)
+    outgoing = (
+        jnp.zeros((ccd_count * capacity, strip_size + 128), jnp.bfloat16).at[slot_index].set(payload)
     )
     returned = lax.all_to_all(
-        outgoing_back.reshape(ccd_count, capacity, strip_size + 128),
+        outgoing.reshape(ccd_count, capacity, strip_size + 128),
         "ccd",
         split_axis=0,
         concat_axis=0,
         tiled=True,
     )
-    returned = returned.reshape(ccd_count * capacity, strip_size + 128)
-    asked_flat = returned[:, strip_size].astype(jnp.int32) - 1
+    slots = ccd_count * capacity
+    returned = returned.reshape(slots, strip_size + 128)
+    got = returned[:, :strip_size].reshape(slots, strip_rows, half_cols)
+    tags = returned[:, strip_size:]
+    got_row_taps = tags[:, 0:6]
+    got_col_taps = tags[:, 6:12]
+    got_row_shift = tags[:, 12].astype(jnp.int32)
+    got_col_shift = tags[:, 13].astype(jnp.int32)
+    asked_flat = tags[:, 14].astype(jnp.int32) - 1
+    back_weights = shift_weights(got_col_taps, got_col_shift)
+    columns_back = static_shift(got, back_weights, -1, half_cols).astype(jnp.bfloat16)
+    back_op = strip_operator(got_row_taps, got_row_shift, strip_rows)
+    contribution = jnp.einsum(
+        "qik,qiz->qkz", back_op, columns_back, preferred_element_type=jnp.float32
+    )
     owner_select = (asked_flat[:, None] == jnp.arange(strips)[None, :]).astype(jnp.float32)
     stack = jnp.einsum(
         "sp,sz->pz",
         owner_select,
-        returned[:, :strip_size],
+        contribution.reshape(slots, strip_size),
         precision=lax.Precision.HIGHEST,
     )
     return (difference[None], stack.reshape(template.shape))

time: 108 us -> 106 us (0.981)
  blocking collectives: 18.6 us -> 13 us
  local copies, waits for them, and re-layouts: 17.1 us -> 20.9 us
    all_to_all x1, blocking collectives: 18.6 us -> 13 us  [body(): lax.all_to_all(outgoing.reshape(ccd_count, capacity, strip_size + 128), '...]
    convert_element_type x0 -> x6, local copies, waits for them, and re-layouts: none -> 3.47 us  [the longest x2 1.35 us: lanczos_taps(): return (jnp.sinc(spread) * jnp.sinc(spread / 3.0)).astype(jnp.bfloat16)]
    convert_element_type x0 -> x3, other arithmetic: none -> 3.27 us  [the longest x1 1.35 us: body(): col_shift.astype(jnp.bfloat16)[:, None]]
    add x1 -> x0, other arithmetic: 1.23 us -> none  [body(): strip_list.astype(jnp.float32)[:, None] + 1.0]
    scatter x0 -> x1, local copies, waits for them, and re-layouts: none -> 1.14 us  [body(): jnp.zeros((ccd_count * capacity, strip_size + 128), jnp.bfloat16)]
    scatter x1 -> x0, other arithmetic: 1.14 us -> none  [body(): jnp.zeros((ccd_count * capacity, strip_size + 128), jnp.float32)]
    unnamed x117 -> x65, local copies, waits for them, and re-layouts: 3.47 us -> 3.19 us
  transfers between devices with their start and end apart: 5 -> 5, of which waited for: 2 -> 2; matrix products, arithmetic and copies ran while one was open for 20% -> 24% of each run, Pallas kernels for 0% -> 0%
where the time goes in v4:
time: 106 us
  waiting for transfers between devices  24.7 us (23%)
  local copies, waits for them, and re-layouts  20.9 us (20%)
  other arithmetic  15.8 us (15%)
  between operations  14.8 us (14%)
  blocking collectives  13 us (12%)
  matrix products  8.67 us (8%)
  starting transfers between devices  8.09 us (8%)
    all_gather x1, waiting for transfers between devices, body(): lax.all_gather(template, 'ccd', axis=0, tiled=True).reshape(-1, strip_size)  21 us
    all_to_all x1, blocking collectives, body(): lax.all_to_all(outgoing.reshape(ccd_count, capacity, strip_size + 128), '...  13 us
    dot_general x1, matrix products, body(): terms = jnp.dot(across_all, column_mats, preferred_element_type=jnp.float32)  6.06 us
    ppermute x2, starting transfers between devices, padded_2(): before = lax.ppermute(last, axis, up)  5.3 us
    reshape x6, local copies, waits for them, and re-layouts, band_operator(): return flat.reshape(count, width)  4.73 us
    another operation x12, local copies, waits for them, and re-layouts, band_operator(): flat = jnp.tile(line, count)[:count * width]  4.14 us
    convert_element_type x1, other arithmetic, body(): difference.astype(jnp.bfloat16).reshape(strips, strip_rows, half_cols)  3.95 us
    unnamed x65, local copies, waits for them, and re-layouts  3.19 us
  transfers between devices with their start and end apart: 5, of which 2 were waited for; matrix products, arithmetic and copies ran while one was open for 24% of the time, Pallas kernels for 0%

profile of v4, /device:TPU:0, one launch (start us, length us, event | category | flops | bytes accessed | tf_op | source)
XLA Modules:
  0.0 105.9 jit_solution(7664171334587528190)
XLA Ops:
  7.2 0.7 all-gather.2.cloned.1.call-update
  8.0 0.6 exponential_reduce_fusion.1
  8.6 0.8 slice_bitcast_fusion.7
  9.3 1.4 %convert_bitcast_fusion.1 = (bf16[8,1]{0,1:T(2,128)(2,1)}, bf16[8,1]{0,1:T(2,128)(2,1)}, s32[8]{0:T(128)S(1)}, s32[8]{0:T(128)S(1)}) fusion(s32[1,1,1,2,8]{4,3,2,1,0:T(2,128)} %param.12), kind=kLoop, calls=%fused_computation.302 | loop fusion | flops 16 | bytes 160 | tf_op jit(solution)/shard_map/convert_element_type | solution.py:162
  10.7 1.2 %convert_bitcast_fusion = bf16[8,1]{0,1:T(2,128)(2,1)} fusion(s32[1,1,1,8]{3,2,1,0:T(1,128)} %param.11), kind=kLoop, calls=%fused_computation.301 | loop fusion | flops 16 | bytes 48 | tf_op jit(solution)/shard_map/convert_element_type | solution.py:163
  11.9 0.7 bitcast_add_fusion.1
  12.7 0.7 fusion.176
  13.4 0.1 select_reduce_fusion.1
  13.4 0.4 slice_reduce_fusion.23
  13.8 0.9 select_reduce_fusion.2
  14.8 0.7 convert_bitcast_fusion.5
  15.4 0.6 abs_reduce_fusion
  16.0 1.2 %fusion.183 = s32[8]{0:T(128)} fusion(s32[8]{0:T(128)S(1)} %select_reduce_fusion.2, s32[1,1,1,8,1]{3,4,2,1,0:T(1,128)} %param.10), kind=kLoop, calls=%fused_computation.298 | loop fusion | flops 40 | bytes 96 | tf_op jit(solution)/shard_map/select_n | solution.py:170
  17.2 0.7 slice_bitcast_fusion.10
  18.0 0.6 fusion.206
  18.7 0.6 fusion.205
  19.3 21.0 %all-gather.2.cloned.1.call-done = bf16[4,1,1,8,32,512]{5,4,3,2,1,0:T(8,128)(2,1)} async-done(((bf16[1,1,1,8,32,512]{5,4,3,2,1,0:T(8,128)(2,1)}), bf16[4,1,1,8,32,512]{5,4,3,2,1,0:T(8,128)(2,1)}) %all-gather.2.cloned.1.call-update) | async-done | bytes 1048592 | tf_op jit(solution)/shard_map/all_gather | solution.py:104
  40.3 1.8 %copy.77 = bf16[4,8,32,512]{3,1,2,0:T(8,128)(2,1)S(1)} copy(bf16[4,8,32,512]{3,2,1,0:T(8,128)(2,1)} %bitcast.107) | data formatting | bytes 2097152
  42.1 0.3 convolution_convert_fusion
  42.4 0.4 convolution_convert_fusion.2
  42.8 1.2 %add_convert_fusion.1 = bf16[8,32,512]{2,1,0:T(8,128)(2,1)S(1)} fusion(bf16[8,32,512]{2,1,0:T(8,128)(2,1)S(1)} %convolution_convert_fusion.2, f32[8]{0:T(128)S(1)} %get-tuple-element.37, f32[8]{0:T(128)S(1)} %get-tuple-element.38, f32[8]{0:T(128)S(1)} %get-tuple-element.39, f32[8]{0:T(128)S(1)} %get-tuple-element.40, f32[8]{0:T(128)S(1)} %get-tuple-element.41, ...), kind=kLoop, calls=%fused_computation.36 | loop fusion | flops 4718592 | bytes 524672 | tf_op jit(solution)/shard_map/convert_element_type | solution.py:121
  44.0 3.4 %collective-permute-start = (bf16[9,512]{1,0:T(8,128)(2,1)S(1)}, bf16[9,512]{1,0:T(8,128)(2,1)S(1)}, u32[]{:S(2)}, u32[]{:S(2)}) collective-permute-start(bf16[9,512]{1,0:T(8,128)(2,1)S(1)} %get-tuple-element.52), channel_id=1, source_target_pairs={{0,2},{1,3},{4,6},{5,7},{8,10},{9,11},{12,14},{13,15},{16,18},{17,... | collective-permute-start | bytes 27656 | tf_op jit(solution)/shard_map/ppermute | solution.py:19
  47.4 1.3 %collective-permute-start.1 = (bf16[9,512]{1,0:T(8,128)(2,1)S(1)}, bf16[9,512]{1,0:T(8,128)(2,1)S(1)}, u32[]{:S(2)}, u32[]{:S(2)}) collective-permute-start(bf16[9,512]{1,0:T(8,128)(2,1)S(1)} %get-tuple-element.53), channel_id=1, source_target_pairs={{2,0},{3,1},{6,4},{7,5},{10,8},{11,9},{14,12},{15,13},{18,16},{19,... | collective-permute-start | bytes 27656 | tf_op jit(solution)/shard_map/ppermute | solution.py:20
  48.7 0.7 convert_bitcast_fusion.4
  49.4 0.6 exponential_reduce_fusion
  50.0 3.1 %collective-permute-done.1 = bf16[9,512]{1,0:T(8,128)(2,1)S(1)} collective-permute-done((bf16[9,512]{1,0:T(8,128)(2,1)S(1)}, bf16[9,512]{1,0:T(8,128)(2,1)S(1)}, u32[]{:S(2)}, u32[]{:S(2)}) %collective-permute-start.1) | collective-permute-done | bytes 9248 | tf_op jit(solution)/shard_map/ppermute | solution.py:20
  53.1 0.1 pad_maximum_fusion.2
  53.2 1.9 %collective-permute-start.2 = (bf16[274,9]{1,0:T(8,128)(2,1)S(1)}, bf16[274,9]{1,0:T(8,128)(2,1)}, u32[]{:S(2)}, u32[]{:S(2)}) collective-permute-start(bf16[274,9]{1,0:T(8,128)(2,1)S(1)} %get-tuple-element.50), channel_id=1, source_target_pairs={{0,1},{2,3},{4,5},{6,7},{8,9},{10,11},{12,13},{14,15},{16,17},{18,... | collective-permute-start | bytes 14804 | tf_op jit(solution)/shard_map/ppermute | solution.py:19
  55.1 1.5 %collective-permute-start.3 = (bf16[274,9]{1,0:T(8,128)(2,1)S(1)}, bf16[274,9]{1,0:T(8,128)(2,1)}, u32[]{:S(2)}, u32[]{:S(2)}) collective-permute-start(bf16[274,9]{1,0:T(8,128)(2,1)S(1)} %get-tuple-element.51), channel_id=1, source_target_pairs={{1,0},{3,2},{5,4},{7,6},{9,8},{11,10},{13,12},{15,14},{17,16},{19,... | collective-permute-start | bytes 14804 | tf_op jit(solution)/shard_map/ppermute | solution.py:20
  56.6 0.6 convert_bitcast_fusion.3
  57.2 0.7 copy.67
  57.9 0.9 tile.61
  58.9 1.1 %reshape.378 = bf16[512,530]{1,0:T(8,128)(2,1)S(1)} reshape(bf16[271360]{0:T(1024)(128)(2,1)S(1)} %slice.468) | data formatting | bytes 1085440 | tf_op jit(solution)/shard_map/reshape | solution.py:84
  60.1 0.9 tile.63
  61.1 1.1 %reshape.379 = bf16[512,530]{1,0:T(8,128)(2,1)S(1)} reshape(bf16[271360]{0:T(1024)(128)(2,1)S(1)} %slice.469) | data formatting | bytes 1085440 | tf_op jit(solution)/shard_map/reshape | solution.py:84
  62.3 0.9 tile.65
  63.2 1.1 %reshape.380 = bf16[512,530]{1,0:T(8,128)(2,1)S(1)} reshape(bf16[271360]{0:T(1024)(128)(2,1)S(1)} %slice.470) | data formatting | bytes 1085440 | tf_op jit(solution)/shard_map/reshape | solution.py:84
  64.5 0.4 tile.25
  64.9 0.4 reshape.370
  65.3 0.4 tile.27
  65.7 0.4 reshape.371
  66.2 0.4 tile.29
  66.6 0.4 reshape.372
  67.1 0.7 copy.68
  67.7 0.7 copy.69
  68.4 0.7 copy.70
  69.1 0.7 copy.71
  70.0 6.1 %fusion = f32[768,1536]{1,0:T(8,128)} fusion(bf16[530,512]{0,1:T(8,128)(2,1)S(1)} %bitcast.112, bf16[530,512]{0,1:T(8,128)(2,1)S(1)} %bitcast.111, bf16[530,512]{0,1:T(8,128)(2,1)S(1)} %bitcast.110, bf16[256,274]{1,0:T(8,128)(2,1)S(1)} %reshape.372, bf16[256,274]{1,0:T(8,128)(2,1)S(1)} %reshape.371, bf16[256,274]{1,0:T(8,128)(2,1)S(1)} %reshape.370, ...), kind=kOutput, calls=%fused_computation.2 | convolution fusion | flops 1481491072 | bytes 7058056 | tf_op jit(solution)/shard_map/dot_general | solution.py:143
  76.2 4.0 %fusion.202 = (bf16[256,512]{1,0:T(8,128)(2,1)S(1)}, f32[256,512]{1,0:T(8,128)}) fusion(f32[768,1536]{1,0:T(8,128)} %fusion, f32[256]{0:T(256)S(1)} %bitcast.128, f32[512]{0:T(512)S(1)} %bitcast.119, f32[256]{0:T(256)S(1)} %bitcast.129, f32[512]{0:T(512)S(1)} %bitcast.120, f32[256]{0:T(256)S(1)} %bitcast.130, f32[512]{0:T(512)S(1)} %bitcast.121, ...), kind=kLoop, calls=%fused_computation.344 | loop fusion | flops 3670016 | bytes 6056960 | tf_op jit(solution)/shard_map/convert_element_type | solution.py:154
  80.2 0.1 copy.78
  80.4 0.1 concatenate.43
  80.5 1.1 %scatter_custom_fusion = bf16[8,16512]{1,0:T(8,128)(2,1)S(1)} fusion(s32[8]{0:T(128)} %fusion.183, bf16[8,16512]{1,0:T(8,128)(2,1)S(1)} %concatenate.43, bf16[]{:T(256)} %constant.22.clone.1), kind=kCustom, calls=%fused_computation.81 | custom fusion | bytes 264704 | tf_op jit(solution)/shard_map/scatter | solution.py:170
  81.6 0.1 reshape.383
  81.7 13.0 %all_to_all.5 = bf16[4,2,16512]{2,1,0:T(2,128)(2,1)S(1)} all-to-all(bf16[4,2,16512]{2,1,0:T(2,128)(2,1)S(1)} %reshape.383), channel_id=1, replica_groups=mesh['grp'=2,'ccd'=4,'row'=2,'amp'=2] {'ccd'}, dimensions={0} | all-to-all | bytes 528384 | tf_op jit(solution)/shard_map/all_to_all | solution.py:172
  94.7 0.1 reshape.384
  94.9 0.2 add_reduce_fusion
  95.1 0.2 slice_reduce_fusion.29
  95.4 0.1 copy.72
  95.5 0.1 select_reduce_fusion
  95.6 0.4 slice_reduce_fusion.11
  96.0 0.1 copy.73
  96.1 1.2 %convolution_bitcast_fusion.1 = f32[1,8,32,512]{3,2,1,0:T(8,128)S(1)} fusion(bf16[8,32,512]{2,1,0:T(8,128)(2,1)S(1)} %copy.73, f32[8]{0:T(128)S(1)} %get-tuple-element.25, f32[8]{0:T(128)S(1)} %get-tuple-element.26, f32[8]{0:T(128)S(1)} %get-tuple-element.27, f32[8]{0:T(128)S(1)} %get-tuple-element.28, f32[8]{0:T(128)S(1)} %get-tuple-element.29, ...), kind=kOutput, calls=%fused_computation.10 | convolution fusion | flops 13213696 | bytes 791040 | tf_op jit(solution)/shard_map/qik,qiz->qkz/dot_general | solution.py:191
  97.3 0.7 convolution_bitcast_fusion
  98.0 1.1 %copy.75 = f32[1,1,1,8,32,512]{5,4,3,2,1,0:T(8,128)} copy(f32[1,1,1,8,32,512]{5,3,4,2,1,0:T(8,128)S(1)} %convolution_bitcast_fusion) | data formatting | bytes 1048576
  (96 shorter events, 1.0 us)
Async XLA Ops:
  7.2 33.1 %all-gather.2.cloned.1.call-start = ((), (), s32[]{:S(2)}) async-start(), calls=%async_computation.1 | async-start | bytes 1310720 | tf_op jit(solution)/shard_map/all_gather | solution.py:104
  7.9 4.8 %copy-start.26 = (s32[6]{0:T(128)}, s32[6]{0:T(128)S(1)}, u32[]{:S(2)}) copy-start(s32[6]{0:T(128)S(1)} %iota_add_fusion) | copy-start | bytes 76
  8.0 5.9 %copy-start.24 = (s32[12]{0:T(128)}, s32[12]{0:T(128)S(1)}, u32[]{:S(2)}) copy-start(s32[12]{0:T(128)S(1)} %iota_add_fusion.1) | copy-start | bytes 148
  44.0 5.9 %collective-permute-start = (bf16[9,512]{1,0:T(8,128)(2,1)S(1)}, bf16[9,512]{1,0:T(8,128)(2,1)S(1)}, u32[]{:S(2)}, u32[]{:S(2)}) collective-permute-start(bf16[9,512]{1,0:T(8,128)(2,1)S(1)} %get-tuple-element.52), channel_id=1, source_target_pairs={{0,2},{1,3},{4,6},{5,7},{8,10},{9,11},{12,14},{13,15},{16,18},{17,... | collective-permute-start | bytes 27656 | tf_op jit(solution)/shard_map/ppermute | solution.py:19
  47.4 5.6 %collective-permute-start.1 = (bf16[9,512]{1,0:T(8,128)(2,1)S(1)}, bf16[9,512]{1,0:T(8,128)(2,1)S(1)}, u32[]{:S(2)}, u32[]{:S(2)}) collective-permute-start(bf16[9,512]{1,0:T(8,128)(2,1)S(1)} %get-tuple-element.53), channel_id=1, source_target_pairs={{2,0},{3,1},{6,4},{7,5},{10,8},{11,9},{14,12},{15,13},{18,16},{19,... | collective-permute-start | bytes 27656 | tf_op jit(solution)/shard_map/ppermute | solution.py:20
  53.0 4.1 %copy-start.1 = (bf16[9,512]{1,0:T(8,128)(2,1)}, bf16[9,512]{1,0:T(8,128)(2,1)S(1)}, u32[]{:S(2)}) copy-start(bf16[9,512]{1,0:T(8,128)(2,1)S(1)} %collective-permute-done.1) | copy-start | bytes 27652
  53.2 16.6 %collective-permute-start.2 = (bf16[274,9]{1,0:T(8,128)(2,1)S(1)}, bf16[274,9]{1,0:T(8,128)(2,1)}, u32[]{:S(2)}, u32[]{:S(2)}) collective-permute-start(bf16[274,9]{1,0:T(8,128)(2,1)S(1)} %get-tuple-element.50), channel_id=1, source_target_pairs={{0,1},{2,3},{4,5},{6,7},{8,9},{10,11},{12,13},{14,15},{16,17},{18,... | collective-permute-start | bytes 14804 | tf_op jit(solution)/shard_map/ppermute | solution.py:19
  55.1 14.7 %collective-permute-start.3 = (bf16[274,9]{1,0:T(8,128)(2,1)S(1)}, bf16[274,9]{1,0:T(8,128)(2,1)}, u32[]{:S(2)}, u32[]{:S(2)}) collective-permute-start(bf16[274,9]{1,0:T(8,128)(2,1)S(1)} %get-tuple-element.51), channel_id=1, source_target_pairs={{1,0},{3,2},{5,4},{7,6},{9,8},{11,10},{13,12},{15,14},{17,16},{19,... | collective-permute-start | bytes 14804 | tf_op jit(solution)/shard_map/ppermute | solution.py:20
  64.4 2.7 %copy-start.14 = (bf16[8,6]{0,1:T(8,128)(2,1)S(1)}, bf16[8,6]{0,1:T(8,128)(2,1)}, u32[]{:S(2)}) copy-start(bf16[8,6]{0,1:T(8,128)(2,1)} %get-tuple-element.85) | copy-start | bytes 292
  64.4 3.4 %copy-start.29 = (bf16[8,1]{0,1:T(2,128)(2,1)S(1)}, bf16[8,1]{0,1:T(2,128)(2,1)}, u32[]{:S(2)}) copy-start(bf16[8,1]{0,1:T(2,128)(2,1)} %get-tuple-element.82) | copy-start | bytes 52
  64.4 4.0 %copy-start.28 = (bf16[8,1]{0,1:T(2,128)(2,1)S(1)}, bf16[8,1]{0,1:T(2,128)(2,1)}, u32[]{:S(2)}) copy-start(bf16[8,1]{0,1:T(2,128)(2,1)} %get-tuple-element.81) | copy-start | bytes 52
  64.4 4.7 %copy-start.30 = (bf16[8,1]{0,1:T(2,128)(2,1)S(1)}, bf16[8,1]{0,1:T(2,128)(2,1)}, u32[]{:S(2)}) copy-start(bf16[8,1]{0,1:T(2,128)(2,1)} %convert_bitcast_fusion) | copy-start | bytes 52
  64.4 5.4 %copy-start.2 = (bf16[9,512]{1,0:T(8,128)(2,1)S(1)}, bf16[9,512]{1,0:T(8,128)(2,1)}, u32[]{:S(2)}) copy-start(bf16[9,512]{1,0:T(8,128)(2,1)} %copy-done.1) | copy-start | bytes 27652
  69.8 6.2 %copy-start = (f32[1,256,512]{2,1,0:T(8,128)S(1)}, f32[1,256,512]{2,1,0:T(8,128)}, u32[]{:S(2)}) copy-start(f32[1,256,512]{2,1,0:T(8,128)} %param.8) | copy-start | bytes 1572868
  69.8 6.2 %copy-start.3 = (f32[1,512]{1,0:T(1,128)S(1)}, f32[1,512]{1,0:T(1,128)}, u32[]{:S(2)}) copy-start(f32[1,512]{1,0:T(1,128)} %get-tuple-element.57) | copy-start | bytes 6148
  69.8 6.2 %copy-start.4 = (f32[1,512]{1,0:T(1,128)S(1)}, f32[1,512]{1,0:T(1,128)}, u32[]{:S(2)}) copy-start(f32[1,512]{1,0:T(1,128)} %get-tuple-element.58) | copy-start | bytes 6148
  69.8 6.2 %copy-start.5 = (f32[1,512]{1,0:T(1,128)S(1)}, f32[1,512]{1,0:T(1,128)}, u32[]{:S(2)}) copy-start(f32[1,512]{1,0:T(1,128)} %get-tuple-element.59) | copy-start | bytes 6148
  69.8 6.2 %copy-start.6 = (f32[1,512]{1,0:T(1,128)S(1)}, f32[1,512]{1,0:T(1,128)}, u32[]{:S(2)}) copy-start(f32[1,512]{1,0:T(1,128)} %get-tuple-element.60) | copy-start | bytes 6148
  69.8 6.2 %copy-start.7 = (f32[1,512]{1,0:T(1,128)S(1)}, f32[1,512]{1,0:T(1,128)}, u32[]{:S(2)}) copy-start(f32[1,512]{1,0:T(1,128)} %get-tuple-element.61) | copy-start | bytes 6148
  69.9 6.2 %copy-start.8 = (f32[1,512]{1,0:T(1,128)S(1)}, f32[1,512]{1,0:T(1,128)}, u32[]{:S(2)}) copy-start(f32[1,512]{1,0:T(1,128)} %get-tuple-element.62) | copy-start | bytes 6148
  69.9 6.2 %copy-start.15 = (f32[1,256]{1,0:T(1,128)S(1)}, f32[1,256]{1,0:T(1,128)}, u32[]{:S(2)}) copy-start(f32[1,256]{1,0:T(1,128)} %get-tuple-element.63) | copy-start | bytes 3076
  69.9 6.2 %copy-start.16 = (f32[1,256]{1,0:T(1,128)S(1)}, f32[1,256]{1,0:T(1,128)}, u32[]{:S(2)}) copy-start(f32[1,256]{1,0:T(1,128)} %get-tuple-element.64) | copy-start | bytes 3076
  69.9 6.2 %copy-start.17 = (f32[1,256]{1,0:T(1,128)S(1)}, f32[1,256]{1,0:T(1,128)}, u32[]{:S(2)}) copy-start(f32[1,256]{1,0:T(1,128)} %get-tuple-element.65) | copy-start | bytes 3076
  69.9 6.2 %copy-start.18 = (f32[1,256]{1,0:T(1,128)S(1)}, f32[1,256]{1,0:T(1,128)}, u32[]{:S(2)}) copy-start(f32[1,256]{1,0:T(1,128)} %get-tuple-element.66) | copy-start | bytes 3076
  69.9 6.2 %copy-start.19 = (f32[1,256]{1,0:T(1,128)S(1)}, f32[1,256]{1,0:T(1,128)}, u32[]{:S(2)}) copy-start(f32[1,256]{1,0:T(1,128)} %get-tuple-element.67) | copy-start | bytes 3076
  69.9 6.2 %copy-start.20 = (f32[1,256]{1,0:T(1,128)S(1)}, f32[1,256]{1,0:T(1,128)}, u32[]{:S(2)}) copy-start(f32[1,256]{1,0:T(1,128)} %get-tuple-element.68) | copy-start | bytes 3076
  69.9 6.2 %copy-start.21 = (f32[1,256]{1,0:T(1,128)S(1)}, f32[1,256]{1,0:T(1,128)}, u32[]{:S(2)}) copy-start(f32[1,256]{1,0:T(1,128)} %get-tuple-element.69) | copy-start | bytes 3076
  69.9 6.2 %copy-start.22 = (f32[1,256]{1,0:T(1,128)S(1)}, f32[1,256]{1,0:T(1,128)}, u32[]{:S(2)}) copy-start(f32[1,256]{1,0:T(1,128)} %get-tuple-element.70) | copy-start | bytes 3076
  69.9 6.2 %copy-start.23 = (f32[1,256]{1,0:T(1,128)S(1)}, f32[1,256]{1,0:T(1,128)}, u32[]{:S(2)}) copy-start(f32[1,256]{1,0:T(1,128)} %get-tuple-element.71) | copy-start | bytes 3076
  76.2 4.2 %copy-start.9 = (bf16[8,1]{1,0:T(8,128)(2,1)S(1)}, bf16[8,1]{1,0:T(8,128)(2,1)}, u32[]{:S(2)}) copy-start(bf16[8,1]{1,0:T(8,128)(2,1)} %copy.69) | copy-start | bytes 52
  76.2 4.2 %copy-start.10 = (bf16[8,1]{1,0:T(8,128)(2,1)S(1)}, bf16[8,1]{1,0:T(8,128)(2,1)}, u32[]{:S(2)}) copy-start(bf16[8,1]{1,0:T(8,128)(2,1)} %copy.70) | copy-start | bytes 52
  76.2 4.2 %copy-start.11 = (bf16[8,1]{1,0:T(8,128)(2,1)S(1)}, bf16[8,1]{1,0:T(8,128)(2,1)}, u32[]{:S(2)}) copy-start(bf16[8,1]{1,0:T(8,128)(2,1)} %copy.71) | copy-start | bytes 52
  76.2 4.2 %copy-start.12 = (bf16[8,6]{1,0:T(8,128)(2,1)S(1)}, bf16[8,6]{1,0:T(8,128)(2,1)}, u32[]{:S(2)}) copy-start(bf16[8,6]{1,0:T(8,128)(2,1)} %copy.67) | copy-start | bytes 292
  76.2 4.2 %copy-start.13 = (bf16[8,6]{1,0:T(8,128)(2,1)S(1)}, bf16[8,6]{1,0:T(8,128)(2,1)}, u32[]{:S(2)}) copy-start(bf16[8,6]{1,0:T(8,128)(2,1)} %copy.68) | copy-start | bytes 292
  80.2 15.3 %copy-start.27 = (s32[6]{0:T(128)S(1)}, s32[6]{0:T(128)}, u32[]{:S(2)}) copy-start(s32[6]{0:T(128)} %copy-done.26) | copy-start | bytes 76
  80.2 15.3 %copy-start.25 = (s32[12]{0:T(128)S(1)}, s32[12]{0:T(128)}, u32[]{:S(2)}) copy-start(s32[12]{0:T(128)} %copy-done.24) | copy-start | bytes 148
Sparse Core Ops, SparseCore 0:
  9.5 30.6 all-gather.1

commit v5 on v4

--- a/solution.py
+++ b/solution.py
@@ -20,6 +20,39 @@
         after = lax.ppermute(first, axis, down)
         value = jnp.concatenate([before, value, after], axis=dim)
     return value
+
+
+def halo_once(image, width):
+    rows, cols = (lax.axis_size("row"), lax.axis_size("amp"))
+
+    def place(r, a):
+        return r * cols + a
+
+    def diagonal(block, dr, da):
+        pairs = [
+            (place(r, a), place(r + dr, a + da))
+            for r in range(rows)
+            for a in range(cols)
+            if 0 <= r + dr < rows and 0 <= a + da < cols
+        ]
+        return lax.ppermute(block, ("row", "amp"), pairs)
+
+    up = [(i, i + 1) for i in range(rows - 1)]
+    down = [(j, i) for i, j in up]
+    right = [(i, i + 1) for i in range(cols - 1)]
+    left = [(j, i) for i, j in right]
+    above = lax.ppermute(image[-width:], "row", up)
+    below = lax.ppermute(image[:width], "row", down)
+    west = lax.ppermute(image[:, -width:], "amp", right)
+    east = lax.ppermute(image[:, :width], "amp", left)
+    north_west = diagonal(image[-width:, -width:], 1, 1)
+    north_east = diagonal(image[-width:, :width], 1, -1)
+    south_west = diagonal(image[:width, -width:], -1, 1)
+    south_east = diagonal(image[:width, :width], -1, -1)
+    top = jnp.concatenate([north_west, above, north_east], axis=1)
+    middle = jnp.concatenate([west, image, east], axis=1)
+    bottom = jnp.concatenate([south_west, below, south_east], axis=1)
+    return jnp.concatenate([top, middle, bottom], axis=0)
 
 
 def lanczos_taps(fraction):
@@ -120,7 +153,7 @@
     col_weights = shift_weights(col_taps, col_shift)
     warped = static_shift(rows_done, col_weights, 1, half_cols).astype(jnp.bfloat16)
     image = warped.reshape(band_rows, half_cols)
-    padded = padded_2(image, (("row", 0), ("amp", 1)), RADIUS)
+    padded = halo_once(image, RADIUS)
     row_place = (
         (lax.axis_index("row") * band_rows + jnp.arange(band_rows) + 0.5)
         / (band_rows * row_count)

time: 106 us -> 101 us (0.953)
  starting transfers between devices: 8.09 us -> 16 us
  local copies, waits for them, and re-layouts: 20.9 us -> 16.2 us
  waiting for transfers between devices: 24.7 us -> 20.2 us
  other arithmetic: 15.8 us -> 13.3 us
  blocking collectives: 13 us -> 11.5 us
    ppermute x4 -> x8, starting transfers between devices: 8.05 us -> 15.9 us  [the longest x4 8.07 us: diagonal(): return lax.ppermute(block, ('row', 'amp'), pairs)]
    all_gather x1, waiting for transfers between devices: 21 us -> 15.6 us  [body(): lax.all_gather(template, 'ccd', axis=0, tiled=True).reshape(-1, strip_size)]
    all_to_all x1, blocking collectives: 13 us -> 11.5 us  [body(): lax.all_to_all(outgoing.reshape(ccd_count, capacity, strip_size + 128), '...]
    slice x2, local copies, waits for them, and re-layouts: 1.24 us -> 0.03 us  [body(): weight = col_weight[basis][None, :] + row_weight[basis][:, None]]
    convert_element_type x2, local copies, waits for them, and re-layouts: 1.35 us -> 0.19 us  [lanczos_taps(): return (jnp.sinc(spread) * jnp.sinc(spread / 3.0)).astype(jnp.bfloat16)]
    ppermute x4 -> x8, waiting for transfers between devices: 3.08 us -> 3.89 us  [the longest x4 3.87 us: diagonal(): return lax.ppermute(block, ('row', 'amp'), pairs)]
    unnamed x65 -> x9, local copies, waits for them, and re-layouts: 3.19 us -> 3.08 us
  transfers between devices with their start and end apart: 5 -> 9, of which waited for: 2 -> 3; matrix products, arithmetic and copies ran while one was open for 24% -> 19% of each run, Pallas kernels for 0% -> 0%
where the time goes in v5:
time: 101 us; the launch traced here: 100 us
  waiting for transfers between devices  20.2 us (20%)
  local copies, waits for them, and re-layouts  16.2 us (16%)
  starting transfers between devices  16 us (16%)
  between operations  14.5 us (14%)
  other arithmetic  13.3 us (13%)
  blocking collectives  11.5 us (11%)
  matrix products  8.62 us (9%)
    all_gather x1, waiting for transfers between devices, body(): lax.all_gather(template, 'ccd', axis=0, tiled=True).reshape(-1, strip_size)  15.6 us
    all_to_all x1, blocking collectives, body(): lax.all_to_all(outgoing.reshape(ccd_count, capacity, strip_size + 128), '...  11.5 us
    ppermute x4, starting transfers between devices, diagonal(): return lax.ppermute(block, ('row', 'amp'), pairs)  8.07 us
    dot_general x1, matrix products, body(): terms = jnp.dot(across_all, column_mats, preferred_element_type=jnp.float32)  6.01 us
    reshape x6, local copies, waits for them, and re-layouts, band_operator(): return flat.reshape(count, width)  4.78 us
    another operation x12, local copies, waits for them, and re-layouts, band_operator(): flat = jnp.tile(line, count)[:count * width]  4.18 us
    ppermute x4, waiting for transfers between devices, diagonal(): return lax.ppermute(block, ('row', 'amp'), pairs)  3.87 us
    convert_element_type x1, other arithmetic, body(): difference.astype(jnp.bfloat16).reshape(strips, strip_rows, half_cols)  3.74 us
  transfers between devices with their start and end apart: 9, of which 3 were waited for; matrix products, arithmetic and copies ran while one was open for 19% of the time, Pallas kernels for 0%

profile of v5, /device:TPU:0, one launch (start us, length us, event | category | flops | bytes accessed | tf_op | source)
XLA Modules:
  0.0 100.2 jit_solution(18071731160133349078)
XLA Ops:
  7.2 0.7 all-gather.2.cloned.1.call-update
  7.9 0.7 exponential_reduce_fusion.1
  8.6 0.6 abs_reduce_fusion
  9.3 0.6 exponential_reduce_fusion
  9.9 0.8 slice_bitcast_fusion.7
  10.6 0.8 convert_bitcast_fusion.1
  11.4 0.7 convert_bitcast_fusion
  12.0 0.7 bitcast_add_fusion.1
  12.8 0.1 fusion.192
  13.0 0.4 slice_reduce_fusion.23
  13.3 0.7 convert_bitcast_fusion.5
  14.0 0.7 convert_bitcast_fusion.4
  14.7 0.9 select_reduce_fusion.2
  15.7 0.7 convert_bitcast_fusion.3
  16.5 0.9 tile.61
  17.4 1.2 %reshape.378 = bf16[512,530]{1,0:T(8,128)(2,1)S(1)} reshape(bf16[271360]{0:T(1024)(128)(2,1)S(1)} %slice.490) | data formatting | bytes 1085440 | tf_op jit(solution)/shard_map/reshape | solution.py:117
  18.7 0.9 tile.63
  19.6 1.2 %reshape.379 = bf16[512,530]{1,0:T(8,128)(2,1)S(1)} reshape(bf16[271360]{0:T(1024)(128)(2,1)S(1)} %slice.491) | data formatting | bytes 1085440 | tf_op jit(solution)/shard_map/reshape | solution.py:117
  20.9 0.9 tile.65
  21.8 1.2 %reshape.380 = bf16[512,530]{1,0:T(8,128)(2,1)S(1)} reshape(bf16[271360]{0:T(1024)(128)(2,1)S(1)} %slice.492) | data formatting | bytes 1085440 | tf_op jit(solution)/shard_map/reshape | solution.py:117
  23.0 0.4 tile.25
  23.5 0.4 reshape.370
  23.9 0.1 copy.67
  24.0 0.5 fusion.199
  24.7 15.6 %all-gather.2.cloned.1.call-done = bf16[4,1,1,8,32,512]{5,4,3,2,1,0:T(8,128)(2,1)} async-done(((bf16[1,1,1,8,32,512]{5,4,3,2,1,0:T(8,128)(2,1)}), bf16[4,1,1,8,32,512]{5,4,3,2,1,0:T(8,128)(2,1)}) %all-gather.2.cloned.1.call-update) | async-done | bytes 1048592 | tf_op jit(solution)/shard_map/all_gather | solution.py:137
  40.3 1.8 %copy.77 = bf16[4,8,32,512]{3,1,2,0:T(8,128)(2,1)S(1)} copy(bf16[4,8,32,512]{3,2,1,0:T(8,128)(2,1)} %bitcast.104) | data formatting | bytes 2097152
  42.1 0.3 convolution_convert_fusion
  42.4 0.4 convolution_convert_fusion.2
  42.8 1.2 %add_convert_fusion.1 = bf16[8,32,512]{2,1,0:T(8,128)(2,1)S(1)} fusion(bf16[8,32,512]{2,1,0:T(8,128)(2,1)S(1)} %convolution_convert_fusion.2, f32[8]{0:T(128)S(1)} %get-tuple-element.37, f32[8]{0:T(128)S(1)} %get-tuple-element.38, f32[8]{0:T(128)S(1)} %get-tuple-element.39, f32[8]{0:T(128)S(1)} %get-tuple-element.40, f32[8]{0:T(128)S(1)} %get-tuple-element.41, ...), kind=kLoop, calls=%fused_computation.36 | loop fusion | flops 4718592 | bytes 524672 | tf_op jit(solution)/shard_map/convert_element_type | solution.py:154
  44.0 0.1 fusion.222
  44.1 1.9 %collective-permute-start.3 = (bf16[256,9]{1,0:T(8,128)(2,1)S(1)}, bf16[256,9]{1,0:T(8,128)(2,1)}, u32[]{:S(2)}, u32[]{:S(2)}) collective-permute-start(bf16[256,9]{1,0:T(8,128)(2,1)S(1)} %get-tuple-element.56), channel_id=1, source_target_pairs={{0,1},{2,3},{4,5},{6,7},{8,9},{10,11},{12,13},{14,15},{16,17},{18,... | collective-permute-start | bytes 13832 | tf_op jit(solution)/shard_map/ppermute | solution.py:46
  46.0 1.3 %collective-permute-start.4 = (bf16[256,9]{1,0:T(8,128)(2,1)S(1)}, bf16[256,9]{1,0:T(8,128)(2,1)}, u32[]{:S(2)}, u32[]{:S(2)}) collective-permute-start(bf16[256,9]{1,0:T(8,128)(2,1)S(1)} %get-tuple-element.57), channel_id=1, source_target_pairs={{1,0},{3,2},{5,4},{7,6},{9,8},{11,10},{13,12},{15,14},{17,16},{19,... | collective-permute-start | bytes 13832 | tf_op jit(solution)/shard_map/ppermute | solution.py:47
  47.3 3.4 %collective-permute-start.1 = (bf16[9,512]{1,0:T(8,128)(2,1)S(1)}, bf16[9,512]{1,0:T(8,128)(2,1)S(1)}, u32[]{:S(2)}, u32[]{:S(2)}) collective-permute-start(bf16[9,512]{1,0:T(8,128)(2,1)S(1)} %get-tuple-element.54), channel_id=1, source_target_pairs={{0,2},{1,3},{4,6},{5,7},{8,10},{9,11},{12,14},{13,15},{16,18},{17,... | collective-permute-start | bytes 27656 | tf_op jit(solution)/shard_map/ppermute | solution.py:44
  50.7 1.3 %collective-permute-start.6 = (bf16[9,512]{1,0:T(8,128)(2,1)S(1)}, bf16[9,512]{1,0:T(8,128)(2,1)S(1)}, u32[]{:S(2)}, u32[]{:S(2)}) collective-permute-start(bf16[9,512]{1,0:T(8,128)(2,1)S(1)} %get-tuple-element.55), channel_id=1, source_target_pairs={{2,0},{3,1},{6,4},{7,5},{10,8},{11,9},{14,12},{15,13},{18,16},{19,... | collective-permute-start | bytes 27656 | tf_op jit(solution)/shard_map/ppermute | solution.py:45
  52.1 5.3 %collective-permute-start = (bf16[9,9]{1,0:T(8,128)(2,1)S(1)}, bf16[9,9]{1,0:T(8,128)(2,1)S(1)}, u32[]{:S(2)}, u32[]{:S(2)}) collective-permute-start(bf16[9,9]{1,0:T(8,128)(2,1)S(1)} %get-tuple-element.50), channel_id=1, source_target_pairs={{0,3},{4,7},{8,11},{12,15},{16,19},{20,23},{24,27},{28,31}} | collective-permute-start | bytes 494 | tf_op jit(solution)/shard_map/ppermute | solution.py:38
  57.4 0.4 tile.27
  57.8 0.4 reshape.371
  58.3 0.4 collective-permute-done
  58.7 0.8 collective-permute-start.2
  59.6 0.4 tile.29
  60.0 0.4 reshape.372
  60.4 0.7 collective-permute-start.5
  61.1 0.1 copy.68
  61.2 0.1 copy.69
  61.3 1.3 %collective-permute-start.7 = (bf16[9,9]{1,0:T(8,128)(2,1)S(1)}, bf16[9,9]{1,0:T(8,128)(2,1)S(1)}, u32[]{:S(2)}, u32[]{:S(2)}) collective-permute-start(bf16[9,9]{1,0:T(8,128)(2,1)S(1)} %get-tuple-element.51), channel_id=1, source_target_pairs={{3,0},{7,4},{11,8},{15,12},{19,16},{23,20},{27,24},{31,28}} | collective-permute-start | bytes 494 | tf_op jit(solution)/shard_map/ppermute | solution.py:38
  62.6 0.1 copy.70
  62.7 0.1 copy.71
  62.8 3.4 %collective-permute-done.7 = bf16[9,9]{1,0:T(8,128)(2,1)S(1)} collective-permute-done((bf16[9,9]{1,0:T(8,128)(2,1)S(1)}, bf16[9,9]{1,0:T(8,128)(2,1)S(1)}, u32[]{:S(2)}, u32[]{:S(2)}) %collective-permute-start.7) | collective-permute-done | bytes 194 | tf_op jit(solution)/shard_map/ppermute | solution.py:38
  66.2 6.0 %fusion = f32[768,1536]{1,0:T(8,128)} fusion(bf16[530,512]{0,1:T(8,128)(2,1)S(1)} %bitcast.113, bf16[530,512]{0,1:T(8,128)(2,1)S(1)} %bitcast.112, bf16[530,512]{0,1:T(8,128)(2,1)S(1)} %bitcast.111, bf16[256,274]{1,0:T(8,128)(2,1)S(1)} %reshape.372, bf16[256,274]{1,0:T(8,128)(2,1)S(1)} %reshape.371, bf16[256,274]{1,0:T(8,128)(2,1)S(1)} %reshape.370, ...), kind=kOutput, calls=%fused_computation.2 | convolution fusion | flops 1482652928 | bytes 7058056 | tf_op jit(solution)/shard_map/dot_general | solution.py:176
  72.3 3.7 %fusion.218 = (bf16[256,512]{1,0:T(8,128)(2,1)S(1)}, f32[256,512]{1,0:T(8,128)}) fusion(f32[768,1536]{1,0:T(8,128)} %fusion, f32[256]{0:T(256)S(1)} %bitcast.129, f32[512]{0:T(512)S(1)} %bitcast.120, f32[256]{0:T(256)S(1)} %bitcast.130, f32[512]{0:T(512)S(1)} %bitcast.121, f32[256]{0:T(256)S(1)} %bitcast.131, f32[512]{0:T(512)S(1)} %bitcast.122, ...), kind=kLoop, calls=%fused_computation.349 | loop fusion | flops 3670016 | bytes 6056960 | tf_op jit(solution)/shard_map/convert_element_type | solution.py:187
  76.0 0.1 copy.78
  76.2 0.1 concatenate.51
  76.3 1.1 %scatter_custom_fusion = bf16[8,16512]{1,0:T(8,128)(2,1)S(1)} fusion(s32[8]{0:T(128)} %fusion.199, bf16[8,16512]{1,0:T(8,128)(2,1)S(1)} %concatenate.51, bf16[]{:T(256)} %constant.22.clone.1), kind=kCustom, calls=%fused_computation.89 | custom fusion | bytes 264704 | tf_op jit(solution)/shard_map/scatter | solution.py:203
  77.4 0.1 reshape.383
  77.5 11.5 %all_to_all.5 = bf16[4,2,16512]{2,1,0:T(2,128)(2,1)S(1)} all-to-all(bf16[4,2,16512]{2,1,0:T(2,128)(2,1)S(1)} %reshape.383), channel_id=1, replica_groups=mesh['grp'=2,'ccd'=4,'row'=2,'amp'=2] {'ccd'}, dimensions={0} | all-to-all | bytes 528384 | tf_op jit(solution)/shard_map/all_to_all | solution.py:205
  89.0 0.1 reshape.384
  89.2 0.2 add_reduce_fusion
  89.5 0.2 slice_reduce_fusion.29
  89.8 0.1 select_reduce_fusion
  89.9 0.4 slice_reduce_fusion.11
  90.3 0.1 copy.73
  90.4 1.2 %convolution_bitcast_fusion.1 = f32[1,8,32,512]{3,2,1,0:T(8,128)S(1)} fusion(bf16[8,32,512]{2,1,0:T(8,128)(2,1)S(1)} %copy.73, f32[8]{0:T(128)S(1)} %get-tuple-element.25, f32[8]{0:T(128)S(1)} %get-tuple-element.26, f32[8]{0:T(128)S(1)} %get-tuple-element.27, f32[8]{0:T(128)S(1)} %get-tuple-element.28, f32[8]{0:T(128)S(1)} %get-tuple-element.29, ...), kind=kOutput, calls=%fused_computation.10 | convolution fusion | flops 13213696 | bytes 791040 | tf_op jit(solution)/shard_map/qik,qiz->qkz/dot_general | solution.py:224
  91.6 0.7 convolution_bitcast_fusion
  92.3 1.1 %copy.75 = f32[1,1,1,8,32,512]{5,4,3,2,1,0:T(8,128)} copy(f32[1,1,1,8,32,512]{5,3,4,2,1,0:T(8,128)S(1)} %convolution_bitcast_fusion) | data formatting | bytes 1048576
  (49 shorter events, 1.1 us)
Async XLA Ops:
  7.2 33.1 %all-gather.2.cloned.1.call-start = ((), (), s32[]{:S(2)}) async-start(), calls=%async_computation.1 | async-start | bytes 1310720 | tf_op jit(solution)/shard_map/all_gather | solution.py:137
  20.8 3.1 %copy-start.2 = (s32[1,1,1,8,1]{3,4,2,1,0:T(1,128)S(1)}, s32[1,1,1,8,1]{3,4,2,1,0:T(1,128)}, u32[]{:S(2)}) copy-start(s32[1,1,1,8,1]{3,4,2,1,0:T(1,128)} %param.10) | copy-start | bytes 100
  20.9 3.6 %copy-start.1 = (f32[1,3,9]{2,0,1:T(1,128)S(1)}, f32[1,3,9]{2,0,1:T(1,128)}, u32[]{:S(2)}) copy-start(f32[1,3,9]{2,0,1:T(1,128)} %param.14) | copy-start | bytes 328
  44.1 22.1 %collective-permute-start.3 = (bf16[256,9]{1,0:T(8,128)(2,1)S(1)}, bf16[256,9]{1,0:T(8,128)(2,1)}, u32[]{:S(2)}, u32[]{:S(2)}) collective-permute-start(bf16[256,9]{1,0:T(8,128)(2,1)S(1)} %get-tuple-element.56), channel_id=1, source_target_pairs={{0,1},{2,3},{4,5},{6,7},{8,9},{10,11},{12,13},{14,15},{16,17},{18,... | collective-permute-start | bytes 13832 | tf_op jit(solution)/shard_map/ppermute | solution.py:46
  46.0 20.2 %collective-permute-start.4 = (bf16[256,9]{1,0:T(8,128)(2,1)S(1)}, bf16[256,9]{1,0:T(8,128)(2,1)}, u32[]{:S(2)}, u32[]{:S(2)}) collective-permute-start(bf16[256,9]{1,0:T(8,128)(2,1)S(1)} %get-tuple-element.57), channel_id=1, source_target_pairs={{1,0},{3,2},{5,4},{7,6},{9,8},{11,10},{13,12},{15,14},{17,16},{19,... | collective-permute-start | bytes 13832 | tf_op jit(solution)/shard_map/ppermute | solution.py:47
  47.3 18.9 %collective-permute-start.1 = (bf16[9,512]{1,0:T(8,128)(2,1)S(1)}, bf16[9,512]{1,0:T(8,128)(2,1)S(1)}, u32[]{:S(2)}, u32[]{:S(2)}) collective-permute-start(bf16[9,512]{1,0:T(8,128)(2,1)S(1)} %get-tuple-element.54), channel_id=1, source_target_pairs={{0,2},{1,3},{4,6},{5,7},{8,10},{9,11},{12,14},{13,15},{16,18},{17,... | collective-permute-start | bytes 27656 | tf_op jit(solution)/shard_map/ppermute | solution.py:44
  50.7 15.5 %collective-permute-start.6 = (bf16[9,512]{1,0:T(8,128)(2,1)S(1)}, bf16[9,512]{1,0:T(8,128)(2,1)S(1)}, u32[]{:S(2)}, u32[]{:S(2)}) collective-permute-start(bf16[9,512]{1,0:T(8,128)(2,1)S(1)} %get-tuple-element.55), channel_id=1, source_target_pairs={{2,0},{3,1},{6,4},{7,5},{10,8},{11,9},{14,12},{15,13},{18,16},{19,... | collective-permute-start | bytes 27656 | tf_op jit(solution)/shard_map/ppermute | solution.py:45
  52.1 6.6 %collective-permute-start = (bf16[9,9]{1,0:T(8,128)(2,1)S(1)}, bf16[9,9]{1,0:T(8,128)(2,1)S(1)}, u32[]{:S(2)}, u32[]{:S(2)}) collective-permute-start(bf16[9,9]{1,0:T(8,128)(2,1)S(1)} %get-tuple-element.50), channel_id=1, source_target_pairs={{0,3},{4,7},{8,11},{12,15},{16,19},{20,23},{24,27},{28,31}} | collective-permute-start | bytes 494 | tf_op jit(solution)/shard_map/ppermute | solution.py:38
  58.7 1.7 %collective-permute-start.2 = (bf16[9,9]{1,0:T(8,128)(2,1)S(1)}, bf16[9,9]{1,0:T(8,128)(2,1)S(1)}, u32[]{:S(2)}, u32[]{:S(2)}) collective-permute-start(bf16[9,9]{1,0:T(8,128)(2,1)S(1)} %get-tuple-element.53), channel_id=1, source_target_pairs={{1,2},{5,6},{9,10},{13,14},{17,18},{21,22},{25,26},{29,30}} | collective-permute-start | bytes 494 | tf_op jit(solution)/shard_map/ppermute | solution.py:38
  60.4 0.9 collective-permute-start.5
  61.3 4.9 %collective-permute-start.7 = (bf16[9,9]{1,0:T(8,128)(2,1)S(1)}, bf16[9,9]{1,0:T(8,128)(2,1)S(1)}, u32[]{:S(2)}, u32[]{:S(2)}) collective-permute-start(bf16[9,9]{1,0:T(8,128)(2,1)S(1)} %get-tuple-element.51), channel_id=1, source_target_pairs={{3,0},{7,4},{11,8},{15,12},{19,16},{23,20},{27,24},{31,28}} | collective-permute-start | bytes 494 | tf_op jit(solution)/shard_map/ppermute | solution.py:38
  66.2 6.0 %copy-start = (f32[1,256,512]{2,1,0:T(8,128)S(1)}, f32[1,256,512]{2,1,0:T(8,128)}, u32[]{:S(2)}) copy-start(f32[1,256,512]{2,1,0:T(8,128)} %param.8) | copy-start | bytes 1572868
Sparse Core Ops, SparseCore 0:
  9.5 30.6 all-gather.1

commit v6 on v5

--- a/solution.py
+++ b/solution.py
@@ -133,11 +133,19 @@
     same_owner = owner_list[None, :] == owner_list[:, None]
     place_rank = jnp.sum(jnp.where(earlier & same_owner, 1, 0), axis=1).astype(jnp.int32)
     slot_index = owner_list * capacity + place_rank
-    global_index = owner_list * strips + strip_list
-    rows_here = lax.all_gather(template, "ccd", axis=0, tiled=True).reshape(-1, strip_size)
-    labels = jnp.arange(rows_here.shape[0])
-    select = (global_index[:, None] == labels[None, :]).astype(jnp.bfloat16)
-    chosen = jnp.dot(select, rows_here, preferred_element_type=jnp.float32)
+    slot_match = jnp.arange(ccd_count * capacity)[:, None] == slot_index[None, :]
+    wanted = jnp.sum(jnp.where(slot_match, strip_list[None, :] + 1, 0), axis=1) - 1
+    asked = lax.all_to_all(
+        wanted.reshape(ccd_count, capacity), "ccd", split_axis=0, concat_axis=0, tiled=True
+    ).reshape(ccd_count * capacity)
+    own_rows = template.reshape(strips, strip_size)
+    give = (asked[:, None] == jnp.arange(strips)[None, :]).astype(jnp.bfloat16)
+    sending = jnp.dot(give, own_rows, preferred_element_type=jnp.float32).astype(jnp.bfloat16)
+    fetched = lax.all_to_all(
+        sending.reshape(ccd_count, capacity, strip_size), "ccd", split_axis=0, concat_axis=0, tiled=True
+    ).reshape(ccd_count * capacity, strip_size)
+    select = slot_match.astype(jnp.bfloat16)
+    chosen = jnp.dot(select.T, fetched, preferred_element_type=jnp.float32)
     chosen = chosen.astype(jnp.bfloat16)
     chosen = chosen.reshape(strips, strip_rows, half_cols)
     row_taps = lanczos_taps(fractions[0, 0, 0, 0])

time: 101 us -> 93.5 us (0.926)
  waiting for transfers between devices: 20.2 us -> 3.87 us
  between operations: 14.5 us -> 1.38 us
  starting transfers between devices: 16 us -> 26.8 us
  local copies, waits for them, and re-layouts: 16.2 us -> 22.1 us
  other arithmetic: 13.3 us -> 17 us
  blocking collectives: 11.5 us -> 13 us
    all_gather x1 -> x0, waiting for transfers between devices: 15.6 us -> none  [body(): lax.all_gather(template, 'ccd', axis=0, tiled=True).reshape(-1, strip_size)]
    all_to_all x0 -> x2, starting transfers between devices: none -> 11.4 us  [the longest x1 6.35 us: body(): lax.all_to_all(wanted.reshape(ccd_count, capacity), 'ccd', split_axis=0,...]
    concatenate x6, local copies, waits for them, and re-layouts: 0.03 us -> 1.75 us  [band_operator(): line = jnp.concatenate([kernel, jnp.zeros((count,), kernel.dtype)])]
    all_to_all x1, blocking collectives: 11.5 us -> 13 us  [body(): lax.all_to_all(outgoing.reshape(ccd_count, capacity, strip_size + 128), '...]
    unnamed x9 -> x65, local copies, waits for them, and re-layouts: 3.08 us -> 2.48 us
  transfers between devices with their start and end apart: 9 -> 10, of which waited for: 3 -> 2; matrix products, arithmetic and copies ran while one was open for 19% -> 26% of each run, Pallas kernels for 0% -> 0%
where the time goes in v6:
time: 93.5 us; the launch traced here: 92.9 us
  starting transfers between devices  26.8 us (29%)
  local copies, waits for them, and re-layouts  22.1 us (24%)
  other arithmetic  17 us (18%)
  blocking collectives  13 us (14%)
  matrix products  8.8 us (9%)
  waiting for transfers between devices  3.87 us (4%)
  between operations  1.38 us (1%)
    all_to_all x1, blocking collectives, body(): lax.all_to_all(outgoing.reshape(ccd_count, capacity, strip_size + 128), '...  13 us
    ppermute x4, starting transfers between devices, diagonal(): return lax.ppermute(block, ('row', 'amp'), pairs)  8.07 us
    all_to_all x1, starting transfers between devices, body(): lax.all_to_all(wanted.reshape(ccd_count, capacity), 'ccd', split_axis=0,...  6.35 us
    dot_general x1, matrix products, body(): terms = jnp.dot(across_all, column_mats, preferred_element_type=jnp.float32)  5.95 us
    all_to_all x1, starting transfers between devices, body(): lax.all_to_all(sending.reshape(ccd_count, capacity, strip_size), 'ccd', s...  5.09 us
    another operation x12, local copies, waits for them, and re-layouts, band_operator(): flat = jnp.tile(line, count)[:count * width]  4.8 us
    reshape x6, local copies, waits for them, and re-layouts, band_operator(): return flat.reshape(count, width)  4.75 us
    ppermute x4, waiting for transfers between devices, diagonal(): return lax.ppermute(block, ('row', 'amp'), pairs)  3.85 us
  transfers between devices with their start and end apart: 10, of which 2 were waited for; matrix products, arithmetic and copies ran while one was open for 26% of the time, Pallas kernels for 0%

profile of v6, /device:TPU:0, one launch (start us, length us, event | category | flops | bytes accessed | tf_op | source)
XLA Modules:
  0.0 92.9 jit_solution(1130914696386896082)
XLA Ops:
  0.6 0.9 select_reduce_fusion.3
  1.5 0.7 multiply_add_fusion.7
  2.2 1.2 %convert_bitcast_fusion = (bf16[8,1]{0,1:T(2,128)(2,1)}, s32[8]{0:T(128)S(1)}) fusion(s32[1,1,1,8]{3,2,1,0:T(1,128)} %param.11), kind=kLoop, calls=%fused_computation.309 | loop fusion | flops 16 | bytes 80 | tf_op jit(solution)/shard_map/convert_element_type | solution.py:204
  3.6 0.7 sub.142
  4.2 6.3 %all-to-all-start = ((s32[4,1,2]{2,1,0:T(1,128)}), s32[4,1,2]{2,1,0:T(1,128)S(1)}, u32[]{:S(2)}, u32[]{:S(2)}) async-start(s32[4,1,2]{2,1,0:T(1,128)} %bitcast.21), calls=%async_computation | async-start | bytes 4096 | tf_op jit(solution)/shard_map/all_to_all | solution.py:138
  10.6 0.6 iota_subtract_fusion
  11.2 0.6 exponential_reduce_fusion.1
  11.8 0.6 abs_reduce_fusion
  12.4 0.7 exponential_reduce_fusion
  13.1 1.2 %fusion.200 = s32[8]{0:T(128)} fusion(s32[8]{0:T(128)S(1)} %select_reduce_fusion.3, s32[1,1,1,8,1]{3,4,2,1,0:T(1,128)} %param.10), kind=kLoop, calls=%fused_computation.307 | loop fusion | flops 40 | bytes 96 | tf_op jit(solution)/shard_map/select_n | solution.py:211
  14.3 0.8 slice_bitcast_fusion.7
  15.1 0.7 fusion.192
  15.7 0.6 slice_bitcast_fusion.5
  16.3 1.1 %copy.80 = bf16[1,8,32,512]{3,1,2,0:T(8,128)(2,1)S(1)} copy(bf16[1,8,32,512]{3,2,1,0:T(8,128)(2,1)} %bitcast.120) | data formatting | bytes 524288
  17.4 1.4 %convert_bitcast_fusion.1 = (bf16[8,1]{0,1:T(2,128)(2,1)}, bf16[8,1]{0,1:T(2,128)(2,1)}, s32[8]{0:T(128)}, s32[8]{0:T(128)S(1)}) fusion(s32[1,1,1,2,8]{4,3,2,1,0:T(2,128)} %param.12), kind=kLoop, calls=%fused_computation.310 | loop fusion | flops 16 | bytes 160 | tf_op jit(solution)/shard_map/convert_element_type | solution.py:203
  18.8 0.6 convert_bitcast_fusion.5
  19.4 0.6 convert_bitcast_fusion.4
  20.0 0.7 slice_bitcast_fusion.10
  20.8 0.6 fusion.225
  21.7 0.5 broadcast.485
  22.2 0.7 reduce.69
  22.9 0.3 convolution_convert_fusion.1
  23.2 0.9 reshape.404
  24.1 5.1 %all-to-all-start.1 = ((bf16[4,2,16384]{2,1,0:T(2,128)(2,1)}), bf16[4,2,16384]{2,1,0:T(2,128)(2,1)S(1)}, u32[]{:S(2)}, u32[]{:S(2)}) async-start(bf16[4,2,16384]{2,1,0:T(2,128)(2,1)} %reshape.404), calls=%async_computation.1 | async-start | bytes 524288 | tf_op jit(solution)/shard_map/all_to_all | solution.py:144
  29.2 0.7 convert_bitcast_fusion.3
  29.9 0.6 concatenate.39
  30.5 0.6 concatenate.40
  31.1 0.6 concatenate.41
  31.8 0.9 tile.61
  32.8 1.2 %reshape.408 = bf16[512,530]{1,0:T(8,128)(2,1)S(1)} reshape(bf16[271360]{0:T(1024)(128)(2,1)S(1)} %slice.490) | data formatting | bytes 1085440 | tf_op jit(solution)/shard_map/reshape | solution.py:117
  34.0 0.9 tile.63
  34.9 1.2 %reshape.409 = bf16[512,530]{1,0:T(8,128)(2,1)S(1)} reshape(bf16[271360]{0:T(1024)(128)(2,1)S(1)} %slice.491) | data formatting | bytes 1085440 | tf_op jit(solution)/shard_map/reshape | solution.py:117
  36.2 0.9 tile.65
  37.2 1.2 %reshape.410 = bf16[512,530]{1,0:T(8,128)(2,1)S(1)} reshape(bf16[271360]{0:T(1024)(128)(2,1)S(1)} %slice.492) | data formatting | bytes 1085440 | tf_op jit(solution)/shard_map/reshape | solution.py:117
  38.4 0.7 tile.24
  39.1 0.4 tile.25
  39.5 0.4 reshape.399
  39.9 0.4 slice_reduce_fusion.23
  40.4 0.3 convolution_convert_fusion
  40.8 0.4 convolution_convert_fusion.3
  41.2 1.2 %add_convert_fusion.1 = bf16[8,32,512]{2,1,0:T(8,128)(2,1)S(1)} fusion(bf16[8,32,512]{2,1,0:T(8,128)(2,1)S(1)} %convolution_convert_fusion.3, f32[8]{0:T(128)S(1)} %get-tuple-element.37, f32[8]{0:T(128)S(1)} %get-tuple-element.38, f32[8]{0:T(128)S(1)} %get-tuple-element.39, f32[8]{0:T(128)S(1)} %get-tuple-element.40, f32[8]{0:T(128)S(1)} %get-tuple-element.41, ...), kind=kLoop, calls=%fused_computation.37 | loop fusion | flops 4718592 | bytes 524672 | tf_op jit(solution)/shard_map/convert_element_type | solution.py:162
  42.5 1.3 %collective-permute-start.3 = (bf16[256,9]{1,0:T(8,128)(2,1)S(1)}, bf16[256,9]{1,0:T(8,128)(2,1)S(1)}, u32[]{:S(2)}, u32[]{:S(2)}) collective-permute-start(bf16[256,9]{1,0:T(8,128)(2,1)S(1)} %get-tuple-element.56), channel_id=1, source_target_pairs={{0,1},{2,3},{4,5},{6,7},{8,9},{10,11},{12,13},{14,15},{16,17},{18,... | collective-permute-start | bytes 13832 | tf_op jit(solution)/shard_map/ppermute | solution.py:46
  43.9 1.3 %collective-permute-start.4 = (bf16[256,9]{1,0:T(8,128)(2,1)S(1)}, bf16[256,9]{1,0:T(8,128)(2,1)}, u32[]{:S(2)}, u32[]{:S(2)}) collective-permute-start(bf16[256,9]{1,0:T(8,128)(2,1)S(1)} %get-tuple-element.57), channel_id=1, source_target_pairs={{1,0},{3,2},{5,4},{7,6},{9,8},{11,10},{13,12},{15,14},{17,16},{19,... | collective-permute-start | bytes 13832 | tf_op jit(solution)/shard_map/ppermute | solution.py:47
  45.1 3.4 %collective-permute-start.1 = (bf16[9,512]{1,0:T(8,128)(2,1)S(1)}, bf16[9,512]{1,0:T(8,128)(2,1)S(1)}, u32[]{:S(2)}, u32[]{:S(2)}) collective-permute-start(bf16[9,512]{1,0:T(8,128)(2,1)S(1)} %get-tuple-element.54), channel_id=1, source_target_pairs={{0,2},{1,3},{4,6},{5,7},{8,10},{9,11},{12,14},{13,15},{16,18},{17,... | collective-permute-start | bytes 27656 | tf_op jit(solution)/shard_map/ppermute | solution.py:44
  48.6 1.3 %collective-permute-start.6 = (bf16[9,512]{1,0:T(8,128)(2,1)S(1)}, bf16[9,512]{1,0:T(8,128)(2,1)S(1)}, u32[]{:S(2)}, u32[]{:S(2)}) collective-permute-start(bf16[9,512]{1,0:T(8,128)(2,1)S(1)} %get-tuple-element.55), channel_id=1, source_target_pairs={{2,0},{3,1},{6,4},{7,5},{10,8},{11,9},{14,12},{15,13},{18,16},{19,... | collective-permute-start | bytes 27656 | tf_op jit(solution)/shard_map/ppermute | solution.py:45
  49.9 5.3 %collective-permute-start = (bf16[9,9]{1,0:T(8,128)(2,1)S(1)}, bf16[9,9]{1,0:T(8,128)(2,1)S(1)}, u32[]{:S(2)}, u32[]{:S(2)}) collective-permute-start(bf16[9,9]{1,0:T(8,128)(2,1)S(1)} %get-tuple-element.50), channel_id=1, source_target_pairs={{0,3},{4,7},{8,11},{12,15},{16,19},{20,23},{24,27},{28,31}} | collective-permute-start | bytes 494 | tf_op jit(solution)/shard_map/ppermute | solution.py:38
  55.3 0.4 tile.27
  55.7 0.4 reshape.400
  56.1 0.4 collective-permute-done
  56.6 0.8 collective-permute-start.2
  57.4 0.4 tile.29
  57.8 0.4 reshape.401
  58.3 0.7 collective-permute-start.5
  59.2 1.3 %collective-permute-start.7 = (bf16[9,9]{1,0:T(8,128)(2,1)S(1)}, bf16[9,9]{1,0:T(8,128)(2,1)S(1)}, u32[]{:S(2)}, u32[]{:S(2)}) collective-permute-start(bf16[9,9]{1,0:T(8,128)(2,1)S(1)} %get-tuple-element.51), channel_id=1, source_target_pairs={{3,0},{7,4},{11,8},{15,12},{19,16},{23,20},{27,24},{31,28}} | collective-permute-start | bytes 494 | tf_op jit(solution)/shard_map/ppermute | solution.py:38
  60.7 3.4 %collective-permute-done.7 = bf16[9,9]{1,0:T(8,128)(2,1)S(1)} collective-permute-done((bf16[9,9]{1,0:T(8,128)(2,1)S(1)}, bf16[9,9]{1,0:T(8,128)(2,1)S(1)}, u32[]{:S(2)}, u32[]{:S(2)}) %collective-permute-start.7) | collective-permute-done | bytes 194 | tf_op jit(solution)/shard_map/ppermute | solution.py:38
  64.2 6.0 %fusion = f32[768,1536]{1,0:T(8,128)} fusion(bf16[530,512]{0,1:T(8,128)(2,1)S(1)} %bitcast.114, bf16[530,512]{0,1:T(8,128)(2,1)S(1)} %bitcast.113, bf16[530,512]{0,1:T(8,128)(2,1)S(1)} %bitcast.112, bf16[256,274]{1,0:T(8,128)(2,1)S(1)} %reshape.401, bf16[256,274]{1,0:T(8,128)(2,1)S(1)} %reshape.400, bf16[256,274]{1,0:T(8,128)(2,1)S(1)} %reshape.399, ...), kind=kOutput, calls=%fused_computation.3 | convolution fusion | flops 1482652928 | bytes 7058056 | tf_op jit(solution)/shard_map/dot_general | solution.py:184
  70.2 3.7 %fusion.219 = (bf16[256,512]{1,0:T(8,128)(2,1)S(1)}, f32[256,512]{1,0:T(8,128)}) fusion(f32[768,1536]{1,0:T(8,128)} %fusion, f32[256]{0:T(256)S(1)} %bitcast.131, f32[512]{0:T(512)S(1)} %bitcast.122, f32[256]{0:T(256)S(1)} %bitcast.132, f32[512]{0:T(512)S(1)} %bitcast.123, f32[256]{0:T(256)S(1)} %bitcast.133, f32[512]{0:T(512)S(1)} %bitcast.124, ...), kind=kLoop, calls=%fused_computation.355 | loop fusion | flops 3670016 | bytes 6056960 | tf_op jit(solution)/shard_map/convert_element_type | solution.py:195
  74.3 1.1 %scatter_custom_fusion = bf16[8,16512]{1,0:T(8,128)(2,1)S(1)} fusion(s32[8]{0:T(128)} %fusion.200, bf16[8,16512]{1,0:T(8,128)(2,1)S(1)} %concatenate.51, bf16[]{:T(256)} %constant.22.clone.1), kind=kCustom, calls=%fused_computation.90 | custom fusion | bytes 264704 | tf_op jit(solution)/shard_map/scatter | solution.py:211
  75.5 13.0 %all_to_all.16 = bf16[4,2,16512]{2,1,0:T(2,128)(2,1)S(1)} all-to-all(bf16[4,2,16512]{2,1,0:T(2,128)(2,1)S(1)} %reshape.413), channel_id=1, replica_groups=mesh['grp'=2,'ccd'=4,'row'=2,'amp'=2] {'ccd'}, dimensions={0} | all-to-all | bytes 528384 | tf_op jit(solution)/shard_map/all_to_all | solution.py:213
  88.7 0.2 add_reduce_fusion
  89.4 0.4 slice_reduce_fusion.11
  89.9 1.2 %convolution_bitcast_fusion.1 = f32[1,8,32,512]{3,2,1,0:T(8,128)S(1)} fusion(bf16[8,32,512]{2,1,0:T(8,128)(2,1)S(1)} %copy.76, f32[8]{0:T(128)S(1)} %get-tuple-element.25, f32[8]{0:T(128)S(1)} %get-tuple-element.26, f32[8]{0:T(128)S(1)} %get-tuple-element.27, f32[8]{0:T(128)S(1)} %get-tuple-element.28, f32[8]{0:T(128)S(1)} %get-tuple-element.29, ...), kind=kOutput, calls=%fused_computation.11 | convolution fusion | flops 13213696 | bytes 791040 | tf_op jit(solution)/shard_map/qik,qiz->qkz/dot_general | solution.py:232
  91.1 0.7 convolution_bitcast_fusion
  91.8 1.1 %copy.78 = f32[1,1,1,8,32,512]{5,4,3,2,1,0:T(8,128)} copy(f32[1,1,1,8,32,512]{5,3,4,2,1,0:T(8,128)S(1)} %convolution_bitcast_fusion) | data formatting | bytes 1048576
  (115 shorter events, 2.9 us)
Async XLA Ops:
  2.2 1.2 %copy-start.21 = (s32[8]{0:T(128)}, s32[8]{0:T(128)S(1)}, u32[]{:S(2)}) copy-start(s32[8]{0:T(128)S(1)} %multiply_add_fusion.7) | copy-start | bytes 100
  4.2 17.4 %all-to-all-start = ((s32[4,1,2]{2,1,0:T(1,128)}), s32[4,1,2]{2,1,0:T(1,128)S(1)}, u32[]{:S(2)}, u32[]{:S(2)}) async-start(s32[4,1,2]{2,1,0:T(1,128)} %bitcast.21), calls=%async_computation | async-start | bytes 4096 | tf_op jit(solution)/shard_map/all_to_all | solution.py:138
  11.2 12.9 %copy-start.17 = (s32[6]{0:T(128)}, s32[6]{0:T(128)S(1)}, u32[]{:S(2)}) copy-start(s32[6]{0:T(128)S(1)} %iota_add_fusion) | copy-start | bytes 76
  11.2 12.9 %copy-start.15 = (s32[12]{0:T(128)}, s32[12]{0:T(128)S(1)}, u32[]{:S(2)}) copy-start(s32[12]{0:T(128)S(1)} %iota_add_fusion.1) | copy-start | bytes 148
  24.1 16.2 %all-to-all-start.1 = ((bf16[4,2,16384]{2,1,0:T(2,128)(2,1)}), bf16[4,2,16384]{2,1,0:T(2,128)(2,1)S(1)}, u32[]{:S(2)}, u32[]{:S(2)}) async-start(bf16[4,2,16384]{2,1,0:T(2,128)(2,1)} %reshape.404), calls=%async_computation.1 | async-start | bytes 524288 | tf_op jit(solution)/shard_map/all_to_all | solution.py:144
  37.1 3.3 %copy-start.22 = (s32[8]{0:T(128)S(1)}, s32[8]{0:T(128)}, u32[]{:S(2)}) copy-start(s32[8]{0:T(128)} %copy-done.21) | copy-start | bytes 100
  37.1 3.6 %copy-start.1 = (s32[32,32]{0,1:T(8,128)S(1)}, s32[32,32]{0,1:T(8,128)}, u32[]{:S(2)}) copy-start(s32[32,32]{0,1:T(8,128)} %iota_subtract_fusion) | copy-start | bytes 12292
  37.1 3.6 %copy-start.24 = (bf16[8]{0:T(256)(128)(2,1)S(1)}, bf16[8]{0:T(256)(128)(2,1)}, u32[]{:S(2)}) copy-start(bf16[8]{0:T(256)(128)(2,1)} %get-tuple-element.76) | copy-start | bytes 52
  37.1 3.6 %copy-start.25 = (bf16[8]{0:T(256)(128)(2,1)S(1)}, bf16[8]{0:T(256)(128)(2,1)}, u32[]{:S(2)}) copy-start(bf16[8]{0:T(256)(128)(2,1)} %get-tuple-element.77) | copy-start | bytes 52
  37.2 3.6 %copy-start.26 = (bf16[8]{0:T(256)(128)(2,1)S(1)}, bf16[8]{0:T(256)(128)(2,1)}, u32[]{:S(2)}) copy-start(bf16[8]{0:T(256)(128)(2,1)} %get-tuple-element.78) | copy-start | bytes 52
  37.2 3.6 %copy-start.27 = (bf16[8]{0:T(256)(128)(2,1)S(1)}, bf16[8]{0:T(256)(128)(2,1)}, u32[]{:S(2)}) copy-start(bf16[8]{0:T(256)(128)(2,1)} %get-tuple-element.79) | copy-start | bytes 52
  37.2 3.6 %copy-start.28 = (bf16[8]{0:T(256)(128)(2,1)S(1)}, bf16[8]{0:T(256)(128)(2,1)}, u32[]{:S(2)}) copy-start(bf16[8]{0:T(256)(128)(2,1)} %get-tuple-element.80) | copy-start | bytes 52
  37.2 3.6 %copy-start.29 = (bf16[8]{0:T(256)(128)(2,1)S(1)}, bf16[8]{0:T(256)(128)(2,1)}, u32[]{:S(2)}) copy-start(bf16[8]{0:T(256)(128)(2,1)} %get-tuple-element.81) | copy-start | bytes 52
  37.2 3.6 %copy-start.30 = (s32[8]{0:T(128)S(1)}, s32[8]{0:T(128)}, u32[]{:S(2)}) copy-start(s32[8]{0:T(128)} %get-tuple-element.87) | copy-start | bytes 100
  38.4 16.9 %copy-start.14 = (bf16[275]{0:T(512)(128)(2,1)S(1)}, bf16[275]{0:T(512)(128)(2,1)}, u32[]{:S(2)}) copy-start(bf16[275]{0:T(512)(128)(2,1)} %concatenate.40) | copy-start | bytes 1654
  39.9 17.5 %copy-start.13 = (bf16[275]{0:T(512)(128)(2,1)S(1)}, bf16[275]{0:T(512)(128)(2,1)}, u32[]{:S(2)}) copy-start(bf16[275]{0:T(512)(128)(2,1)} %concatenate.41) | copy-start | bytes 1654
  40.7 18.3 %copy-start.3 = (bf16[8,6]{0,1:T(8,128)(2,1)S(1)}, bf16[8,6]{0,1:T(8,128)(2,1)}, u32[]{:S(2)}) copy-start(bf16[8,6]{0,1:T(8,128)(2,1)} %get-tuple-element.89) | copy-start | bytes 292
  40.7 18.3 %copy-start.20 = (bf16[8,1]{0,1:T(2,128)(2,1)S(1)}, bf16[8,1]{0,1:T(2,128)(2,1)}, u32[]{:S(2)}) copy-start(bf16[8,1]{0,1:T(2,128)(2,1)} %get-tuple-element.86) | copy-start | bytes 52
  40.7 19.7 %copy-start.19 = (bf16[8,1]{0,1:T(2,128)(2,1)S(1)}, bf16[8,1]{0,1:T(2,128)(2,1)}, u32[]{:S(2)}) copy-start(bf16[8,1]{0,1:T(2,128)(2,1)} %get-tuple-element.85) | copy-start | bytes 52
  40.7 19.8 %copy-start.23 = (bf16[8,1]{0,1:T(2,128)(2,1)S(1)}, bf16[8,1]{0,1:T(2,128)(2,1)}, u32[]{:S(2)}) copy-start(bf16[8,1]{0,1:T(2,128)(2,1)} %get-tuple-element.93) | copy-start | bytes 52
  42.5 21.5 %collective-permute-start.3 = (bf16[256,9]{1,0:T(8,128)(2,1)S(1)}, bf16[256,9]{1,0:T(8,128)(2,1)S(1)}, u32[]{:S(2)}, u32[]{:S(2)}) collective-permute-start(bf16[256,9]{1,0:T(8,128)(2,1)S(1)} %get-tuple-element.56), channel_id=1, source_target_pairs={{0,1},{2,3},{4,5},{6,7},{8,9},{10,11},{12,13},{14,15},{16,17},{18,... | collective-permute-start | bytes 13832 | tf_op jit(solution)/shard_map/ppermute | solution.py:46
  43.9 20.2 %collective-permute-start.4 = (bf16[256,9]{1,0:T(8,128)(2,1)S(1)}, bf16[256,9]{1,0:T(8,128)(2,1)}, u32[]{:S(2)}, u32[]{:S(2)}) collective-permute-start(bf16[256,9]{1,0:T(8,128)(2,1)S(1)} %get-tuple-element.57), channel_id=1, source_target_pairs={{1,0},{3,2},{5,4},{7,6},{9,8},{11,10},{13,12},{15,14},{17,16},{19,... | collective-permute-start | bytes 13832 | tf_op jit(solution)/shard_map/ppermute | solution.py:47
  45.1 18.9 %collective-permute-start.1 = (bf16[9,512]{1,0:T(8,128)(2,1)S(1)}, bf16[9,512]{1,0:T(8,128)(2,1)S(1)}, u32[]{:S(2)}, u32[]{:S(2)}) collective-permute-start(bf16[9,512]{1,0:T(8,128)(2,1)S(1)} %get-tuple-element.54), channel_id=1, source_target_pairs={{0,2},{1,3},{4,6},{5,7},{8,10},{9,11},{12,14},{13,15},{16,18},{17,... | collective-permute-start | bytes 27656 | tf_op jit(solution)/shard_map/ppermute | solution.py:44
  48.6 15.5 %collective-permute-start.6 = (bf16[9,512]{1,0:T(8,128)(2,1)S(1)}, bf16[9,512]{1,0:T(8,128)(2,1)S(1)}, u32[]{:S(2)}, u32[]{:S(2)}) collective-permute-start(bf16[9,512]{1,0:T(8,128)(2,1)S(1)} %get-tuple-element.55), channel_id=1, source_target_pairs={{2,0},{3,1},{6,4},{7,5},{10,8},{11,9},{14,12},{15,13},{18,16},{19,... | collective-permute-start | bytes 27656 | tf_op jit(solution)/shard_map/ppermute | solution.py:45
  49.9 6.6 %collective-permute-start = (bf16[9,9]{1,0:T(8,128)(2,1)S(1)}, bf16[9,9]{1,0:T(8,128)(2,1)S(1)}, u32[]{:S(2)}, u32[]{:S(2)}) collective-permute-start(bf16[9,9]{1,0:T(8,128)(2,1)S(1)} %get-tuple-element.50), channel_id=1, source_target_pairs={{0,3},{4,7},{8,11},{12,15},{16,19},{20,23},{24,27},{28,31}} | collective-permute-start | bytes 494 | tf_op jit(solution)/shard_map/ppermute | solution.py:38
  56.6 1.7 %collective-permute-start.2 = (bf16[9,9]{1,0:T(8,128)(2,1)S(1)}, bf16[9,9]{1,0:T(8,128)(2,1)S(1)}, u32[]{:S(2)}, u32[]{:S(2)}) collective-permute-start(bf16[9,9]{1,0:T(8,128)(2,1)S(1)} %get-tuple-element.53), channel_id=1, source_target_pairs={{1,2},{5,6},{9,10},{13,14},{17,18},{21,22},{25,26},{29,30}} | collective-permute-start | bytes 494 | tf_op jit(solution)/shard_map/ppermute | solution.py:38
  58.3 0.9 collective-permute-start.5
  59.2 4.9 %collective-permute-start.7 = (bf16[9,9]{1,0:T(8,128)(2,1)S(1)}, bf16[9,9]{1,0:T(8,128)(2,1)S(1)}, u32[]{:S(2)}, u32[]{:S(2)}) collective-permute-start(bf16[9,9]{1,0:T(8,128)(2,1)S(1)} %get-tuple-element.51), channel_id=1, source_target_pairs={{3,0},{7,4},{11,8},{15,12},{19,16},{23,20},{27,24},{31,28}} | collective-permute-start | bytes 494 | tf_op jit(solution)/shard_map/ppermute | solution.py:38
  64.1 6.1 %copy-start = (f32[1,256,512]{2,1,0:T(8,128)S(1)}, f32[1,256,512]{2,1,0:T(8,128)}, u32[]{:S(2)}) copy-start(f32[1,256,512]{2,1,0:T(8,128)} %param.8) | copy-start | bytes 1572868
  64.1 6.0 %copy-start.4 = (f32[1,256]{1,0:T(1,128)S(1)}, f32[1,256]{1,0:T(1,128)}, u32[]{:S(2)}) copy-start(f32[1,256]{1,0:T(1,128)} %get-tuple-element.67) | copy-start | bytes 3076
  64.1 6.0 %copy-start.5 = (f32[1,256]{1,0:T(1,128)S(1)}, f32[1,256]{1,0:T(1,128)}, u32[]{:S(2)}) copy-start(f32[1,256]{1,0:T(1,128)} %get-tuple-element.68) | copy-start | bytes 3076
  64.1 6.0 %copy-start.6 = (f32[1,256]{1,0:T(1,128)S(1)}, f32[1,256]{1,0:T(1,128)}, u32[]{:S(2)}) copy-start(f32[1,256]{1,0:T(1,128)} %get-tuple-element.69) | copy-start | bytes 3076
  64.1 6.0 %copy-start.7 = (f32[1,256]{1,0:T(1,128)S(1)}, f32[1,256]{1,0:T(1,128)}, u32[]{:S(2)}) copy-start(f32[1,256]{1,0:T(1,128)} %get-tuple-element.70) | copy-start | bytes 3076
  64.2 6.0 %copy-start.8 = (f32[1,256]{1,0:T(1,128)S(1)}, f32[1,256]{1,0:T(1,128)}, u32[]{:S(2)}) copy-start(f32[1,256]{1,0:T(1,128)} %get-tuple-element.71) | copy-start | bytes 3076
  64.2 6.0 %copy-start.9 = (f32[1,256]{1,0:T(1,128)S(1)}, f32[1,256]{1,0:T(1,128)}, u32[]{:S(2)}) copy-start(f32[1,256]{1,0:T(1,128)} %get-tuple-element.72) | copy-start | bytes 3076
  64.2 6.0 %copy-start.10 = (f32[1,256]{1,0:T(1,128)S(1)}, f32[1,256]{1,0:T(1,128)}, u32[]{:S(2)}) copy-start(f32[1,256]{1,0:T(1,128)} %get-tuple-element.73) | copy-start | bytes 3076
  64.2 6.0 %copy-start.11 = (f32[1,256]{1,0:T(1,128)S(1)}, f32[1,256]{1,0:T(1,128)}, u32[]{:S(2)}) copy-start(f32[1,256]{1,0:T(1,128)} %get-tuple-element.74) | copy-start | bytes 3076
  64.2 6.0 %copy-start.12 = (f32[1,256]{1,0:T(1,128)S(1)}, f32[1,256]{1,0:T(1,128)}, u32[]{:S(2)}) copy-start(f32[1,256]{1,0:T(1,128)} %get-tuple-element.75) | copy-start | bytes 3076
  74.0 15.3 %copy-start.18 = (s32[6]{0:T(128)S(1)}, s32[6]{0:T(128)}, u32[]{:S(2)}) copy-start(s32[6]{0:T(128)} %copy-done.17) | copy-start | bytes 76
  74.0 15.3 %copy-start.16 = (s32[12]{0:T(128)S(1)}, s32[12]{0:T(128)}, u32[]{:S(2)}) copy-start(s32[12]{0:T(128)} %copy-done.15) | copy-start | bytes 148
  74.0 15.9 %copy-start.2 = (s32[32,32]{0,1:T(8,128)S(1)}, s32[32,32]{0,1:T(8,128)}, u32[]{:S(2)}) copy-start(s32[32,32]{0,1:T(8,128)} %iota_subtract_fusion) | copy-start | bytes 12292

commit v7 on v6

--- a/solution.py
+++ b/solution.py
@@ -157,7 +157,6 @@
     rows_done = jnp.einsum(
         "qik,qkz->qiz", row_warp, chosen, preferred_element_type=jnp.float32
     ).astype(jnp.bfloat16)
-    rows_done = lax.optimization_barrier(rows_done)
     col_weights = shift_weights(col_taps, col_shift)
     warped = static_shift(rows_done, col_weights, 1, half_cols).astype(jnp.bfloat16)
     image = warped.reshape(band_rows, half_cols)

time: 93.5 us -> 93.5 us (level)
  no operation moved by 1% of the time
where the time goes in v7:
time: 93.5 us; the launch traced here: 92.9 us
  starting transfers between devices  26.8 us (29%)
  local copies, waits for them, and re-layouts  22.1 us (24%)
  other arithmetic  17 us (18%)
  blocking collectives  13 us (14%)
  matrix products  8.8 us (9%)
  waiting for transfers between devices  3.87 us (4%)
  between operations  1.38 us (1%)
    all_to_all x1, blocking collectives, body(): lax.all_to_all(outgoing.reshape(ccd_count, capacity, strip_size + 128), '...  13 us
    ppermute x4, starting transfers between devices, diagonal(): return lax.ppermute(block, ('row', 'amp'), pairs)  8.07 us
    all_to_all x1, starting transfers between devices, body(): lax.all_to_all(wanted.reshape(ccd_count, capacity), 'ccd', split_axis=0,...  6.35 us
    dot_general x1, matrix products, body(): terms = jnp.dot(across_all, column_mats, preferred_element_type=jnp.float32)  5.95 us
    all_to_all x1, starting transfers between devices, body(): lax.all_to_all(sending.reshape(ccd_count, capacity, strip_size), 'ccd', s...  5.09 us
    another operation x12, local copies, waits for them, and re-layouts, band_operator(): flat = jnp.tile(line, count)[:count * width]  4.8 us
    reshape x6, local copies, waits for them, and re-layouts, band_operator(): return flat.reshape(count, width)  4.75 us
    ppermute x4, waiting for transfers between devices, diagonal(): return lax.ppermute(block, ('row', 'amp'), pairs)  3.85 us
  transfers between devices with their start and end apart: 10, of which 2 were waited for; matrix products, arithmetic and copies ran while one was open for 26% of the time, Pallas kernels for 0%

profile of v7, /device:TPU:0, one launch (start us, length us, event | category | flops | bytes accessed | tf_op | source)
XLA Modules:
  0.0 92.9 jit_solution(1130914696386896082)
XLA Ops:
  0.6 0.9 select_reduce_fusion.3
  1.5 0.7 multiply_add_fusion.7
  2.2 1.2 %convert_bitcast_fusion = (bf16[8,1]{0,1:T(2,128)(2,1)}, s32[8]{0:T(128)S(1)}) fusion(s32[1,1,1,8]{3,2,1,0:T(1,128)} %param.11), kind=kLoop, calls=%fused_computation.309 | loop fusion | flops 16 | bytes 80 | tf_op jit(solution)/shard_map/convert_element_type | solution.py:203
  3.6 0.7 sub.142
  4.2 6.3 %all-to-all-start = ((s32[4,1,2]{2,1,0:T(1,128)}), s32[4,1,2]{2,1,0:T(1,128)S(1)}, u32[]{:S(2)}, u32[]{:S(2)}) async-start(s32[4,1,2]{2,1,0:T(1,128)} %bitcast.21), calls=%async_computation | async-start | bytes 4096 | tf_op jit(solution)/shard_map/all_to_all | solution.py:138
  10.6 0.6 iota_subtract_fusion
  11.2 0.6 exponential_reduce_fusion.1
  11.8 0.6 abs_reduce_fusion
  12.4 0.7 exponential_reduce_fusion
  13.1 1.2 %fusion.200 = s32[8]{0:T(128)} fusion(s32[8]{0:T(128)S(1)} %select_reduce_fusion.3, s32[1,1,1,8,1]{3,4,2,1,0:T(1,128)} %param.10), kind=kLoop, calls=%fused_computation.307 | loop fusion | flops 40 | bytes 96 | tf_op jit(solution)/shard_map/select_n | solution.py:210
  14.3 0.8 slice_bitcast_fusion.7
  15.1 0.7 fusion.192
  15.7 0.6 slice_bitcast_fusion.5
  16.3 1.1 %copy.80 = bf16[1,8,32,512]{3,1,2,0:T(8,128)(2,1)S(1)} copy(bf16[1,8,32,512]{3,2,1,0:T(8,128)(2,1)} %bitcast.120) | data formatting | bytes 524288
  17.4 1.4 %convert_bitcast_fusion.1 = (bf16[8,1]{0,1:T(2,128)(2,1)}, bf16[8,1]{0,1:T(2,128)(2,1)}, s32[8]{0:T(128)}, s32[8]{0:T(128)S(1)}) fusion(s32[1,1,1,2,8]{4,3,2,1,0:T(2,128)} %param.12), kind=kLoop, calls=%fused_computation.310 | loop fusion | flops 16 | bytes 160 | tf_op jit(solution)/shard_map/convert_element_type | solution.py:202
  18.8 0.6 convert_bitcast_fusion.5
  19.4 0.6 convert_bitcast_fusion.4
  20.0 0.7 slice_bitcast_fusion.10
  20.8 0.6 fusion.225
  21.7 0.5 broadcast.485
  22.2 0.7 reduce.69
  22.9 0.3 convolution_convert_fusion.1
  23.2 0.9 reshape.404
  24.1 5.1 %all-to-all-start.1 = ((bf16[4,2,16384]{2,1,0:T(2,128)(2,1)}), bf16[4,2,16384]{2,1,0:T(2,128)(2,1)S(1)}, u32[]{:S(2)}, u32[]{:S(2)}) async-start(bf16[4,2,16384]{2,1,0:T(2,128)(2,1)} %reshape.404), calls=%async_computation.1 | async-start | bytes 524288 | tf_op jit(solution)/shard_map/all_to_all | solution.py:144
  29.2 0.7 convert_bitcast_fusion.3
  29.9 0.6 concatenate.39
  30.5 0.6 concatenate.40
  31.1 0.6 concatenate.41
  31.8 0.9 tile.61
  32.8 1.2 %reshape.408 = bf16[512,530]{1,0:T(8,128)(2,1)S(1)} reshape(bf16[271360]{0:T(1024)(128)(2,1)S(1)} %slice.490) | data formatting | bytes 1085440 | tf_op jit(solution)/shard_map/reshape | solution.py:117
  34.0 0.9 tile.63
  34.9 1.2 %reshape.409 = bf16[512,530]{1,0:T(8,128)(2,1)S(1)} reshape(bf16[271360]{0:T(1024)(128)(2,1)S(1)} %slice.491) | data formatting | bytes 1085440 | tf_op jit(solution)/shard_map/reshape | solution.py:117
  36.2 0.9 tile.65
  37.2 1.2 %reshape.410 = bf16[512,530]{1,0:T(8,128)(2,1)S(1)} reshape(bf16[271360]{0:T(1024)(128)(2,1)S(1)} %slice.492) | data formatting | bytes 1085440 | tf_op jit(solution)/shard_map/reshape | solution.py:117
  38.4 0.7 tile.24
  39.1 0.4 tile.25
  39.5 0.4 reshape.399
  39.9 0.4 slice_reduce_fusion.23
  40.4 0.3 convolution_convert_fusion
  40.8 0.4 convolution_convert_fusion.3
  41.2 1.2 %add_convert_fusion.1 = bf16[8,32,512]{2,1,0:T(8,128)(2,1)S(1)} fusion(bf16[8,32,512]{2,1,0:T(8,128)(2,1)S(1)} %convolution_convert_fusion.3, f32[8]{0:T(128)S(1)} %get-tuple-element.37, f32[8]{0:T(128)S(1)} %get-tuple-element.38, f32[8]{0:T(128)S(1)} %get-tuple-element.39, f32[8]{0:T(128)S(1)} %get-tuple-element.40, f32[8]{0:T(128)S(1)} %get-tuple-element.41, ...), kind=kLoop, calls=%fused_computation.37 | loop fusion | flops 4718592 | bytes 524672 | tf_op jit(solution)/shard_map/convert_element_type | solution.py:161
  42.5 1.3 %collective-permute-start.3 = (bf16[256,9]{1,0:T(8,128)(2,1)S(1)}, bf16[256,9]{1,0:T(8,128)(2,1)S(1)}, u32[]{:S(2)}, u32[]{:S(2)}) collective-permute-start(bf16[256,9]{1,0:T(8,128)(2,1)S(1)} %get-tuple-element.56), channel_id=1, source_target_pairs={{0,1},{2,3},{4,5},{6,7},{8,9},{10,11},{12,13},{14,15},{16,17},{18,... | collective-permute-start | bytes 13832 | tf_op jit(solution)/shard_map/ppermute | solution.py:46
  43.9 1.3 %collective-permute-start.4 = (bf16[256,9]{1,0:T(8,128)(2,1)S(1)}, bf16[256,9]{1,0:T(8,128)(2,1)}, u32[]{:S(2)}, u32[]{:S(2)}) collective-permute-start(bf16[256,9]{1,0:T(8,128)(2,1)S(1)} %get-tuple-element.57), channel_id=1, source_target_pairs={{1,0},{3,2},{5,4},{7,6},{9,8},{11,10},{13,12},{15,14},{17,16},{19,... | collective-permute-start | bytes 13832 | tf_op jit(solution)/shard_map/ppermute | solution.py:47
  45.1 3.4 %collective-permute-start.1 = (bf16[9,512]{1,0:T(8,128)(2,1)S(1)}, bf16[9,512]{1,0:T(8,128)(2,1)S(1)}, u32[]{:S(2)}, u32[]{:S(2)}) collective-permute-start(bf16[9,512]{1,0:T(8,128)(2,1)S(1)} %get-tuple-element.54), channel_id=1, source_target_pairs={{0,2},{1,3},{4,6},{5,7},{8,10},{9,11},{12,14},{13,15},{16,18},{17,... | collective-permute-start | bytes 27656 | tf_op jit(solution)/shard_map/ppermute | solution.py:44
  48.6 1.3 %collective-permute-start.6 = (bf16[9,512]{1,0:T(8,128)(2,1)S(1)}, bf16[9,512]{1,0:T(8,128)(2,1)S(1)}, u32[]{:S(2)}, u32[]{:S(2)}) collective-permute-start(bf16[9,512]{1,0:T(8,128)(2,1)S(1)} %get-tuple-element.55), channel_id=1, source_target_pairs={{2,0},{3,1},{6,4},{7,5},{10,8},{11,9},{14,12},{15,13},{18,16},{19,... | collective-permute-start | bytes 27656 | tf_op jit(solution)/shard_map/ppermute | solution.py:45
  49.9 5.3 %collective-permute-start = (bf16[9,9]{1,0:T(8,128)(2,1)S(1)}, bf16[9,9]{1,0:T(8,128)(2,1)S(1)}, u32[]{:S(2)}, u32[]{:S(2)}) collective-permute-start(bf16[9,9]{1,0:T(8,128)(2,1)S(1)} %get-tuple-element.50), channel_id=1, source_target_pairs={{0,3},{4,7},{8,11},{12,15},{16,19},{20,23},{24,27},{28,31}} | collective-permute-start | bytes 494 | tf_op jit(solution)/shard_map/ppermute | solution.py:38
  55.3 0.4 tile.27
  55.7 0.4 reshape.400
  56.1 0.4 collective-permute-done
  56.6 0.8 collective-permute-start.2
  57.4 0.4 tile.29
  57.8 0.4 reshape.401
  58.3 0.7 collective-permute-start.5
  59.2 1.3 %collective-permute-start.7 = (bf16[9,9]{1,0:T(8,128)(2,1)S(1)}, bf16[9,9]{1,0:T(8,128)(2,1)S(1)}, u32[]{:S(2)}, u32[]{:S(2)}) collective-permute-start(bf16[9,9]{1,0:T(8,128)(2,1)S(1)} %get-tuple-element.51), channel_id=1, source_target_pairs={{3,0},{7,4},{11,8},{15,12},{19,16},{23,20},{27,24},{31,28}} | collective-permute-start | bytes 494 | tf_op jit(solution)/shard_map/ppermute | solution.py:38
  60.7 3.4 %collective-permute-done.7 = bf16[9,9]{1,0:T(8,128)(2,1)S(1)} collective-permute-done((bf16[9,9]{1,0:T(8,128)(2,1)S(1)}, bf16[9,9]{1,0:T(8,128)(2,1)S(1)}, u32[]{:S(2)}, u32[]{:S(2)}) %collective-permute-start.7) | collective-permute-done | bytes 194 | tf_op jit(solution)/shard_map/ppermute | solution.py:38
  64.2 6.0 %fusion = f32[768,1536]{1,0:T(8,128)} fusion(bf16[530,512]{0,1:T(8,128)(2,1)S(1)} %bitcast.114, bf16[530,512]{0,1:T(8,128)(2,1)S(1)} %bitcast.113, bf16[530,512]{0,1:T(8,128)(2,1)S(1)} %bitcast.112, bf16[256,274]{1,0:T(8,128)(2,1)S(1)} %reshape.401, bf16[256,274]{1,0:T(8,128)(2,1)S(1)} %reshape.400, bf16[256,274]{1,0:T(8,128)(2,1)S(1)} %reshape.399, ...), kind=kOutput, calls=%fused_computation.3 | convolution fusion | flops 1482652928 | bytes 7058056 | tf_op jit(solution)/shard_map/dot_general | solution.py:183
  70.2 3.7 %fusion.219 = (bf16[256,512]{1,0:T(8,128)(2,1)S(1)}, f32[256,512]{1,0:T(8,128)}) fusion(f32[768,1536]{1,0:T(8,128)} %fusion, f32[256]{0:T(256)S(1)} %bitcast.131, f32[512]{0:T(512)S(1)} %bitcast.122, f32[256]{0:T(256)S(1)} %bitcast.132, f32[512]{0:T(512)S(1)} %bitcast.123, f32[256]{0:T(256)S(1)} %bitcast.133, f32[512]{0:T(512)S(1)} %bitcast.124, ...), kind=kLoop, calls=%fused_computation.355 | loop fusion | flops 3670016 | bytes 6056960 | tf_op jit(solution)/shard_map/convert_element_type | solution.py:194
  74.3 1.1 %scatter_custom_fusion = bf16[8,16512]{1,0:T(8,128)(2,1)S(1)} fusion(s32[8]{0:T(128)} %fusion.200, bf16[8,16512]{1,0:T(8,128)(2,1)S(1)} %concatenate.51, bf16[]{:T(256)} %constant.22.clone.1), kind=kCustom, calls=%fused_computation.90 | custom fusion | bytes 264704 | tf_op jit(solution)/shard_map/scatter | solution.py:210
  75.5 13.0 %all_to_all.16 = bf16[4,2,16512]{2,1,0:T(2,128)(2,1)S(1)} all-to-all(bf16[4,2,16512]{2,1,0:T(2,128)(2,1)S(1)} %reshape.413), channel_id=1, replica_groups=mesh['grp'=2,'ccd'=4,'row'=2,'amp'=2] {'ccd'}, dimensions={0} | all-to-all | bytes 528384 | tf_op jit(solution)/shard_map/all_to_all | solution.py:212
  88.7 0.2 add_reduce_fusion
  89.4 0.4 slice_reduce_fusion.11
  89.9 1.2 %convolution_bitcast_fusion.1 = f32[1,8,32,512]{3,2,1,0:T(8,128)S(1)} fusion(bf16[8,32,512]{2,1,0:T(8,128)(2,1)S(1)} %copy.76, f32[8]{0:T(128)S(1)} %get-tuple-element.25, f32[8]{0:T(128)S(1)} %get-tuple-element.26, f32[8]{0:T(128)S(1)} %get-tuple-element.27, f32[8]{0:T(128)S(1)} %get-tuple-element.28, f32[8]{0:T(128)S(1)} %get-tuple-element.29, ...), kind=kOutput, calls=%fused_computation.11 | convolution fusion | flops 13213696 | bytes 791040 | tf_op jit(solution)/shard_map/qik,qiz->qkz/dot_general | solution.py:231
  91.1 0.7 convolution_bitcast_fusion
  91.8 1.1 %copy.78 = f32[1,1,1,8,32,512]{5,4,3,2,1,0:T(8,128)} copy(f32[1,1,1,8,32,512]{5,3,4,2,1,0:T(8,128)S(1)} %convolution_bitcast_fusion) | data formatting | bytes 1048576
  (115 shorter events, 2.9 us)
Async XLA Ops:
  2.2 1.2 %copy-start.21 = (s32[8]{0:T(128)}, s32[8]{0:T(128)S(1)}, u32[]{:S(2)}) copy-start(s32[8]{0:T(128)S(1)} %multiply_add_fusion.7) | copy-start | bytes 100
  4.2 17.4 %all-to-all-start = ((s32[4,1,2]{2,1,0:T(1,128)}), s32[4,1,2]{2,1,0:T(1,128)S(1)}, u32[]{:S(2)}, u32[]{:S(2)}) async-start(s32[4,1,2]{2,1,0:T(1,128)} %bitcast.21), calls=%async_computation | async-start | bytes 4096 | tf_op jit(solution)/shard_map/all_to_all | solution.py:138
  11.2 12.9 %copy-start.17 = (s32[6]{0:T(128)}, s32[6]{0:T(128)S(1)}, u32[]{:S(2)}) copy-start(s32[6]{0:T(128)S(1)} %iota_add_fusion) | copy-start | bytes 76
  11.2 12.9 %copy-start.15 = (s32[12]{0:T(128)}, s32[12]{0:T(128)S(1)}, u32[]{:S(2)}) copy-start(s32[12]{0:T(128)S(1)} %iota_add_fusion.1) | copy-start | bytes 148
  24.1 16.2 %all-to-all-start.1 = ((bf16[4,2,16384]{2,1,0:T(2,128)(2,1)}), bf16[4,2,16384]{2,1,0:T(2,128)(2,1)S(1)}, u32[]{:S(2)}, u32[]{:S(2)}) async-start(bf16[4,2,16384]{2,1,0:T(2,128)(2,1)} %reshape.404), calls=%async_computation.1 | async-start | bytes 524288 | tf_op jit(solution)/shard_map/all_to_all | solution.py:144
  37.1 3.3 %copy-start.22 = (s32[8]{0:T(128)S(1)}, s32[8]{0:T(128)}, u32[]{:S(2)}) copy-start(s32[8]{0:T(128)} %copy-done.21) | copy-start | bytes 100
  37.1 3.6 %copy-start.1 = (s32[32,32]{0,1:T(8,128)S(1)}, s32[32,32]{0,1:T(8,128)}, u32[]{:S(2)}) copy-start(s32[32,32]{0,1:T(8,128)} %iota_subtract_fusion) | copy-start | bytes 12292
  37.1 3.6 %copy-start.24 = (bf16[8]{0:T(256)(128)(2,1)S(1)}, bf16[8]{0:T(256)(128)(2,1)}, u32[]{:S(2)}) copy-start(bf16[8]{0:T(256)(128)(2,1)} %get-tuple-element.76) | copy-start | bytes 52
  37.1 3.6 %copy-start.25 = (bf16[8]{0:T(256)(128)(2,1)S(1)}, bf16[8]{0:T(256)(128)(2,1)}, u32[]{:S(2)}) copy-start(bf16[8]{0:T(256)(128)(2,1)} %get-tuple-element.77) | copy-start | bytes 52
  37.2 3.6 %copy-start.26 = (bf16[8]{0:T(256)(128)(2,1)S(1)}, bf16[8]{0:T(256)(128)(2,1)}, u32[]{:S(2)}) copy-start(bf16[8]{0:T(256)(128)(2,1)} %get-tuple-element.78) | copy-start | bytes 52
  37.2 3.6 %copy-start.27 = (bf16[8]{0:T(256)(128)(2,1)S(1)}, bf16[8]{0:T(256)(128)(2,1)}, u32[]{:S(2)}) copy-start(bf16[8]{0:T(256)(128)(2,1)} %get-tuple-element.79) | copy-start | bytes 52
  37.2 3.6 %copy-start.28 = (bf16[8]{0:T(256)(128)(2,1)S(1)}, bf16[8]{0:T(256)(128)(2,1)}, u32[]{:S(2)}) copy-start(bf16[8]{0:T(256)(128)(2,1)} %get-tuple-element.80) | copy-start | bytes 52
  37.2 3.6 %copy-start.29 = (bf16[8]{0:T(256)(128)(2,1)S(1)}, bf16[8]{0:T(256)(128)(2,1)}, u32[]{:S(2)}) copy-start(bf16[8]{0:T(256)(128)(2,1)} %get-tuple-element.81) | copy-start | bytes 52
  37.2 3.6 %copy-start.30 = (s32[8]{0:T(128)S(1)}, s32[8]{0:T(128)}, u32[]{:S(2)}) copy-start(s32[8]{0:T(128)} %get-tuple-element.87) | copy-start | bytes 100
  38.4 16.9 %copy-start.14 = (bf16[275]{0:T(512)(128)(2,1)S(1)}, bf16[275]{0:T(512)(128)(2,1)}, u32[]{:S(2)}) copy-start(bf16[275]{0:T(512)(128)(2,1)} %concatenate.40) | copy-start | bytes 1654
  39.9 17.5 %copy-start.13 = (bf16[275]{0:T(512)(128)(2,1)S(1)}, bf16[275]{0:T(512)(128)(2,1)}, u32[]{:S(2)}) copy-start(bf16[275]{0:T(512)(128)(2,1)} %concatenate.41) | copy-start | bytes 1654
  40.7 18.3 %copy-start.3 = (bf16[8,6]{0,1:T(8,128)(2,1)S(1)}, bf16[8,6]{0,1:T(8,128)(2,1)}, u32[]{:S(2)}) copy-start(bf16[8,6]{0,1:T(8,128)(2,1)} %get-tuple-element.89) | copy-start | bytes 292
  40.7 18.3 %copy-start.20 = (bf16[8,1]{0,1:T(2,128)(2,1)S(1)}, bf16[8,1]{0,1:T(2,128)(2,1)}, u32[]{:S(2)}) copy-start(bf16[8,1]{0,1:T(2,128)(2,1)} %get-tuple-element.86) | copy-start | bytes 52
  40.7 19.7 %copy-start.19 = (bf16[8,1]{0,1:T(2,128)(2,1)S(1)}, bf16[8,1]{0,1:T(2,128)(2,1)}, u32[]{:S(2)}) copy-start(bf16[8,1]{0,1:T(2,128)(2,1)} %get-tuple-element.85) | copy-start | bytes 52
  40.7 19.8 %copy-start.23 = (bf16[8,1]{0,1:T(2,128)(2,1)S(1)}, bf16[8,1]{0,1:T(2,128)(2,1)}, u32[]{:S(2)}) copy-start(bf16[8,1]{0,1:T(2,128)(2,1)} %get-tuple-element.93) | copy-start | bytes 52
  42.5 21.5 %collective-permute-start.3 = (bf16[256,9]{1,0:T(8,128)(2,1)S(1)}, bf16[256,9]{1,0:T(8,128)(2,1)S(1)}, u32[]{:S(2)}, u32[]{:S(2)}) collective-permute-start(bf16[256,9]{1,0:T(8,128)(2,1)S(1)} %get-tuple-element.56), channel_id=1, source_target_pairs={{0,1},{2,3},{4,5},{6,7},{8,9},{10,11},{12,13},{14,15},{16,17},{18,... | collective-permute-start | bytes 13832 | tf_op jit(solution)/shard_map/ppermute | solution.py:46
  43.9 20.2 %collective-permute-start.4 = (bf16[256,9]{1,0:T(8,128)(2,1)S(1)}, bf16[256,9]{1,0:T(8,128)(2,1)}, u32[]{:S(2)}, u32[]{:S(2)}) collective-permute-start(bf16[256,9]{1,0:T(8,128)(2,1)S(1)} %get-tuple-element.57), channel_id=1, source_target_pairs={{1,0},{3,2},{5,4},{7,6},{9,8},{11,10},{13,12},{15,14},{17,16},{19,... | collective-permute-start | bytes 13832 | tf_op jit(solution)/shard_map/ppermute | solution.py:47
  45.1 18.9 %collective-permute-start.1 = (bf16[9,512]{1,0:T(8,128)(2,1)S(1)}, bf16[9,512]{1,0:T(8,128)(2,1)S(1)}, u32[]{:S(2)}, u32[]{:S(2)}) collective-permute-start(bf16[9,512]{1,0:T(8,128)(2,1)S(1)} %get-tuple-element.54), channel_id=1, source_target_pairs={{0,2},{1,3},{4,6},{5,7},{8,10},{9,11},{12,14},{13,15},{16,18},{17,... | collective-permute-start | bytes 27656 | tf_op jit(solution)/shard_map/ppermute | solution.py:44
  48.6 15.5 %collective-permute-start.6 = (bf16[9,512]{1,0:T(8,128)(2,1)S(1)}, bf16[9,512]{1,0:T(8,128)(2,1)S(1)}, u32[]{:S(2)}, u32[]{:S(2)}) collective-permute-start(bf16[9,512]{1,0:T(8,128)(2,1)S(1)} %get-tuple-element.55), channel_id=1, source_target_pairs={{2,0},{3,1},{6,4},{7,5},{10,8},{11,9},{14,12},{15,13},{18,16},{19,... | collective-permute-start | bytes 27656 | tf_op jit(solution)/shard_map/ppermute | solution.py:45
  49.9 6.6 %collective-permute-start = (bf16[9,9]{1,0:T(8,128)(2,1)S(1)}, bf16[9,9]{1,0:T(8,128)(2,1)S(1)}, u32[]{:S(2)}, u32[]{:S(2)}) collective-permute-start(bf16[9,9]{1,0:T(8,128)(2,1)S(1)} %get-tuple-element.50), channel_id=1, source_target_pairs={{0,3},{4,7},{8,11},{12,15},{16,19},{20,23},{24,27},{28,31}} | collective-permute-start | bytes 494 | tf_op jit(solution)/shard_map/ppermute | solution.py:38
  56.6 1.7 %collective-permute-start.2 = (bf16[9,9]{1,0:T(8,128)(2,1)S(1)}, bf16[9,9]{1,0:T(8,128)(2,1)S(1)}, u32[]{:S(2)}, u32[]{:S(2)}) collective-permute-start(bf16[9,9]{1,0:T(8,128)(2,1)S(1)} %get-tuple-element.53), channel_id=1, source_target_pairs={{1,2},{5,6},{9,10},{13,14},{17,18},{21,22},{25,26},{29,30}} | collective-permute-start | bytes 494 | tf_op jit(solution)/shard_map/ppermute | solution.py:38
  58.3 0.9 collective-permute-start.5
  59.2 4.9 %collective-permute-start.7 = (bf16[9,9]{1,0:T(8,128)(2,1)S(1)}, bf16[9,9]{1,0:T(8,128)(2,1)S(1)}, u32[]{:S(2)}, u32[]{:S(2)}) collective-permute-start(bf16[9,9]{1,0:T(8,128)(2,1)S(1)} %get-tuple-element.51), channel_id=1, source_target_pairs={{3,0},{7,4},{11,8},{15,12},{19,16},{23,20},{27,24},{31,28}} | collective-permute-start | bytes 494 | tf_op jit(solution)/shard_map/ppermute | solution.py:38
  64.1 6.1 %copy-start = (f32[1,256,512]{2,1,0:T(8,128)S(1)}, f32[1,256,512]{2,1,0:T(8,128)}, u32[]{:S(2)}) copy-start(f32[1,256,512]{2,1,0:T(8,128)} %param.8) | copy-start | bytes 1572868
  64.1 6.0 %copy-start.4 = (f32[1,256]{1,0:T(1,128)S(1)}, f32[1,256]{1,0:T(1,128)}, u32[]{:S(2)}) copy-start(f32[1,256]{1,0:T(1,128)} %get-tuple-element.67) | copy-start | bytes 3076
  64.1 6.0 %copy-start.5 = (f32[1,256]{1,0:T(1,128)S(1)}, f32[1,256]{1,0:T(1,128)}, u32[]{:S(2)}) copy-start(f32[1,256]{1,0:T(1,128)} %get-tuple-element.68) | copy-start | bytes 3076
  64.1 6.0 %copy-start.6 = (f32[1,256]{1,0:T(1,128)S(1)}, f32[1,256]{1,0:T(1,128)}, u32[]{:S(2)}) copy-start(f32[1,256]{1,0:T(1,128)} %get-tuple-element.69) | copy-start | bytes 3076
  64.1 6.0 %copy-start.7 = (f32[1,256]{1,0:T(1,128)S(1)}, f32[1,256]{1,0:T(1,128)}, u32[]{:S(2)}) copy-start(f32[1,256]{1,0:T(1,128)} %get-tuple-element.70) | copy-start | bytes 3076
  64.2 6.0 %copy-start.8 = (f32[1,256]{1,0:T(1,128)S(1)}, f32[1,256]{1,0:T(1,128)}, u32[]{:S(2)}) copy-start(f32[1,256]{1,0:T(1,128)} %get-tuple-element.71) | copy-start | bytes 3076
  64.2 6.0 %copy-start.9 = (f32[1,256]{1,0:T(1,128)S(1)}, f32[1,256]{1,0:T(1,128)}, u32[]{:S(2)}) copy-start(f32[1,256]{1,0:T(1,128)} %get-tuple-element.72) | copy-start | bytes 3076
  64.2 6.0 %copy-start.10 = (f32[1,256]{1,0:T(1,128)S(1)}, f32[1,256]{1,0:T(1,128)}, u32[]{:S(2)}) copy-start(f32[1,256]{1,0:T(1,128)} %get-tuple-element.73) | copy-start | bytes 3076
  64.2 6.0 %copy-start.11 = (f32[1,256]{1,0:T(1,128)S(1)}, f32[1,256]{1,0:T(1,128)}, u32[]{:S(2)}) copy-start(f32[1,256]{1,0:T(1,128)} %get-tuple-element.74) | copy-start | bytes 3076
  64.2 6.0 %copy-start.12 = (f32[1,256]{1,0:T(1,128)S(1)}, f32[1,256]{1,0:T(1,128)}, u32[]{:S(2)}) copy-start(f32[1,256]{1,0:T(1,128)} %get-tuple-element.75) | copy-start | bytes 3076
  74.0 15.3 %copy-start.18 = (s32[6]{0:T(128)S(1)}, s32[6]{0:T(128)}, u32[]{:S(2)}) copy-start(s32[6]{0:T(128)} %copy-done.17) | copy-start | bytes 76
  74.0 15.3 %copy-start.16 = (s32[12]{0:T(128)S(1)}, s32[12]{0:T(128)}, u32[]{:S(2)}) copy-start(s32[12]{0:T(128)} %copy-done.15) | copy-start | bytes 148
  74.0 15.9 %copy-start.2 = (s32[32,32]{0,1:T(8,128)S(1)}, s32[32,32]{0,1:T(8,128)}, u32[]{:S(2)}) copy-start(s32[32,32]{0,1:T(8,128)} %iota_subtract_fusion) | copy-start | bytes 12292
